TPU v7x, 32 devices: a whole 2x2x4 slice. The times are simulated.
32 devices in a mesh: groups: 2 (over y), pix: 8 (over z, x), dp: 2 (over core).
Axes of the slice: x: 2, y: 2, z: 4, core: 2. Of those that a mesh axis runs over, the one named last changes fastest.
Arguments:
- features: bfloat16 [64, 64, 512], P('pix', None, ('groups', 'dp')), parts along dimension 2, may hold values from -6 to 6
- cheb_weights: bfloat16 [4, 64, 64], replicated, may hold values from -0.375 to 0.375
- out_bias: float32 [64], replicated, may hold values from -3 to 3
- lap_tiles: bfloat16 [64, 64, 576], P('pix'), as said below
- neighbours: int32 [64, 2], P('pix'), may hold values from 0 to 15, as said below
- send_blocks: int32 [8, 4, 2], P('pix'), may hold values from 0 to 7, as said below
- pixel_mask: int32 [64, 64], P('pix'), may hold values 0 or 1
- cotangent: bfloat16 [64, 64, 512], P('pix', None, ('groups', 'dp')), parts along dimension 2, may hold values from -6 to 6
Outputs:
- output_maps: bfloat16 [64, 64, 512], P('pix', None, ('groups', 'dp')), parts along dimension 2
- grad_features: bfloat16 [64, 64, 512], P('pix', None, ('groups', 'dp')), parts along dimension 2
- grad_weights: float32 [8, 64, 64], P('groups'), parts along dimension 0
- grad_bias: float32 [128], P('groups'), parts along dimension 0
There are 2 independent parts, one for each index of `groups`. A program takes and returns all parts, laid end to end along the dimension named above; an argument that names none is the same for every part. Nothing has to cross between parts.
Inputs may be any that keep to these rules, and one draw needn't show every extreme that they name: `send_blocks`: for device p and direction d (to devices p + 1, p - 1, p + 2, p - 2 modulo 8, in this order), 2 distinct local block numbers of device p; no block is listed in two directions. `neighbours`: column 0 names a local block or a received slot 8 + d * 2 + s; every received slot is named by exactly one row, every local block by column 0 of at most one row. Column 1 names a local block other than the row's own, every local block by exactly one row. Both neighbour relations are symmetric. `lap_tiles`: the operator is symmetric: the tile of block b in the row of block a is the transpose of the tile of block a in the row of block b, and a block's own tile is symmetric.
All inputs are finite; a program needn't handle non-finite values. No bound on the sum of `pixel_mask` on one device may be relied on, other than what follows from the above.
Results may differ from a plain program's by a relative error of at most 0.0047.
Values may be sent and summed in bfloat16 or wider, within the bound.
No kernel may reach another device: no remote copies, remote signals or barrier semaphores. Data moves between devices by JAX's collectives and lax.ppermute only.
A program may use at most 64 MiB of HBM per device.

v0:
```python
import math

import jax
import jax.numpy as jnp
from jax import lax
from jax.sharding import PartitionSpec as P

DIRECTIONS = (1, -1, 2, -2)
CYCLE_STEPS = (0, -1, 1, -2, 2, -3, 3)


def shifted(block, axis, distance):
    devices = range(lax.axis_size(axis))
    route = [((i - distance) % len(devices), i) for i in devices]
    return lax.ppermute(block, axis, route)


def collect_halo(masked_values, outgoing):
    pieces = []
    for heading_index, travel in enumerate(DIRECTIONS):
        pieces.append(shifted(masked_values[outgoing[heading_index]], "pix", travel))
    return jnp.concatenate(pieces, axis=0)


def tile_product(masked_values, extended, lap_tiles, neighbours, keep_mask):
    block_count, pixel_count, lane_count = masked_values.shape
    columns = [jnp.roll(masked_values, -offset, axis=0) for offset in CYCLE_STEPS]
    columns.append(extended[neighbours[:, 0]])
    columns.append(extended[neighbours[:, 1]])
    picked = jnp.stack(columns, axis=1).reshape(block_count, -1, lane_count)
    product = jnp.einsum("bpk,bkl->bpl", lap_tiles, picked, preferred_element_type=jnp.float32)
    return product * keep_mask


def forward_apply(values, lap_tiles, neighbours, outgoing, keep_mask):
    masked_values = values * keep_mask
    halo_blocks = collect_halo(masked_values, outgoing)
    extended = jnp.concatenate([masked_values, halo_blocks], axis=0)
    return tile_product(masked_values, extended, lap_tiles, neighbours, keep_mask)


def pushed_apply(values, lap_tiles, neighbours, outgoing, keep_mask):
    masked_values = values * keep_mask
    block_count, pixel_count, lane_count = values.shape
    cycle_count = len(CYCLE_STEPS)
    partial_terms = jnp.einsum(
        "bpk,bpl->bkl", lap_tiles, masked_values, preferred_element_type=jnp.float32
    )
    partial_terms = partial_terms.reshape(block_count, -1, pixel_count, lane_count)
    running = jnp.zeros((block_count, pixel_count, lane_count), jnp.float32)
    for column, offset in enumerate(CYCLE_STEPS):
        running = running + jnp.roll(partial_terms[:, column], offset, axis=0)
    slot_count = outgoing.shape[1]
    halo_count = len(DIRECTIONS) * slot_count
    irregular = jnp.concatenate(
        [partial_terms[:, cycle_count], partial_terms[:, cycle_count + 1]], axis=0
    )
    target_ids = jnp.concatenate([neighbours[:, 0], neighbours[:, 1]], axis=0)
    pooled = jax.ops.segment_sum(irregular, target_ids, num_segments=block_count + halo_count)
    running = running + pooled[:block_count]
    returned_all = pooled[block_count:].reshape(
        len(DIRECTIONS), slot_count, pixel_count, lane_count
    )
    for heading_index, travel in enumerate(DIRECTIONS):
        returned = shifted(returned_all[heading_index], "pix", -travel)
        running = running.at[outgoing[heading_index]].add(returned)
    return running * keep_mask


def local(
    features, cheb_weights, out_bias, lap_tiles, neighbours, send_blocks, pixel_mask, cotangent
):
    block_count, pixel_count, lane_count = features.shape
    term_count, chan_in, chan_out = cheb_weights.shape
    map_count = lane_count // chan_in
    outgoing = send_blocks[0]
    keep_mask = pixel_mask.astype(jnp.bfloat16)[:, :, None]
    cheb_terms = [features]
    for degree in range(1, term_count):
        applied = forward_apply(cheb_terms[-1], lap_tiles, neighbours, outgoing, keep_mask)
        if degree == 1:
            cheb_terms.append(applied.astype(jnp.bfloat16))
        else:
            cheb_terms.append((2.0 * applied - cheb_terms[-2]).astype(jnp.bfloat16))
    flat_rows = block_count * pixel_count
    mixed_sum = jnp.zeros((flat_rows, map_count, chan_out), jnp.float32)
    for degree in range(term_count):
        term_block = cheb_terms[degree].reshape(flat_rows, map_count, chan_in)
        mixed_sum = mixed_sum + jnp.einsum(
            "rmc,co->rmo", term_block, cheb_weights[degree], preferred_element_type=jnp.float32
        )
    output_maps = (
        (mixed_sum + out_bias)
        .reshape(block_count, pixel_count, map_count * chan_out)
        .astype(jnp.bfloat16)
    )
    upstream = cotangent.reshape(flat_rows, map_count, chan_out)

    def direct(degree):
        return jnp.einsum(
            "rmo,co->rmc", upstream, cheb_weights[degree], preferred_element_type=jnp.float32
        ).reshape(block_count, pixel_count, lane_count)

    def adjoint(values):
        return pushed_apply(values, lap_tiles, neighbours, outgoing, keep_mask)

    adjoints = [None] * term_count
    for degree in range(term_count - 1, 0, -1):
        running = direct(degree)
        if degree + 1 < term_count:
            running = running + 2.0 * adjoint(adjoints[degree + 1])
        if degree + 2 < term_count:
            running = running - adjoints[degree + 2]
        adjoints[degree] = running.astype(jnp.bfloat16)
    running = direct(0) + adjoint(adjoints[1]) - adjoints[2]
    grad_features = running.astype(jnp.bfloat16)
    grad_list = []
    for degree in range(term_count):
        term_block = cheb_terms[degree].reshape(flat_rows, map_count, chan_in)
        grad_list.append(
            jnp.einsum("rmc,rmo->co", term_block, upstream, preferred_element_type=jnp.float32)
        )
    partial_grads = jnp.stack(grad_list)
    bias_part = jnp.sum(upstream.astype(jnp.float32), axis=(0, 1))
    summed_weights, summed_bias = lax.psum((partial_grads, bias_part), ("pix", "dp"))
    factor = 1.0 / math.sqrt(flat_rows * map_count * lax.axis_size("pix") * lax.axis_size("dp"))
    return (output_maps, grad_features, summed_weights * factor, summed_bias * factor)


def solution(mesh):
    return jax.shard_map(
        local,
        mesh=mesh,
        in_specs=(
            P("pix", None, ("groups", "dp")),
            P(),
            P(),
            P("pix", None, None),
            P("pix", None),
            P("pix", None, None),
            P("pix", None),
            P("pix", None, ("groups", "dp")),
        ),
        out_specs=(
            P("pix", None, ("groups", "dp")),
            P("pix", None, ("groups", "dp")),
            P("groups", None, None),
            P("groups"),
        ),
        check_vma=False,
    )
```

profile of v0, /device:TPU:0, one launch (start us, length us, event | category | flops | bytes accessed | tf_op | source)
XLA Modules:
  0.0 316.4 jit_solution(6542873860701884093)
XLA Ops:
  9.0 1.7 constant_dynamic-update-slice_fusion.4
  11.9 2.9 collective-permute-start
  16.0 3.0 collective-permute-start.1
  21.5 3.8 %collective-permute-start.3 = (bf16[2,64,128]{2,1,0:T(8,128)(2,1)}, bf16[2,64,128]{2,1,0:T(8,128)(2,1)}, u32[]{:S(2)}, u32[]{:S(2)}) collective-permute-start(bf16[2,64,128]{2,1,0:T(8,128)(2,1)} %gather_fusion.3), channel_id=1, source_target_pairs={{4,0},{6,2},{8,4},{10,6},{12,8},{14,10},{0,12},{2,14},{5,1},{7,3},... | collective-permute-start | bytes 98312 | tf_op jit(solution)/shard_map/ppermute | solution.py:15
  31.6 3.0 scatter_fusion
  34.7 1.7 fusion.90
  55.6 30.1 %psum.15 = f32[64]{0:T(128)} all-reduce(f32[64]{0:T(128)} %reduce_sum.18), channel_id=1, replica_groups=mesh['groups'=2,'pix'=8,'dp'=2] {'pix','dp'}, use_global_device_ids=true, to_apply=%region_18.19 | all-reduce | flops 64 | bytes 512 | tf_op jit(solution)/shard_map/psum | solution.py:125
  103.1 2.1 collective-permute-start.15
  114.5 3.3 %collective-permute-start.4 = (bf16[2,64,128]{2,1,0:T(8,128)(2,1)}, bf16[2,64,128]{2,1,0:T(8,128)(2,1)}, u32[]{:S(2)}, u32[]{:S(2)}) collective-permute-start(bf16[2,64,128]{2,1,0:T(8,128)(2,1)} %gather_fusion.6), channel_id=1, source_target_pairs={{14,0},{0,2},{2,4},{4,6},{6,8},{8,10},{10,12},{12,14},{15,1},{1,3}... | collective-permute-start | bytes 98312 | tf_op jit(solution)/shard_map/ppermute | solution.py:15
  119.0 1.7 convolution_add_fusion.2
  123.8 3.3 %collective-permute-start.5 = (bf16[2,64,128]{2,1,0:T(8,128)(2,1)S(1)}, bf16[2,64,128]{2,1,0:T(8,128)(2,1)S(1)}, u32[]{:S(2)}, u32[]{:S(2)}) collective-permute-start(bf16[2,64,128]{2,1,0:T(8,128)(2,1)S(1)} %gather_fusion.7), channel_id=1, source_target_pairs={{2,0},{4,2},{6,4},{8,6},{10,8},{12,10},{14,12},{0,14},{3,1},{5,3},... | collective-permute-start | bytes 98312 | tf_op jit(solution)/shard_map/ppermute | solution.py:15
  128.8 5.8 %collective-permute-done.6 = bf16[2,64,128]{2,1,0:T(8,128)(2,1)S(1)} collective-permute-done((bf16[2,64,128]{2,1,0:T(8,128)(2,1)S(1)}, bf16[2,64,128]{2,1,0:T(8,128)(2,1)S(1)}, u32[]{:S(2)}, u32[]{:S(2)}) %collective-permute-start.6) | collective-permute-done | bytes 32800 | tf_op jit(solution)/shard_map/ppermute | solution.py:15
  135.5 2.9 collective-permute-done.7
  163.5 2.0 collective-permute-start.8
  165.4 3.0 collective-permute-start.9
  168.4 3.8 %collective-permute-start.11 = (bf16[2,64,128]{2,1,0:T(8,128)(2,1)}, bf16[2,64,128]{2,1,0:T(8,128)(2,1)}, u32[]{:S(2)}, u32[]{:S(2)}) collective-permute-start(bf16[2,64,128]{2,1,0:T(8,128)(2,1)} %gather_fusion.15), channel_id=1, source_target_pairs={{4,0},{6,2},{8,4},{10,6},{12,8},{14,10},{0,12},{2,14},{5,1},{7,3},... | collective-permute-start | bytes 98312 | tf_op jit(solution)/shard_map/ppermute | solution.py:15
  173.3 1.9 pad_maximum_fusion.1
  176.0 3.3 %scatter_fusion.5 = f32[16,64,128]{2,1,0:T(8,128)} fusion(f32[16,64,128]{2,1,0:T(8,128)} %broadcast.94.clone.1, s32[16]{0:T(128)} %copy-done.72, f32[16,64,128]{2,1,0:T(8,128)} %pad_maximum_fusion.1), kind=kCustom, calls=%fused_computation.23 | custom fusion | flops 131072 | bytes 1572928 | tf_op jit(solution)/shard_map/scatter-add | solution.py:59
  179.5 1.8 fusion.89
  191.6 1.8 collective-permute-start.17
  196.1 2.0 collective-permute-start.19
  202.6 1.6 gather_fusion.17
  214.0 1.6 fusion.31
  220.9 2.2 scatter_fusion.10
  223.8 4.7 %collective-permute-start.20 = (f32[2,64,128]{2,1,0:T(8,128)}, f32[2,64,128]{2,1,0:T(8,128)}, u32[]{:S(2)}, u32[]{:S(2)}) collective-permute-start(f32[2,64,128]{2,1,0:T(8,128)} %get-tuple-element.69), channel_id=1, source_target_pairs={{2,0},{4,2},{6,4},{8,6},{10,8},{12,10},{14,12},{0,14},{3,1},{5,3},... | collective-permute-start | bytes 196616 | tf_op jit(solution)/shard_map/ppermute | solution.py:15
  230.6 2.3 slice_add_fusion
  232.9 64.8 %all-reduce.2.cloned.1.call-done = f32[4,64,64]{2,1,0:T(8,128)} async-done(((f32[4,64,64]{2,1,0:T(8,128)}), f32[4,64,64]{2,1,0:T(8,128)}) %all-reduce.2.cloned.1.call-update) | async-done | bytes 65552 | tf_op jit(solution)/shard_map/psum | solution.py:125
  299.3 2.1 scatter_fusion.11
  301.4 2.1 scatter_fusion.12
  303.4 2.2 scatter_fusion.13
  305.6 2.1 scatter_fusion.14
  307.7 1.8 subtract_convert_fusion
  (358 shorter events, 128.6 us)
Async XLA Ops:
  7.2 290.5 %all-reduce.2.cloned.1.call-start = ((), (), s32[]{:S(2)}) async-start(), calls=%async_computation | async-start | bytes 262144 | tf_op jit(solution)/shard_map/psum | solution.py:125
  11.9 89.6 %collective-permute-start = (bf16[2,64,128]{2,1,0:T(8,128)(2,1)}, bf16[2,64,128]{2,1,0:T(8,128)(2,1)}, u32[]{:S(2)}, u32[]{:S(2)}) collective-permute-start(bf16[2,64,128]{2,1,0:T(8,128)(2,1)} %gather_fusion), channel_id=1, source_target_pairs={{14,0},{0,2},{2,4},{4,6},{6,8},{8,10},{10,12},{12,14},{15,1},{1,3}... | collective-permute-start | bytes 98312 | tf_op jit(solution)/shard_map/ppermute | solution.py:15
  16.0 86.2 %collective-permute-start.1 = (bf16[2,64,128]{2,1,0:T(8,128)(2,1)}, bf16[2,64,128]{2,1,0:T(8,128)(2,1)}, u32[]{:S(2)}, u32[]{:S(2)}) collective-permute-start(bf16[2,64,128]{2,1,0:T(8,128)(2,1)} %gather_fusion.1), channel_id=1, source_target_pairs={{2,0},{4,2},{6,4},{8,6},{10,8},{12,10},{14,12},{0,14},{3,1},{5,3},... | collective-permute-start | bytes 98312 | tf_op jit(solution)/shard_map/ppermute | solution.py:15
  20.3 82.8 %collective-permute-start.2 = (bf16[2,64,128]{2,1,0:T(8,128)(2,1)}, bf16[2,64,128]{2,1,0:T(8,128)(2,1)}, u32[]{:S(2)}, u32[]{:S(2)}) collective-permute-start(bf16[2,64,128]{2,1,0:T(8,128)(2,1)} %gather_fusion.2), channel_id=1, source_target_pairs={{12,0},{14,2},{0,4},{2,6},{4,8},{6,10},{8,12},{10,14},{13,1},{15,3... | collective-permute-start | bytes 98312 | tf_op jit(solution)/shard_map/ppermute | solution.py:15
  21.5 84.5 %collective-permute-start.3 = (bf16[2,64,128]{2,1,0:T(8,128)(2,1)}, bf16[2,64,128]{2,1,0:T(8,128)(2,1)}, u32[]{:S(2)}, u32[]{:S(2)}) collective-permute-start(bf16[2,64,128]{2,1,0:T(8,128)(2,1)} %gather_fusion.3), channel_id=1, source_target_pairs={{4,0},{6,2},{8,4},{10,6},{12,8},{14,10},{0,12},{2,14},{5,1},{7,3},... | collective-permute-start | bytes 98312 | tf_op jit(solution)/shard_map/ppermute | solution.py:15
  36.3 115.4 %collective-permute-start.12 = (f32[2,64,128]{2,1,0:T(8,128)}, f32[2,64,128]{2,1,0:T(8,128)}, u32[]{:S(2)}, u32[]{:S(2)}) collective-permute-start(f32[2,64,128]{2,1,0:T(8,128)} %get-tuple-element.77), channel_id=1, source_target_pairs={{2,0},{4,2},{6,4},{8,6},{10,8},{12,10},{14,12},{0,14},{3,1},{5,3},... | collective-permute-start | bytes 196616 | tf_op jit(solution)/shard_map/ppermute | solution.py:15
  49.2 39.4 %copy-start.32 = (bf16[7,64,128]{2,1,0:T(8,128)(2,1)S(1)}, bf16[7,64,128]{2,1,0:T(8,128)(2,1)}, u32[]{:S(2)}) copy-start(bf16[7,64,128]{2,1,0:T(8,128)(2,1)} %get-tuple-element.110) | copy-start | bytes 344068
  49.2 42.4 %copy-start.37 = (bf16[6,64,128]{2,1,0:T(8,128)(2,1)S(1)}, bf16[6,64,128]{2,1,0:T(8,128)(2,1)}, u32[]{:S(2)}) copy-start(bf16[6,64,128]{2,1,0:T(8,128)(2,1)} %get-tuple-element.106) | copy-start | bytes 294916
  49.2 45.3 %copy-start.50 = (bf16[3,64,128]{2,1,0:T(8,128)(2,1)S(1)}, bf16[3,64,128]{2,1,0:T(8,128)(2,1)}, u32[]{:S(2)}) copy-start(bf16[3,64,128]{2,1,0:T(8,128)(2,1)} %get-tuple-element.104) | copy-start | bytes 147460
  51.6 44.5 %copy-start.35 = (f32[3,64,128]{2,1,0:T(8,128)S(1)}, f32[3,64,128]{2,1,0:T(8,128)}, u32[]{:S(2)}) copy-start(f32[3,64,128]{2,1,0:T(8,128)} %get-tuple-element.52) | copy-start | bytes 294916
  51.6 44.5 %copy-start.55 = (f32[1,64,128]{2,1,0:T(8,128)S(1)}, f32[1,64,128]{2,1,0:T(8,128)}, u32[]{:S(2)}) copy-start(f32[1,64,128]{2,1,0:T(8,128)} %get-tuple-element.60) | copy-start | bytes 98308
  101.5 51.7 %collective-permute-start.13 = (f32[2,64,128]{2,1,0:T(8,128)}, f32[2,64,128]{2,1,0:T(8,128)}, u32[]{:S(2)}, u32[]{:S(2)}) collective-permute-start(f32[2,64,128]{2,1,0:T(8,128)} %get-tuple-element.76), channel_id=1, source_target_pairs={{14,0},{0,2},{2,4},{4,6},{6,8},{8,10},{10,12},{12,14},{15,1},{1,3}... | collective-permute-start | bytes 196616 | tf_op jit(solution)/shard_map/ppermute | solution.py:15
  102.3 52.3 %collective-permute-start.14 = (f32[2,64,128]{2,1,0:T(8,128)}, f32[2,64,128]{2,1,0:T(8,128)}, u32[]{:S(2)}, u32[]{:S(2)}) collective-permute-start(f32[2,64,128]{2,1,0:T(8,128)} %get-tuple-element.75), channel_id=1, source_target_pairs={{4,0},{6,2},{8,4},{10,6},{12,8},{14,10},{0,12},{2,14},{5,1},{7,3},... | collective-permute-start | bytes 196616 | tf_op jit(solution)/shard_map/ppermute | solution.py:15
  103.1 53.0 %collective-permute-start.15 = (f32[2,64,128]{2,1,0:T(8,128)}, f32[2,64,128]{2,1,0:T(8,128)}, u32[]{:S(2)}, u32[]{:S(2)}) collective-permute-start(f32[2,64,128]{2,1,0:T(8,128)} %get-tuple-element.74), channel_id=1, source_target_pairs={{12,0},{14,2},{0,4},{2,6},{4,8},{6,10},{8,12},{10,14},{13,1},{15,3... | collective-permute-start | bytes 196616 | tf_op jit(solution)/shard_map/ppermute | solution.py:15
  114.5 9.3 %collective-permute-start.4 = (bf16[2,64,128]{2,1,0:T(8,128)(2,1)}, bf16[2,64,128]{2,1,0:T(8,128)(2,1)}, u32[]{:S(2)}, u32[]{:S(2)}) collective-permute-start(bf16[2,64,128]{2,1,0:T(8,128)(2,1)} %gather_fusion.6), channel_id=1, source_target_pairs={{14,0},{0,2},{2,4},{4,6},{6,8},{8,10},{10,12},{12,14},{15,1},{1,3}... | collective-permute-start | bytes 98312 | tf_op jit(solution)/shard_map/ppermute | solution.py:15
  123.8 4.9 %collective-permute-start.5 = (bf16[2,64,128]{2,1,0:T(8,128)(2,1)S(1)}, bf16[2,64,128]{2,1,0:T(8,128)(2,1)S(1)}, u32[]{:S(2)}, u32[]{:S(2)}) collective-permute-start(bf16[2,64,128]{2,1,0:T(8,128)(2,1)S(1)} %gather_fusion.7), channel_id=1, source_target_pairs={{2,0},{4,2},{6,4},{8,6},{10,8},{12,10},{14,12},{0,14},{3,1},{5,3},... | collective-permute-start | bytes 98312 | tf_op jit(solution)/shard_map/ppermute | solution.py:15
  128.7 5.8 %collective-permute-start.6 = (bf16[2,64,128]{2,1,0:T(8,128)(2,1)S(1)}, bf16[2,64,128]{2,1,0:T(8,128)(2,1)S(1)}, u32[]{:S(2)}, u32[]{:S(2)}) collective-permute-start(bf16[2,64,128]{2,1,0:T(8,128)(2,1)S(1)} %gather_fusion.8), channel_id=1, source_target_pairs={{12,0},{14,2},{0,4},{2,6},{4,8},{6,10},{8,12},{10,14},{13,1},{15,3... | collective-permute-start | bytes 98312 | tf_op jit(solution)/shard_map/ppermute | solution.py:15
  134.6 3.9 %collective-permute-start.7 = (bf16[2,64,128]{2,1,0:T(8,128)(2,1)S(1)}, bf16[2,64,128]{2,1,0:T(8,128)(2,1)S(1)}, u32[]{:S(2)}, u32[]{:S(2)}) collective-permute-start(bf16[2,64,128]{2,1,0:T(8,128)(2,1)S(1)} %gather_fusion.9), channel_id=1, source_target_pairs={{4,0},{6,2},{8,4},{10,6},{12,8},{14,10},{0,12},{2,14},{5,1},{7,3},... | collective-permute-start | bytes 98312 | tf_op jit(solution)/shard_map/ppermute | solution.py:15
  163.5 28.1 %collective-permute-start.8 = (bf16[2,64,128]{2,1,0:T(8,128)(2,1)}, bf16[2,64,128]{2,1,0:T(8,128)(2,1)}, u32[]{:S(2)}, u32[]{:S(2)}) collective-permute-start(bf16[2,64,128]{2,1,0:T(8,128)(2,1)} %gather_fusion.12), channel_id=1, source_target_pairs={{14,0},{0,2},{2,4},{4,6},{6,8},{8,10},{10,12},{12,14},{15,1},{1,3}... | collective-permute-start | bytes 98312 | tf_op jit(solution)/shard_map/ppermute | solution.py:15
  165.4 29.3 %collective-permute-start.9 = (bf16[2,64,128]{2,1,0:T(8,128)(2,1)}, bf16[2,64,128]{2,1,0:T(8,128)(2,1)}, u32[]{:S(2)}, u32[]{:S(2)}) collective-permute-start(bf16[2,64,128]{2,1,0:T(8,128)(2,1)} %gather_fusion.13), channel_id=1, source_target_pairs={{2,0},{4,2},{6,4},{8,6},{10,8},{12,10},{14,12},{0,14},{3,1},{5,3},... | collective-permute-start | bytes 98312 | tf_op jit(solution)/shard_map/ppermute | solution.py:15
  168.4 27.8 %collective-permute-start.10 = (bf16[2,64,128]{2,1,0:T(8,128)(2,1)}, bf16[2,64,128]{2,1,0:T(8,128)(2,1)}, u32[]{:S(2)}, u32[]{:S(2)}) collective-permute-start(bf16[2,64,128]{2,1,0:T(8,128)(2,1)} %gather_fusion.14), channel_id=1, source_target_pairs={{12,0},{14,2},{0,4},{2,6},{4,8},{6,10},{8,12},{10,14},{13,1},{15,3... | collective-permute-start | bytes 98312 | tf_op jit(solution)/shard_map/ppermute | solution.py:15
  168.4 31.1 %collective-permute-start.11 = (bf16[2,64,128]{2,1,0:T(8,128)(2,1)}, bf16[2,64,128]{2,1,0:T(8,128)(2,1)}, u32[]{:S(2)}, u32[]{:S(2)}) collective-permute-start(bf16[2,64,128]{2,1,0:T(8,128)(2,1)} %gather_fusion.15), channel_id=1, source_target_pairs={{4,0},{6,2},{8,4},{10,6},{12,8},{14,10},{0,12},{2,14},{5,1},{7,3},... | collective-permute-start | bytes 98312 | tf_op jit(solution)/shard_map/ppermute | solution.py:15
  181.2 29.4 %collective-permute-start.16 = (f32[2,64,128]{2,1,0:T(8,128)}, f32[2,64,128]{2,1,0:T(8,128)}, u32[]{:S(2)}, u32[]{:S(2)}) collective-permute-start(f32[2,64,128]{2,1,0:T(8,128)} %get-tuple-element.73), channel_id=1, source_target_pairs={{2,0},{4,2},{6,4},{8,6},{10,8},{12,10},{14,12},{0,14},{3,1},{5,3},... | collective-permute-start | bytes 196616 | tf_op jit(solution)/shard_map/ppermute | solution.py:15
  191.6 20.5 %collective-permute-start.17 = (f32[2,64,128]{2,1,0:T(8,128)}, f32[2,64,128]{2,1,0:T(8,128)S(1)}, u32[]{:S(2)}, u32[]{:S(2)}) collective-permute-start(f32[2,64,128]{2,1,0:T(8,128)} %get-tuple-element.72), channel_id=1, source_target_pairs={{14,0},{0,2},{2,4},{4,6},{6,8},{8,10},{10,12},{12,14},{15,1},{1,3}... | collective-permute-start | bytes 196616 | tf_op jit(solution)/shard_map/ppermute | solution.py:15
  194.8 17.9 %collective-permute-start.18 = (f32[2,64,128]{2,1,0:T(8,128)}, f32[2,64,128]{2,1,0:T(8,128)S(1)}, u32[]{:S(2)}, u32[]{:S(2)}) collective-permute-start(f32[2,64,128]{2,1,0:T(8,128)} %get-tuple-element.71), channel_id=1, source_target_pairs={{4,0},{6,2},{8,4},{10,6},{12,8},{14,10},{0,12},{2,14},{5,1},{7,3},... | collective-permute-start | bytes 196616 | tf_op jit(solution)/shard_map/ppermute | solution.py:15
  196.1 17.2 %collective-permute-start.19 = (f32[2,64,128]{2,1,0:T(8,128)}, f32[2,64,128]{2,1,0:T(8,128)S(1)}, u32[]{:S(2)}, u32[]{:S(2)}) collective-permute-start(f32[2,64,128]{2,1,0:T(8,128)} %get-tuple-element.70), channel_id=1, source_target_pairs={{12,0},{14,2},{0,4},{2,6},{4,8},{6,10},{8,12},{10,14},{13,1},{15,3... | collective-permute-start | bytes 196616 | tf_op jit(solution)/shard_map/ppermute | solution.py:15
  223.8 75.5 %collective-permute-start.20 = (f32[2,64,128]{2,1,0:T(8,128)}, f32[2,64,128]{2,1,0:T(8,128)}, u32[]{:S(2)}, u32[]{:S(2)}) collective-permute-start(f32[2,64,128]{2,1,0:T(8,128)} %get-tuple-element.69), channel_id=1, source_target_pairs={{2,0},{4,2},{6,4},{8,6},{10,8},{12,10},{14,12},{0,14},{3,1},{5,3},... | collective-permute-start | bytes 196616 | tf_op jit(solution)/shard_map/ppermute | solution.py:15
  228.6 72.8 %collective-permute-start.21 = (f32[2,64,128]{2,1,0:T(8,128)}, f32[2,64,128]{2,1,0:T(8,128)}, u32[]{:S(2)}, u32[]{:S(2)}) collective-permute-start(f32[2,64,128]{2,1,0:T(8,128)} %get-tuple-element.68), channel_id=1, source_target_pairs={{14,0},{0,2},{2,4},{4,6},{6,8},{8,10},{10,12},{12,14},{15,1},{1,3}... | collective-permute-start | bytes 196616 | tf_op jit(solution)/shard_map/ppermute | solution.py:15
  228.6 74.9 %collective-permute-start.22 = (f32[2,64,128]{2,1,0:T(8,128)}, f32[2,64,128]{2,1,0:T(8,128)}, u32[]{:S(2)}, u32[]{:S(2)}) collective-permute-start(f32[2,64,128]{2,1,0:T(8,128)} %get-tuple-element.67), channel_id=1, source_target_pairs={{4,0},{6,2},{8,4},{10,6},{12,8},{14,10},{0,12},{2,14},{5,1},{7,3},... | collective-permute-start | bytes 196616 | tf_op jit(solution)/shard_map/ppermute | solution.py:15
  229.1 76.5 %collective-permute-start.23 = (f32[2,64,128]{2,1,0:T(8,128)}, f32[2,64,128]{2,1,0:T(8,128)}, u32[]{:S(2)}, u32[]{:S(2)}) collective-permute-start(f32[2,64,128]{2,1,0:T(8,128)} %get-tuple-element.66), channel_id=1, source_target_pairs={{12,0},{14,2},{0,4},{2,6},{4,8},{6,10},{8,12},{10,14},{13,1},{15,3... | collective-permute-start | bytes 196616 | tf_op jit(solution)/shard_map/ppermute | solution.py:15
  230.6 75.1 %copy-start.64 = (s32[2]{0:T(128)S(1)}, s32[2]{0:T(128)}, u32[]{:S(2)}) copy-start(s32[2]{0:T(128)} %copy-done.61) | copy-start | bytes 28
  232.9 74.8 %copy-start.11 = (f32[8,64,128]{2,1,0:T(8,128)S(1)}, f32[8,64,128]{2,1,0:T(8,128)}, u32[]{:S(2)}) copy-start(f32[8,64,128]{2,1,0:T(8,128)} %copy.107) | copy-start | bytes 786436
  (70 other events, 464.6 us)
Sparse Core Ops, SparseCore 0:
  208.7 88.9 all-reduce.1
where the time goes:
time: 320 us; the launch traced here: 316 us
  local copies, waits for them, and re-layouts  76.6 us (24%)
  waiting for transfers between devices  74.5 us (23%)
  other arithmetic  63.2 us (20%)
  starting transfers between devices  39.3 us (12%)
  blocking collectives  30.1 us (9%)
  matrix products  17.3 us (5%)
  between operations  15.4 us (5%)
    psum x1, waiting for transfers between devices, local(): lax.psum((partial_grads, bias_part), ('pix', 'dp'))  64.8 us
    ppermute x24, starting transfers between devices, shifted(): return lax.ppermute(block, axis, route)  39.2 us
    psum x1, blocking collectives, local(): lax.psum((partial_grads, bias_part), ('pix', 'dp'))  30.1 us
    unnamed x19, other arithmetic  19.2 us
    scatter-add x12, other arithmetic, pushed_apply(): running = running.at[outgoing[heading_index]].add(returned)  17.4 us
    gather x12, local copies, waits for them, and re-layouts, collect_halo(): masked_values[outgoing[heading_index]]  13.1 us
    slice x18, local copies, waits for them, and re-layouts, pushed_apply(): running = running + jnp.roll(partial_terms[:, column], offset, axis=0)  13 us
    unnamed x170, local copies, waits for them, and re-layouts  12 us
  transfers between devices with their start and end apart: 25, of which 4 were waited for; matrix products, arithmetic and copies ran while one was open for 44% of the time, Pallas kernels for 0%

commit v1 on v0

v1 whole, which is shorter than its diff:
```python
import functools
import math

import jax
import jax.numpy as jnp
from jax import lax
from jax.experimental import pallas as pl
from jax.experimental.pallas import tpu as pltpu
from jax.sharding import PartitionSpec as P

CYCLE_STEPS = (0, -1, 1, -2, 2, -3, 3)
ROW_SPLIT = 2
F32 = jnp.float32
BF16 = jnp.bfloat16


def pair_of(index, pairing, count):
    if pairing == 0:
        return index ^ 1
    if pairing == 1:
        return (index + 1 if index % 2 else index - 1) % count
    low = index % 4 < 2
    step = 2 if low == (pairing == 2) else -2
    return (index + step) % count


def exchange(block, pairing):
    count = lax.axis_size("pix")
    route = [(pair_of(i, pairing, count), i) for i in range(count)]
    return lax.ppermute(block, "pix", route)


def send_heading(pairing, device):
    if pairing < 2:
        return (device + pairing) % 2
    return 2 + (device // 2 + pairing) % 2


def matmul(left, right):
    return jnp.dot(left, right, preferred_element_type=F32)


def matmul_tn(left, right):
    return lax.dot_general(left, right, (((0,), (0,)), ((), ())), preferred_element_type=F32)


def matmul_nt(left, right):
    return lax.dot_general(left, right, (((1,), (1,)), ((), ())), preferred_element_type=F32)


def pack_kernel(
    rows_ref, lists_ref, mask_ref, feat_ref, cot_ref, lap_ref,
    send0, send1, send2, send3, ring_ref, near_ref, far_ref, part_ref,
    value, paired, keep, keep_row,
):
    blocks, pixels, lanes = feat_ref.shape
    group = blocks // ROW_SPLIT
    device = lax.axis_index("pix")
    keep[...] = mask_ref[...].astype(F32)
    for b in range(blocks):
        keep_row[:, b * pixels:(b + 1) * pixels] = jnp.broadcast_to(keep[b:b + 1, :], (8, pixels))
        value[b, :, :lanes] = feat_ref[b]
        value[b, :, lanes:] = cot_ref[b]
    diagonal = lax.broadcasted_iota(jnp.int32, (pixels, pixels), 0) == lax.broadcasted_iota(
        jnp.int32, (pixels, pixels), 1
    )
    ring_ref[...] = jnp.zeros_like(ring_ref)
    near_ref[...] = jnp.zeros_like(near_ref)
    far_ref[...] = jnp.zeros_like(far_ref)
    cycle = len(CYCLE_STEPS) * pixels
    for a in range(blocks):
        column = jnp.sum(
            jnp.where(diagonal, keep[a:a + 1, :], 0.0), axis=1, keepdims=True
        )
        rows = slice(a * pixels, (a + 1) * pixels)
        for j, step in enumerate(CYCLE_STEPS):
            b = (a + step) % blocks
            tile = lap_ref[a, :, j * pixels:(j + 1) * pixels].astype(F32)
            both = column * keep[b:b + 1, :]
            ring_ref[rows, b * pixels:(b + 1) * pixels] = (tile * both).astype(BF16)
        g, t = a // group, a % group
        spot = slice(t * pixels, (t + 1) * pixels)
        second = rows_ref[a, 1]
        tile = lap_ref[a, :, cycle + pixels:cycle + 2 * pixels].astype(F32)
        near_ref[g, spot, spot] = (tile * (column * keep[pl.ds(second, 1), :])).astype(BF16)
        tile = lap_ref[a, :, cycle:cycle + pixels].astype(F32)
        far_ref[g, spot, spot] = (tile * column).astype(BF16)
        paired[a] = value[second]
    whole = value[...].reshape(blocks * pixels, 2 * lanes)
    part = matmul(ring_ref[...], whole)
    for g in range(ROW_SPLIT):
        mates = paired[g * group:(g + 1) * group].reshape(group * pixels, 2 * lanes)
        rows = slice(g * group * pixels, (g + 1) * group * pixels)
        total = part[rows] + matmul(near_ref[g], mates)
        part_ref[g * group:(g + 1) * group] = total.reshape(group, pixels, 2 * lanes)
    for pairing, send in enumerate((send0, send1, send2, send3)):
        heading = send_heading(pairing, device)
        slots = lists_ref.shape[2]
        for s in range(slots):
            b = lists_ref[0, heading, s]
            base = s * 2 * pixels
            send[base:base + pixels, :] = value[b]
            send[base + pixels:base + 2 * pixels, :] = part_ref[b].astype(BF16)
        tail = slots * 2 * pixels
        send[tail:, :] = jnp.zeros((16, 2 * lanes), BF16)
        first = keep[pl.ds(lists_ref[0, heading, 0], 1), :]
        last = keep[pl.ds(lists_ref[0, heading, 1], 1), :]
        which = lax.broadcasted_iota(jnp.int32, (16, pixels), 0)
        send[tail:, :pixels] = jnp.where(
            which == 0, first, jnp.where(which == 1, last, 0.0)
        ).astype(BF16)


def row_of_slot(rows_ref, slot):
    blocks = rows_ref.shape[0]
    found = jnp.int32(0)
    for a in range(blocks):
        found = jnp.where(rows_ref[a, 0] == blocks + slot, a, found)
    return found


def middle_kernel(
    rows_ref, lists_ref, feat_ref, cot_ref, ring_ref, near_ref, far_ref, part_ref,
    got0, got1, got2, got3,
    one_ref, two_ref, cross_ref, send0, send1, send2, send3, sums_ref,
    value, halo, halo_part, paired, keep_far, scratch_two,
):
    blocks, pixels, lanes = feat_ref.shape
    group = blocks // ROW_SPLIT
    flat = blocks * pixels
    device = lax.axis_index("pix")
    for b in range(blocks):
        value[b, :, :lanes] = feat_ref[b]
        value[b, :, lanes:] = cot_ref[b]
    slots = lists_ref.shape[2]
    tail = slots * 2 * pixels
    for pairing, got in enumerate((got0, got1, got2, got3)):
        heading = send_heading(pairing, device) ^ 1
        flags = got[tail:, :pixels].astype(F32)
        for s in range(slots):
            row = row_of_slot(rows_ref, heading * slots + s)
            base = s * 2 * pixels
            halo[row] = got[base:base + pixels, :]
            halo_part[row] = got[base + pixels:base + 2 * pixels, :]
            keep_far[pl.ds(row, 1), :] = flags[s:s + 1, :]
    cross_ref[...] = jnp.zeros_like(cross_ref)
    for a in range(blocks):
        g, t = a // group, a % group
        spot = slice(t * pixels, (t + 1) * pixels)
        tile = far_ref[g, spot, spot].astype(F32)
        cross_ref[g, spot, spot] = (tile * keep_far[a:a + 1, :]).astype(BF16)
    width = 2 * lanes
    size = group * pixels
    for g in range(ROW_SPLIT):
        mine = slice(g * group, (g + 1) * group)
        other = halo[mine].reshape(size, width)
        total = part_ref[mine].reshape(size, width) + matmul(cross_ref[g], other)
        one_ref[mine] = total.astype(BF16).reshape(group, pixels, width)
        own = value[mine].reshape(size, width)
        total = halo_part[mine].reshape(size, width).astype(F32) + matmul_tn(cross_ref[g], own)
        halo[mine] = total.astype(BF16).reshape(group, pixels, width)
    for a in range(blocks):
        paired[a] = one_ref[rows_ref[a, 1]]
    applied = matmul(ring_ref[...], one_ref[...].reshape(flat, width))
    for g in range(ROW_SPLIT):
        mine = slice(g * group, (g + 1) * group)
        total = applied[g * size:(g + 1) * size]
        total = total + matmul(near_ref[g], paired[mine].reshape(size, width))
        total = total + matmul(cross_ref[g], halo[mine].reshape(size, width))
        total = 2.0 * total - value[mine].reshape(size, width).astype(F32)
        total = total.astype(BF16).reshape(group, pixels, width)
        two_ref[mine] = total
    for pairing, send in enumerate((send0, send1, send2, send3)):
        heading = send_heading(pairing, device)
        for s in range(slots):
            send[s * pixels:(s + 1) * pixels, :] = two_ref[lists_ref[0, heading, s]]
    zero = value[...].reshape(flat, width)
    one = one_ref[...].reshape(flat, width)
    two = two_ref[...].reshape(flat, width)
    half = lanes // 2
    cot = zero[:, lanes:]
    cot_one = one[:, lanes:]
    low = matmul_tn(jnp.concatenate([zero[:, :lanes], one[:, :lanes]], axis=1), cot)
    high = matmul_tn(jnp.concatenate([one[:, :lanes], two[:, :lanes]], axis=1), cot_one)

    def trace(product, start):
        return (
            product[start:start + half, :half] + product[start + half:start + lanes, half:]
        )

    zeroth = trace(low, 0)
    first = trace(low, lanes)
    second = 2.0 * trace(high, 0) - zeroth
    third = 2.0 * trace(high, lanes) - first
    sums_ref[:half, :half] = zeroth
    sums_ref[:half, half:] = first
    sums_ref[half:lanes, :half] = second
    sums_ref[half:lanes, half:] = third
    sums_ref[lanes:, :] = jnp.broadcast_to(
        jnp.sum(cot.astype(F32), axis=0, keepdims=True), (8, lanes)
    )


def last_kernel(
    rows_ref, feat_ref, cot_ref, weight_ref, bias_ref, ring_ref, near_ref, cross_ref, one_ref,
    two_ref, got0, got1, got2, got3,
    out_ref, grad_ref,
    halo, paired, mix, mix_wide,
):
    blocks, pixels, lanes = feat_ref.shape
    terms, half, _ = weight_ref.shape
    group = blocks // ROW_SPLIT
    flat, width, size = blocks * pixels, 2 * lanes, group * pixels
    device = lax.axis_index("pix")
    slots = got0.shape[0] // pixels
    for pairing, got in enumerate((got0, got1, got2, got3)):
        heading = send_heading(pairing, device) ^ 1
        for s in range(slots):
            row = row_of_slot(rows_ref, heading * slots + s)
            halo[row] = got[s * pixels:(s + 1) * pixels, :]
    for a in range(blocks):
        paired[a] = two_ref[rows_ref[a, 1]]
    mix[...] = jnp.zeros_like(mix)
    mix_wide[...] = jnp.zeros_like(mix_wide)
    for k in range(terms):
        for m in range(lanes // half):
            spot = slice(m * half, (m + 1) * half)
            shifted = slice(k * lanes + m * half, k * lanes + (m + 1) * half)
            mix[shifted, spot] = weight_ref[k]
            mix_wide[spot, shifted] = weight_ref[k]
    applied = matmul(ring_ref[...], two_ref[...].reshape(flat, width))
    bias = jnp.concatenate([bias_ref[...]] * (lanes // half), axis=1)
    for g in range(ROW_SPLIT):
        mine = slice(g * group, (g + 1) * group)
        total = applied[g * size:(g + 1) * size]
        total = total + matmul(near_ref[g], paired[mine].reshape(size, width))
        total = total + matmul(cross_ref[g], halo[mine].reshape(size, width))
        one = one_ref[mine].reshape(size, width)
        two = two_ref[mine].reshape(size, width)
        three = (2.0 * total - one.astype(F32)).astype(BF16)
        feat = feat_ref[mine].reshape(size, lanes)
        cot = cot_ref[mine].reshape(size, lanes)
        forward = jnp.concatenate(
            [feat, one[:, :lanes], two[:, :lanes], three[:, :lanes]], axis=1
        )
        backward = jnp.concatenate(
            [cot, one[:, lanes:], two[:, lanes:], three[:, lanes:]], axis=1
        )
        out = matmul(forward, mix[...]) + bias
        out_ref[mine] = out.astype(BF16).reshape(group, pixels, lanes)
        grad = matmul_nt(backward, mix_wide[...])
        grad_ref[mine] = grad.astype(BF16).reshape(group, pixels, lanes)


def finish_kernel(factor, mine_ref, other_ref, weight_ref, bias_ref):
    total = (mine_ref[...] + other_ref[...]) * factor
    terms, half, _ = weight_ref.shape
    lanes = 2 * half
    for k in range(terms):
        rows, cols = k // 2 * half, k % 2 * half
        weight_ref[k] = total[rows:rows + half, cols:cols + half]
    bias = total[lanes:lanes + 1, :]
    bias_ref[...] = bias[:, :half] + bias[:, half:]


def call(kernel, outs, ins, scratch, flops):
    vmem = pl.BlockSpec(memory_space=pltpu.VMEM)
    smem = pl.BlockSpec(memory_space=pltpu.SMEM)
    touched = sum(math.prod(x.shape) * x.dtype.itemsize for x in [*ins, *outs])
    return pl.pallas_call(
        kernel,
        out_shape=outs,
        in_specs=[smem if i < 2 and x.dtype == jnp.int32 else vmem for i, x in enumerate(ins)],
        out_specs=[vmem] * len(outs),
        scratch_shapes=scratch,
        cost_estimate=pl.CostEstimate(flops=flops, transcendentals=0, bytes_accessed=touched),
        compiler_params=pltpu.CompilerParams(vmem_limit_bytes=32 << 20),
    )(*ins)


def local(
    features, cheb_weights, out_bias, lap_tiles, neighbours, send_blocks, pixel_mask, cotangent
):
    blocks, pixels, lanes = features.shape
    terms, chan_in, chan_out = cheb_weights.shape
    slots = send_blocks.shape[2]
    width, flat = 2 * lanes, blocks * pixels
    size = flat // ROW_SPLIT
    shape = jax.ShapeDtypeStruct
    apply_flops = 2 * flat * width * (flat + 2 * size)

    operator = [
        shape((flat, flat), BF16),
        shape((ROW_SPLIT, size, size), BF16),
        shape((ROW_SPLIT, size, size), BF16),
    ]
    field = shape((blocks, pixels, width), BF16)
    wide = shape((blocks, pixels, width), F32)
    *sends, ring, near, far, part = call(
        pack_kernel,
        [shape((slots * 2 * pixels + 16, width), BF16)] * 4 + operator + [wide],
        [neighbours, send_blocks, pixel_mask, features, cotangent, lap_tiles],
        [
            pltpu.VMEM((blocks, pixels, width), BF16),
            pltpu.VMEM((blocks, pixels, width), BF16),
            pltpu.VMEM((blocks, pixels), F32),
            pltpu.VMEM((8, flat), F32),
        ],
        apply_flops,
    )
    order = (1, 0, 2, 3)
    got = {k: exchange(sends[k], k) for k in order}
    one, two, cross, *rest = call(
        middle_kernel,
        [field, field, operator[1]]
        + [shape((slots * pixels, width), BF16)] * 4
        + [shape((lanes + 8, lanes), F32)],
        [neighbours, send_blocks, features, cotangent, ring, near, far, part]
        + [got[k] for k in range(4)],
        [
            pltpu.VMEM((blocks, pixels, width), BF16),
            pltpu.VMEM((blocks, pixels, width), BF16),
            pltpu.VMEM((blocks, pixels, width), BF16),
            pltpu.VMEM((blocks, pixels, width), BF16),
            pltpu.VMEM((blocks, pixels), F32),
            pltpu.VMEM((8, 128), F32),
        ],
        2 * apply_flops,
    )
    sends, sums = rest[:4], rest[4]
    got = {k: exchange(sends[k], k) for k in order}
    output_maps, grad_features = call(
        last_kernel,
        [shape(features.shape, BF16), shape(features.shape, BF16)],
        [neighbours, features, cotangent, cheb_weights, out_bias.reshape(1, chan_out)]
        + [ring, near, cross, one, two]
        + [got[k] for k in range(4)],
        [
            pltpu.VMEM((blocks, pixels, width), BF16),
            pltpu.VMEM((blocks, pixels, width), BF16),
            pltpu.VMEM((terms * lanes, lanes), BF16),
            pltpu.VMEM((lanes, terms * lanes), BF16),
        ],
        2 * apply_flops,
    )
    count = lax.axis_size("pix")
    pair = lax.axis_size("dp")
    factor = 1.0 / math.sqrt(flat * (lanes // chan_in) * count * pair)
    other = lax.ppermute(sums, "dp", [(i ^ 1, i) for i in range(pair)])
    reach = 1
    while reach < count:
        sums = sums + other
        other = lax.ppermute(sums, "pix", [(i ^ reach, i) for i in range(count)])
        reach *= 2
    grad_weights, grad_bias = call(
        functools.partial(finish_kernel, factor),
        [shape(cheb_weights.shape, F32), shape((1, chan_out), F32)],
        [sums, other],
        [],
        sums.size,
    )
    return output_maps, grad_features, grad_weights, grad_bias.reshape(chan_out)


def solution(mesh):
    return jax.shard_map(
        local,
        mesh=mesh,
        in_specs=(
            P("pix", None, ("groups", "dp")),
            P(),
            P(),
            P("pix", None, None),
            P("pix", None),
            P("pix", None, None),
            P("pix", None),
            P("pix", None, ("groups", "dp")),
        ),
        out_specs=(
            P("pix", None, ("groups", "dp")),
            P("pix", None, ("groups", "dp")),
            P("groups", None, None),
            P("groups"),
        ),
        check_vma=False,
    )
```

time: 320 us -> 46.2 us (0.14); the launches traced: 316 us -> 46 us
  local copies, waits for them, and re-layouts: 76.6 us -> 4.42 us
  other arithmetic: 63.2 us -> 0.03 us
  waiting for transfers between devices: 74.5 us -> 15.9 us
  blocking collectives: 30.1 us -> 0 us
  starting transfers between devices: 39.3 us -> 17.3 us
  matrix products: 17.3 us -> 0 us
  between operations: 15.4 us -> 0.7 us
  Pallas kernels: 0 us -> 7.55 us
    psum x1 -> x0, waiting for transfers between devices: 64.8 us -> none  [local(): lax.psum((partial_grads, bias_part), ('pix', 'dp'))]
    slice x40 -> x0, local copies, waits for them, and re-layouts: 30.2 us -> none  [the longest x18 13 us: pushed_apply(): running = running + jnp.roll(partial_terms[:, column], offset, axis=0)]
    psum x1 -> x0, blocking collectives: 30.1 us -> none  [local(): lax.psum((partial_grads, bias_part), ('pix', 'dp'))]
    scatter-add x15 -> x0, other arithmetic: 25.9 us -> none  [the longest x12 17.4 us: pushed_apply(): running = running.at[outgoing[heading_index]].add(returned)]
    ppermute x24 -> x12, starting transfers between devices: 39.2 us -> 17.3 us  [the longest x8 14.3 us: exchange(): return lax.ppermute(block, 'pix', route)]
    unnamed x19 -> x0, other arithmetic: 19.2 us -> none
    gather x18 -> x0, local copies, waits for them, and re-layouts: 19.1 us -> none  [the longest x12 13.1 us: collect_halo(): masked_values[outgoing[heading_index]]]
    dot_general x18 -> x0, matrix products: 17.3 us -> none  [the longest x4 5.89 us: local(): jnp.einsum('rmc,co->rmo', term_block, cheb_weights[degree], preferred_ele...]
  transfers between devices with their start and end apart: 25 -> 12, of which waited for: 4 -> 8; matrix products, arithmetic and copies ran while one was open for 44% -> 0% of each run, Pallas kernels for 0% -> 5%
where the time goes in v1:
time: 46.2 us; the launch traced here: 46 us
  starting transfers between devices  17.3 us (37%)
  waiting for transfers between devices  15.9 us (34%)
  Pallas kernels  7.55 us (16%)
  local copies, waits for them, and re-layouts  4.42 us (10%)
  between operations  0.7 us (2%)
    ppermute x8, starting transfers between devices, exchange(): return lax.ppermute(block, 'pix', route)  14.3 us
    ppermute x8, waiting for transfers between devices, exchange(): return lax.ppermute(block, 'pix', route)  11.6 us
    pallas_call x4, Pallas kernels, call(): pl.pallas_call(kernel, out_shape=outs, in_specs=[smem if i < 2 and x.dtyp...  7.55 us
    unnamed x18, local copies, waits for them, and re-layouts  4.42 us
    ppermute x3, waiting for transfers between devices, local(): other = lax.ppermute(sums, 'pix', [(i ^ reach, i) for i in range(count)])  3.1 us
    ppermute x3, starting transfers between devices, local(): other = lax.ppermute(sums, 'pix', [(i ^ reach, i) for i in range(count)])  2.96 us
    ppermute x1, waiting for transfers between devices, local(): other = lax.ppermute(sums, 'dp', [(i ^ 1, i) for i in range(pair)])  1.25 us
  transfers between devices with their start and end apart: 12, of which 8 were waited for; matrix products, arithmetic and copies ran while one was open for 0% of the time, Pallas kernels for 5%

profile of v1, /device:TPU:0, one launch (start us, length us, event | category | flops | bytes accessed | tf_op | source)
XLA Modules:
  0.0 46.0 jit_solution(13561630773134675243)
XLA Ops:
  0.7 0.8 %copy.13.lists_ref = s32[1,4,2]{2,1,0:T(4,128)S(1)} copy(s32[1,4,2]{1,2,0:T(2,128)} %param.13) | data formatting | bytes 64 | tf_op args[5]
  1.4 0.1 copy.16.rows_ref
  1.5 0.9 %copy-done = bf16[8,64,128]{2,1,0:T(8,128)(2,1)S(1)} copy-done((bf16[8,64,128]{2,1,0:T(8,128)(2,1)S(1)}, bf16[8,64,128]{2,1,0:T(8,128)(2,1)}, u32[]{:S(2)}) %copy-start) | copy-done | bytes 131096
  2.4 0.9 %copy-done.2 = bf16[8,64,128]{2,1,0:T(8,128)(2,1)S(1)} copy-done((bf16[8,64,128]{2,1,0:T(8,128)(2,1)S(1)}, bf16[8,64,128]{2,1,0:T(8,128)(2,1)}, u32[]{:S(2)}) %copy-start.2) | copy-done | bytes 131096
  3.3 1.1 %copy-done.5 = bf16[8,64,576]{2,1,0:T(8,128)(2,1)S(1)} copy-done((bf16[8,64,576]{2,1,0:T(8,128)(2,1)S(1)}, bf16[8,64,576]{2,1,0:T(8,128)(2,1)}, u32[]{:S(2)}) %copy-start.5) | copy-done | bytes 589848
  4.4 2.5 %shard_map.111 = (bf16[272,256]{1,0:T(8,128)(2,1)S(1)}, bf16[272,256]{1,0:T(8,128)(2,1)S(1)}, bf16[272,256]{1,0:T(8,128)(2,1)S(1)}, bf16[272,256]{1,0:T(8,128)(2...) custom-call(s32[8,2]{1,0:T(8,128)S(1)} %copy.16.rows_ref, ...), custom_call_target="tpu_custom_call" | custom-call | flops 268435456 | bytes 2984032 | tf_op jit(solution)/shard_map/pallas_call | solution.py:270
  6.9 3.0 %collective-permute-start = (bf16[272,256]{1,0:T(8,128)(2,1)S(1)}, bf16[272,256]{1,0:T(8,128)(2,1)S(1)}, u32[]{:S(2)}, u32[]{:S(2)}) collective-permute-start(bf16[272,256]{1,0:T(8,128)(2,1)S(1)} %get-tuple-element.28), channel_id=1, source_target_pairs={{2,0},{0,2},{6,4},{4,6},{10,8},{8,10},{14,12},{12,14},{3,1},{1,3},... | collective-permute-start | bytes 417800 | tf_op jit(solution)/shard_map/ppermute | solution.py:30
  9.9 3.6 %collective-permute-start.1 = (bf16[272,256]{1,0:T(8,128)(2,1)S(1)}, bf16[272,256]{1,0:T(8,128)(2,1)S(1)}, u32[]{:S(2)}, u32[]{:S(2)}) collective-permute-start(bf16[272,256]{1,0:T(8,128)(2,1)S(1)} %get-tuple-element.29), channel_id=1, source_target_pairs={{14,0},{4,2},{2,4},{8,6},{6,8},{12,10},{10,12},{0,14},{15,1},{5,3}... | collective-permute-start | bytes 417800 | tf_op jit(solution)/shard_map/ppermute | solution.py:30
  13.5 0.0 collective-permute-start.2
  13.5 0.9 %collective-permute-start.3 = (bf16[272,256]{1,0:T(8,128)(2,1)S(1)}, bf16[272,256]{1,0:T(8,128)(2,1)S(1)}, u32[]{:S(2)}, u32[]{:S(2)}) collective-permute-start(bf16[272,256]{1,0:T(8,128)(2,1)S(1)} %get-tuple-element.31), channel_id=1, source_target_pairs={{12,0},{14,2},{8,4},{10,6},{4,8},{6,10},{0,12},{2,14},{13,1},{15,3... | collective-permute-start | bytes 417800 | tf_op jit(solution)/shard_map/ppermute | solution.py:30
  14.4 1.4 %collective-permute-done.got0 = bf16[272,256]{1,0:T(8,128)(2,1)S(1)} collective-permute-done((bf16[272,256]{1,0:T(8,128)(2,1)S(1)}, bf16[272,256]{1,0:T(8,128)(2,1)S(1)}, u32[]{:S(2)}, u32[]{:S(2)}) %collective-permute-start) | collective-permute-done | bytes 139296 | tf_op jit(solution)/shard_map/ppermute | solution.py:30
  15.8 3.4 %collective-permute-done.1.got1 = bf16[272,256]{1,0:T(8,128)(2,1)S(1)} collective-permute-done((bf16[272,256]{1,0:T(8,128)(2,1)S(1)}, bf16[272,256]{1,0:T(8,128)(2,1)S(1)}, u32[]{:S(2)}, u32[]{:S(2)}) %collective-permute-start.1) | collective-permute-done | bytes 139296 | tf_op jit(solution)/shard_map/ppermute | solution.py:30
  19.2 1.4 %collective-permute-done.2.got2 = bf16[272,256]{1,0:T(8,128)(2,1)S(1)} collective-permute-done((bf16[272,256]{1,0:T(8,128)(2,1)S(1)}, bf16[272,256]{1,0:T(8,128)(2,1)S(1)}, u32[]{:S(2)}, u32[]{:S(2)}) %collective-permute-start.2) | collective-permute-done | bytes 139296 | tf_op jit(solution)/shard_map/ppermute | solution.py:30
  20.6 2.5 %collective-permute-done.3.got3 = bf16[272,256]{1,0:T(8,128)(2,1)S(1)} collective-permute-done((bf16[272,256]{1,0:T(8,128)(2,1)S(1)}, bf16[272,256]{1,0:T(8,128)(2,1)S(1)}, u32[]{:S(2)}, u32[]{:S(2)}) %collective-permute-start.3) | collective-permute-done | bytes 139296 | tf_op jit(solution)/shard_map/ppermute | solution.py:30
  23.1 1.9 %shard_map.112 = (bf16[8,64,256]{2,1,0:T(8,128)(2,1)S(1)}, bf16[8,64,256]{2,1,0:T(8,128)(2,1)S(1)}, bf16[2,256,256]{2,1,0:T(8,128)(2,1)S(1)}, bf16[128,256]{1,0:...) custom-call(s32[8,2]{1,0:T(8,128)S(1)} %copy.16.rows_ref, ...), custom_call_target="tpu_custom_call" | custom-call | flops 536870912 | bytes 3510368 | tf_op jit(solution)/shard_map/pallas_call | solution.py:270
  25.0 0.1 collective-permute-start.8
  25.1 1.2 %collective-permute-done.8 = f32[136,128]{1,0:T(8,128)S(1)} collective-permute-done((f32[136,128]{1,0:T(8,128)S(1)}, f32[136,128]{1,0:T(8,128)S(1)}, u32[]{:S(2)}, u32[]{:S(2)}) %collective-permute-start.8) | collective-permute-done | bytes 69664 | tf_op jit(solution)/shard_map/ppermute | solution.py:349
  26.4 1.3 %collective-permute-start.9 = (f32[136,128]{1,0:T(8,128)S(1)}, f32[136,128]{1,0:T(8,128)S(1)}, u32[]{:S(2)}, u32[]{:S(2)}) collective-permute-start(f32[136,128]{1,0:T(8,128)S(1)} %add.9), channel_id=1, source_target_pairs={{2,0},{0,2},{6,4},{4,6},{10,8},{8,10},{14,12},{12,14},{3,1},{1,3},... | collective-permute-start | bytes 208904 | tf_op jit(solution)/shard_map/ppermute | solution.py:353
  27.6 3.1 %collective-permute-done.9 = f32[136,128]{1,0:T(8,128)S(1)} collective-permute-done((f32[136,128]{1,0:T(8,128)S(1)}, f32[136,128]{1,0:T(8,128)S(1)}, u32[]{:S(2)}, u32[]{:S(2)}) %collective-permute-start.9) | collective-permute-done | bytes 69664 | tf_op jit(solution)/shard_map/ppermute | solution.py:353
  30.7 0.1 collective-permute-start.10
  30.8 1.3 %collective-permute-start.4 = (bf16[128,256]{1,0:T(8,128)(2,1)S(1)}, bf16[128,256]{1,0:T(8,128)(2,1)S(1)}, u32[]{:S(2)}, u32[]{:S(2)}) collective-permute-start(bf16[128,256]{1,0:T(8,128)(2,1)S(1)} %get-tuple-element.35), channel_id=1, source_target_pairs={{2,0},{0,2},{6,4},{4,6},{10,8},{8,10},{14,12},{12,14},{3,1},{1,3},... | collective-permute-start | bytes 196616 | tf_op jit(solution)/shard_map/ppermute | solution.py:30
  32.1 3.6 %collective-permute-start.5 = (bf16[128,256]{1,0:T(8,128)(2,1)S(1)}, bf16[128,256]{1,0:T(8,128)(2,1)S(1)}, u32[]{:S(2)}, u32[]{:S(2)}) collective-permute-start(bf16[128,256]{1,0:T(8,128)(2,1)S(1)} %get-tuple-element.36), channel_id=1, source_target_pairs={{14,0},{4,2},{2,4},{8,6},{6,8},{12,10},{10,12},{0,14},{15,1},{5,3}... | collective-permute-start | bytes 196616 | tf_op jit(solution)/shard_map/ppermute | solution.py:30
  35.7 1.9 %collective-permute-start.7 = (bf16[128,256]{1,0:T(8,128)(2,1)S(1)}, bf16[128,256]{1,0:T(8,128)(2,1)S(1)}, u32[]{:S(2)}, u32[]{:S(2)}) collective-permute-start(bf16[128,256]{1,0:T(8,128)(2,1)S(1)} %get-tuple-element.38), channel_id=1, source_target_pairs={{12,0},{14,2},{8,4},{10,6},{4,8},{6,10},{0,12},{2,14},{13,1},{15,3... | collective-permute-start | bytes 196616 | tf_op jit(solution)/shard_map/ppermute | solution.py:30
  37.6 0.0 collective-permute-done.10
  37.7 1.6 %collective-permute-start.11 = (f32[136,128]{1,0:T(8,128)S(1)}, f32[136,128]{1,0:T(8,128)S(1)}, u32[]{:S(2)}, u32[]{:S(2)}) collective-permute-start(f32[136,128]{1,0:T(8,128)S(1)} %add.11.mine_ref), channel_id=1, source_target_pairs={{8,0},{10,2},{12,4},{14,6},{0,8},{2,10},{4,12},{6,14},{9,1},{11,3}... | collective-permute-start | bytes 208904 | tf_op jit(solution)/shard_map/ppermute | solution.py:353
  39.3 0.0 collective-permute-done.4.got0
  39.3 0.0 collective-permute-done.5.got1
  39.3 1.4 %collective-permute-done.6.got2 = bf16[128,256]{1,0:T(8,128)(2,1)S(1)} collective-permute-done((bf16[128,256]{1,0:T(8,128)(2,1)S(1)}, bf16[128,256]{1,0:T(8,128)(2,1)S(1)}, u32[]{:S(2)}, u32[]{:S(2)}) %collective-permute-start.6) | collective-permute-done | bytes 65568 | tf_op jit(solution)/shard_map/ppermute | solution.py:30
  40.6 1.6 %collective-permute-done.7.got3 = bf16[128,256]{1,0:T(8,128)(2,1)S(1)} collective-permute-done((bf16[128,256]{1,0:T(8,128)(2,1)S(1)}, bf16[128,256]{1,0:T(8,128)(2,1)S(1)}, u32[]{:S(2)}, u32[]{:S(2)}) %collective-permute-start.7) | collective-permute-done | bytes 65568 | tf_op jit(solution)/shard_map/ppermute | solution.py:30
  42.2 0.7 %copy-done.4 = f32[64]{0:T(128)S(1)} copy-done((f32[64]{0:T(128)S(1)}, f32[64]{0:T(128)}, u32[]{:S(2)}) %copy-start.4) | copy-done | bytes 280
  42.8 2.4 %shard_map.113 = (bf16[8,64,128]{2,1,0:T(8,128)(2,1)}, bf16[8,64,128]{2,1,0:T(8,128)(2,1)}) custom-call(s32[8,2]{1,0:T(8,128)S(1)} %copy.16.rows_ref, bf16[8,64,128]{2,1,0:T(8,128)(2,1)S(1)} %copy-done.1, bf16[8,64,128]{2,1,0:T(8,128)(2,1)S(1)} %copy-done.2, bf16[4,64,64]{2,1,0:T(8,128)(2,1)S(1)} %copy-done.3, f32[1,64]{1,0:T(1,128)S(1)} %bitcast.2, ...), custom_call_target="tpu_custom_call" | custom-call | flops 536870912 | bytes 2392384 | tf_op jit(solution)/shard_map/pallas_call | solution.py:270
  45.2 0.7 %shard_map.114 = (f32[4,64,64]{2,1,0:T(8,128)}, f32[1,64]{1,0:T(1,128)}) custom-call(f32[136,128]{1,0:T(8,128)S(1)} %add.11.mine_ref, f32[136,128]{1,0:T(8,128)S(1)} %collective-permute-done.11.other_ref), custom_call_target="tpu_custom_call" | custom-call | flops 17408 | bytes 205056 | tf_op jit(solution)/shard_map/pallas_call | solution.py:270
  (17 shorter events, 0.1 us)
Async XLA Ops:
  0.6 0.8 %copy-start.7 = (s32[8,2]{0,1:T(2,128)S(1)}, s32[8,2]{0,1:T(2,128)}, u32[]{:S(2)}) copy-start(s32[8,2]{0,1:T(2,128)} %param.12) | copy-start | bytes 196
  0.6 0.9 %copy-start.6 = (s32[8,64]{1,0:T(8,128)S(1)}, s32[8,64]{1,0:T(8,128)}, u32[]{:S(2)}) copy-start(s32[8,64]{1,0:T(8,128)} %mask_ref.1) | copy-start | bytes 6148
  1.5 0.9 %copy-start = (bf16[8,64,128]{2,1,0:T(8,128)(2,1)S(1)}, bf16[8,64,128]{2,1,0:T(8,128)(2,1)}, u32[]{:S(2)}) copy-start(bf16[8,64,128]{2,1,0:T(8,128)(2,1)} %feat_ref.5) | copy-start | bytes 393220
  2.4 0.9 %copy-start.2 = (bf16[8,64,128]{2,1,0:T(8,128)(2,1)S(1)}, bf16[8,64,128]{2,1,0:T(8,128)(2,1)}, u32[]{:S(2)}) copy-start(bf16[8,64,128]{2,1,0:T(8,128)(2,1)} %cot_ref.5) | copy-start | bytes 393220
  3.3 1.1 %copy-start.5 = (bf16[8,64,576]{2,1,0:T(8,128)(2,1)S(1)}, bf16[8,64,576]{2,1,0:T(8,128)(2,1)}, u32[]{:S(2)}) copy-start(bf16[8,64,576]{2,1,0:T(8,128)(2,1)} %lap_ref.1) | copy-start | bytes 1769476
  4.4 18.7 %copy-start.1 = (bf16[8,64,128]{2,1,0:T(8,128)(2,1)S(1)}, bf16[8,64,128]{2,1,0:T(8,128)(2,1)}, u32[]{:S(2)}) copy-start(bf16[8,64,128]{2,1,0:T(8,128)(2,1)} %feat_ref.5) | copy-start | bytes 393220
  6.9 8.9 %collective-permute-start = (bf16[272,256]{1,0:T(8,128)(2,1)S(1)}, bf16[272,256]{1,0:T(8,128)(2,1)S(1)}, u32[]{:S(2)}, u32[]{:S(2)}) collective-permute-start(bf16[272,256]{1,0:T(8,128)(2,1)S(1)} %get-tuple-element.28), channel_id=1, source_target_pairs={{2,0},{0,2},{6,4},{4,6},{10,8},{8,10},{14,12},{12,14},{3,1},{1,3},... | collective-permute-start | bytes 417800 | tf_op jit(solution)/shard_map/ppermute | solution.py:30
  9.9 9.3 %collective-permute-start.1 = (bf16[272,256]{1,0:T(8,128)(2,1)S(1)}, bf16[272,256]{1,0:T(8,128)(2,1)S(1)}, u32[]{:S(2)}, u32[]{:S(2)}) collective-permute-start(bf16[272,256]{1,0:T(8,128)(2,1)S(1)} %get-tuple-element.29), channel_id=1, source_target_pairs={{14,0},{4,2},{2,4},{8,6},{6,8},{12,10},{10,12},{0,14},{15,1},{5,3}... | collective-permute-start | bytes 417800 | tf_op jit(solution)/shard_map/ppermute | solution.py:30
  13.5 7.1 %collective-permute-start.2 = (bf16[272,256]{1,0:T(8,128)(2,1)S(1)}, bf16[272,256]{1,0:T(8,128)(2,1)S(1)}, u32[]{:S(2)}, u32[]{:S(2)}) collective-permute-start(bf16[272,256]{1,0:T(8,128)(2,1)S(1)} %get-tuple-element.30), channel_id=1, source_target_pairs={{4,0},{6,2},{0,4},{2,6},{12,8},{14,10},{8,12},{10,14},{5,1},{7,3},... | collective-permute-start | bytes 417800 | tf_op jit(solution)/shard_map/ppermute | solution.py:30
  13.5 9.6 %collective-permute-start.3 = (bf16[272,256]{1,0:T(8,128)(2,1)S(1)}, bf16[272,256]{1,0:T(8,128)(2,1)S(1)}, u32[]{:S(2)}, u32[]{:S(2)}) collective-permute-start(bf16[272,256]{1,0:T(8,128)(2,1)S(1)} %get-tuple-element.31), channel_id=1, source_target_pairs={{12,0},{14,2},{8,4},{10,6},{4,8},{6,10},{0,12},{2,14},{13,1},{15,3... | collective-permute-start | bytes 417800 | tf_op jit(solution)/shard_map/ppermute | solution.py:30
  25.0 1.3 %collective-permute-start.8 = (f32[136,128]{1,0:T(8,128)S(1)}, f32[136,128]{1,0:T(8,128)S(1)}, u32[]{:S(2)}, u32[]{:S(2)}) collective-permute-start(f32[136,128]{1,0:T(8,128)S(1)} %get-tuple-element.41), channel_id=1, source_target_pairs={{1,0},{0,1},{3,2},{2,3},{5,4},{4,5},{7,6},{6,7},{9,8},{8,9},{11,10... | collective-permute-start | bytes 208904 | tf_op jit(solution)/shard_map/ppermute | solution.py:349
  26.4 4.4 %collective-permute-start.9 = (f32[136,128]{1,0:T(8,128)S(1)}, f32[136,128]{1,0:T(8,128)S(1)}, u32[]{:S(2)}, u32[]{:S(2)}) collective-permute-start(f32[136,128]{1,0:T(8,128)S(1)} %add.9), channel_id=1, source_target_pairs={{2,0},{0,2},{6,4},{4,6},{10,8},{8,10},{14,12},{12,14},{3,1},{1,3},... | collective-permute-start | bytes 208904 | tf_op jit(solution)/shard_map/ppermute | solution.py:353
  30.7 6.9 %collective-permute-start.10 = (f32[136,128]{1,0:T(8,128)S(1)}, f32[136,128]{1,0:T(8,128)S(1)}, u32[]{:S(2)}, u32[]{:S(2)}) collective-permute-start(f32[136,128]{1,0:T(8,128)S(1)} %add.10), channel_id=1, source_target_pairs={{4,0},{6,2},{0,4},{2,6},{12,8},{14,10},{8,12},{10,14},{5,1},{7,3},... | collective-permute-start | bytes 208904 | tf_op jit(solution)/shard_map/ppermute | solution.py:353
  30.8 8.4 %collective-permute-start.4 = (bf16[128,256]{1,0:T(8,128)(2,1)S(1)}, bf16[128,256]{1,0:T(8,128)(2,1)S(1)}, u32[]{:S(2)}, u32[]{:S(2)}) collective-permute-start(bf16[128,256]{1,0:T(8,128)(2,1)S(1)} %get-tuple-element.35), channel_id=1, source_target_pairs={{2,0},{0,2},{6,4},{4,6},{10,8},{8,10},{14,12},{12,14},{3,1},{1,3},... | collective-permute-start | bytes 196616 | tf_op jit(solution)/shard_map/ppermute | solution.py:30
  32.1 7.1 %collective-permute-start.5 = (bf16[128,256]{1,0:T(8,128)(2,1)S(1)}, bf16[128,256]{1,0:T(8,128)(2,1)S(1)}, u32[]{:S(2)}, u32[]{:S(2)}) collective-permute-start(bf16[128,256]{1,0:T(8,128)(2,1)S(1)} %get-tuple-element.36), channel_id=1, source_target_pairs={{14,0},{4,2},{2,4},{8,6},{6,8},{12,10},{10,12},{0,14},{15,1},{5,3}... | collective-permute-start | bytes 196616 | tf_op jit(solution)/shard_map/ppermute | solution.py:30
  35.7 4.9 %collective-permute-start.6 = (bf16[128,256]{1,0:T(8,128)(2,1)S(1)}, bf16[128,256]{1,0:T(8,128)(2,1)S(1)}, u32[]{:S(2)}, u32[]{:S(2)}) collective-permute-start(bf16[128,256]{1,0:T(8,128)(2,1)S(1)} %get-tuple-element.37), channel_id=1, source_target_pairs={{4,0},{6,2},{0,4},{2,6},{12,8},{14,10},{8,12},{10,14},{5,1},{7,3},... | collective-permute-start | bytes 196616 | tf_op jit(solution)/shard_map/ppermute | solution.py:30
  35.7 6.5 %copy-start.3 = (bf16[4,64,64]{2,1,0:T(8,128)(2,1)S(1)}, bf16[4,64,64]{2,1,0:T(8,128)(2,1)}, u32[]{:S(2)}) copy-start(bf16[4,64,64]{2,1,0:T(8,128)(2,1)} %weight_ref.1) | copy-start | bytes 98308
  35.7 6.5 %collective-permute-start.7 = (bf16[128,256]{1,0:T(8,128)(2,1)S(1)}, bf16[128,256]{1,0:T(8,128)(2,1)S(1)}, u32[]{:S(2)}, u32[]{:S(2)}) collective-permute-start(bf16[128,256]{1,0:T(8,128)(2,1)S(1)} %get-tuple-element.38), channel_id=1, source_target_pairs={{12,0},{14,2},{8,4},{10,6},{4,8},{6,10},{0,12},{2,14},{13,1},{15,3... | collective-permute-start | bytes 196616 | tf_op jit(solution)/shard_map/ppermute | solution.py:30
  37.7 7.6 %collective-permute-start.11 = (f32[136,128]{1,0:T(8,128)S(1)}, f32[136,128]{1,0:T(8,128)S(1)}, u32[]{:S(2)}, u32[]{:S(2)}) collective-permute-start(f32[136,128]{1,0:T(8,128)S(1)} %add.11.mine_ref), channel_id=1, source_target_pairs={{8,0},{10,2},{12,4},{14,6},{0,8},{2,10},{4,12},{6,14},{9,1},{11,3}... | collective-permute-start | bytes 208904 | tf_op jit(solution)/shard_map/ppermute | solution.py:353
  42.2 0.7 %copy-start.4 = (f32[64]{0:T(128)S(1)}, f32[64]{0:T(128)}, u32[]{:S(2)}) copy-start(f32[64]{0:T(128)} %param.10) | copy-start | bytes 772

commit v2 on v1

v2 whole, which is shorter than its diff:
```python
import functools
import math

import jax
import jax.numpy as jnp
from jax import lax
from jax.experimental import pallas as pl
from jax.experimental.pallas import tpu as pltpu
from jax.sharding import PartitionSpec as P

CYCLE_STEPS = (0, -1, 1, -2, 2, -3, 3)
ORDER = (1, 3, 0, 2)
F32 = jnp.float32
BF16 = jnp.bfloat16


def pair_of(index, pairing, count):
    if pairing == 0:
        return index ^ 1
    if pairing == 1:
        return (index + 1 if index % 2 else index - 1) % count
    low = index % 4 < 2
    step = 2 if low == (pairing == 2) else -2
    return (index + step) % count


def exchange(block, pairing):
    count = lax.axis_size("pix")
    route = [(pair_of(i, pairing, count), i) for i in range(count)]
    return lax.ppermute(block, "pix", route)


def send_heading(pairing, device):
    if pairing < 2:
        return (device + pairing) % 2
    return 2 + (device // 2 + pairing) % 2


def matmul(left, right):
    return jnp.dot(left, right, preferred_element_type=F32)


def matmul_tn(left, right):
    return lax.dot_general(left, right, (((0,), (0,)), ((), ())), preferred_element_type=F32)


def matmul_nt(left, right):
    return lax.dot_general(left, right, (((1,), (1,)), ((), ())), preferred_element_type=F32)


def row_of_slot(rows_ref, slot):
    blocks = rows_ref.shape[1]
    found = jnp.int32(0)
    for a in range(blocks):
        found = jnp.where(rows_ref[0, a] == blocks + slot, a, found)
    return found


def ring_rows(field, a):
    blocks = field.shape[0]
    return [field[(a + step) % blocks] for step in CYCLE_STEPS]


def pack_kernel(
    rows_hbm, lists_hbm, mask_hbm, feat_hbm, cot_hbm, lap_hbm, weight_hbm, bias_hbm,
    *refs,
):
    sends, (value, keep, part, rows_ref, lists_ref, mix, mix_last, bias_row) = refs[:4], refs[4:12]
    mask, lap, weight, bias, sem = refs[12:]
    blocks, pixels, lanes = feat_hbm.shape
    slots = lists_hbm.shape[1]
    cycle = len(CYCLE_STEPS) * pixels
    device = lax.axis_index("pix")
    copies = [
        pltpu.make_async_copy(mask_hbm, mask, sem.at[0]),
        pltpu.make_async_copy(feat_hbm, value.at[:, :, pl.ds(0, lanes)], sem.at[1]),
        pltpu.make_async_copy(cot_hbm, value.at[:, :, pl.ds(lanes, lanes)], sem.at[2]),
        pltpu.make_async_copy(lap_hbm, lap, sem.at[3]),
        pltpu.make_async_copy(rows_hbm, rows_ref, sem.at[4]),
        pltpu.make_async_copy(lists_hbm, lists_ref, sem.at[5]),
        pltpu.make_async_copy(weight_hbm, weight, sem.at[6]),
        pltpu.make_async_copy(bias_hbm, bias, sem.at[7]),
    ]
    for copy in copies:
        copy.start()
    diagonal = lax.broadcasted_iota(jnp.int32, (pixels, pixels), 0) == lax.broadcasted_iota(
        jnp.int32, (pixels, pixels), 1
    )
    copies[0].wait()
    for a in range(blocks):
        row = mask[a:a + 1, :].astype(F32)
        column = jnp.sum(jnp.where(diagonal, row, 0.0), axis=1, keepdims=True)
        keep[a] = jnp.broadcast_to(column, (pixels, 2 * lanes)).astype(BF16)
    copies[1].wait()
    copies[2].wait()
    masked = [value[a] * keep[a] for a in range(blocks)]
    for a in range(blocks):
        value[a] = masked[a]
    copies[4].wait()
    copies[5].wait()
    copies[3].wait()
    for a in range(blocks):
        total = matmul(lap[a, :, :cycle], jnp.concatenate(ring_rows(value, a), axis=0))
        total = total + matmul(lap[a, :, cycle + pixels:], value[rows_ref[1, a]])
        part[a] = total * keep[a].astype(F32)
    tail = slots * 2 * pixels
    which = lax.broadcasted_iota(jnp.int32, (16, pixels), 0)
    for pairing, send in zip(ORDER, sends):
        heading = send_heading(pairing, device)
        flags = jnp.zeros((16, pixels), F32)
        for s in range(slots):
            b = lists_ref[0, s, heading]
            base = s * 2 * pixels
            send[base:base + pixels, :] = value[b]
            send[base + pixels:base + 2 * pixels, :] = part[b].astype(BF16)
            flags = jnp.where(which == s, mask[pl.ds(b, 1), :].astype(F32), flags)
        send[tail:, :] = jnp.zeros((16, 2 * lanes), BF16)
        send[tail:, :pixels] = flags.astype(BF16)
    copies[6].wait()
    copies[7].wait()
    terms, half, _ = weight.shape
    mix[...] = jnp.zeros_like(mix)
    mix_last[...] = jnp.zeros_like(mix_last)
    for m in range(lanes // half):
        spot = slice(m * half, (m + 1) * half)
        for k in range(terms - 1):
            shifted = slice(k * lanes + m * half, k * lanes + (m + 1) * half)
            mix[spot, shifted] = weight[k]
        mix_last[spot, spot] = weight[terms - 1]
        bias_row[:, spot] = bias[...]


def middle_kernel(
    rows_ref, lists_ref, feat_ref, cot_ref, lap, value, keep, part, *refs,
):
    gots, (one, two, spread), sends, (sums,) = refs[:4], refs[4:7], refs[7:11], refs[11:12]
    halo, halo_part, keep_far = refs[12:]
    blocks, pixels, lanes = feat_ref.shape
    slots = lists_ref.shape[1]
    cycle = len(CYCLE_STEPS) * pixels
    flat, width = blocks * pixels, 2 * lanes
    device = lax.axis_index("pix")
    tail = slots * 2 * pixels
    for pairing, got in zip(ORDER, gots):
        heading = send_heading(pairing, device) ^ 1
        flags = got[tail:, :pixels].astype(F32)
        for s in range(slots):
            row = row_of_slot(rows_ref, heading * slots + s)
            base = s * 2 * pixels
            halo[row] = got[base:base + pixels, :]
            halo_part[row] = got[base + pixels:base + 2 * pixels, :]
            keep_far[pl.ds(row, 1), :] = flags[s:s + 1, :]
    for a in range(blocks):
        cross = lap[a, :, cycle:cycle + pixels] * keep_far[a:a + 1, :].astype(BF16)
        total = part[a] + matmul(cross, halo[a]) * keep[a].astype(F32)
        one[a] = total.astype(BF16)
        total = halo_part[a].astype(F32) + matmul_tn(cross, value[a])
        halo[a] = total.astype(BF16)
    for a in range(blocks):
        near = ring_rows(one, a) + [halo[a], one[rows_ref[1, a]]]
        total = matmul(lap[a], jnp.concatenate(near, axis=0)) * keep[a].astype(F32)
        base = jnp.concatenate([feat_ref[a], cot_ref[a]], axis=1).astype(F32)
        fresh = (2.0 * total - base).astype(BF16)
        two[a] = fresh
        spread[a] = fresh * keep[a]
    for pairing, send in zip(ORDER, sends):
        heading = send_heading(pairing, device)
        for s in range(slots):
            send[s * pixels:(s + 1) * pixels, :] = spread[lists_ref[0, s, heading]]
    feat = feat_ref[...].reshape(flat, lanes)
    cot = cot_ref[...].reshape(flat, lanes)
    first = one[...].reshape(flat, width)
    second = two[...].reshape(flat, width)
    half = lanes // 2
    low = matmul_tn(jnp.concatenate([feat, first[:, :lanes]], axis=1), cot)
    high = matmul_tn(
        jnp.concatenate([first[:, :lanes], second[:, :lanes]], axis=1), first[:, lanes:]
    )

    def trace(product, start):
        return (
            product[start:start + half, :half] + product[start + half:start + lanes, half:]
        )

    sum_zero = trace(low, 0)
    sum_one = trace(low, lanes)
    sums[:half, :half] = sum_zero
    sums[:half, half:] = sum_one
    sums[half:lanes, :half] = 2.0 * trace(high, 0) - sum_zero
    sums[half:lanes, half:] = 2.0 * trace(high, lanes) - sum_one
    sums[lanes:, :] = jnp.broadcast_to(
        jnp.sum(cot.astype(F32), axis=0, keepdims=True), (8, lanes)
    )


def partial_kernel(feat_ref, cot_ref, mix, bias_row, one, two, out_part, grad_part):
    blocks, pixels, lanes = feat_ref.shape
    flat = blocks * pixels
    first = one[...].reshape(flat, 2 * lanes)
    second = two[...].reshape(flat, 2 * lanes)
    total = jnp.broadcast_to(bias_row[...], (flat, lanes))
    fields = [feat_ref[...].reshape(flat, lanes), first[:, :lanes], second[:, :lanes]]
    for k, field in enumerate(fields):
        total = total + matmul(field, mix[:, k * lanes:(k + 1) * lanes])
    out_part[...] = total.reshape(blocks, pixels, lanes)
    fields = [cot_ref[...].reshape(flat, lanes), first[:, lanes:], second[:, lanes:]]
    total = matmul_nt(jnp.concatenate(fields, axis=1), mix[...])
    grad_part[...] = total.reshape(blocks, pixels, lanes)


def last_kernel(
    rows_ref, lap, keep, one, spread, out_part, grad_part, mix_last, *refs,
):
    gots, (out_ref, grad_ref), (halo, three) = refs[:4], refs[4:6], refs[6:]
    blocks, pixels, lanes = out_part.shape
    device = lax.axis_index("pix")
    slots = gots[0].shape[0] // pixels
    for pairing, got in zip(ORDER, gots):
        heading = send_heading(pairing, device) ^ 1
        for s in range(slots):
            row = row_of_slot(rows_ref, heading * slots + s)
            halo[row] = got[s * pixels:(s + 1) * pixels, :]
    for a in range(blocks):
        near = ring_rows(spread, a) + [halo[a], spread[rows_ref[1, a]]]
        total = matmul(lap[a], jnp.concatenate(near, axis=0)) * keep[a].astype(F32)
        three[a] = (2.0 * total - one[a].astype(F32)).astype(BF16)
    flat = blocks * pixels
    last = three[...].reshape(flat, 2 * lanes)
    total = out_part[...].reshape(flat, lanes) + matmul(last[:, :lanes], mix_last[...])
    out_ref[...] = total.astype(BF16).reshape(blocks, pixels, lanes)
    total = grad_part[...].reshape(flat, lanes) + matmul_nt(last[:, lanes:], mix_last[...])
    grad_ref[...] = total.astype(BF16).reshape(blocks, pixels, lanes)


def finish_kernel(factor, mine, other, weight_ref, bias_ref):
    sums = (mine[...] + other[...]) * factor
    terms, half, _ = weight_ref.shape
    lanes = 2 * half
    for k in range(terms):
        rows, cols = k // 2 * half, k % 2 * half
        weight_ref[k] = sums[rows:rows + half, cols:cols + half]
    bias = sums[lanes:lanes + 1, :]
    bias_ref[...] = bias[:, :half] + bias[:, half:]


def call(kernel, outs, ins, scratch, flops, in_hbm=False):
    vmem = pl.BlockSpec(memory_space=pltpu.VMEM)
    smem = pl.BlockSpec(memory_space=pltpu.SMEM)
    hbm = pl.BlockSpec(memory_space=pltpu.MemorySpace.HBM)
    touched = sum(math.prod(x.shape) * x.dtype.itemsize for x in [*ins, *outs])
    if in_hbm:
        ins = [pltpu.with_memory_space_constraint(x, pltpu.MemorySpace.HBM) for x in ins]

    def place(i, x):
        if in_hbm:
            return hbm
        return smem if i < 2 and x.dtype == jnp.int32 else vmem

    return pl.pallas_call(
        kernel,
        out_shape=outs,
        in_specs=[place(i, x) for i, x in enumerate(ins)],
        out_specs=[smem if x.dtype == jnp.int32 else vmem for x in outs],
        scratch_shapes=scratch,
        cost_estimate=pl.CostEstimate(flops=flops, transcendentals=0, bytes_accessed=touched),
        compiler_params=pltpu.CompilerParams(vmem_limit_bytes=32 << 20),
    )(*ins)


def local(
    features, cheb_weights, out_bias, lap_tiles, neighbours, send_blocks, pixel_mask, cotangent
):
    blocks, pixels, lanes = features.shape
    terms, chan_in, chan_out = cheb_weights.shape
    slots = send_blocks.shape[2]
    width, flat = 2 * lanes, blocks * pixels
    shape = jax.ShapeDtypeStruct
    apply_flops = 2 * flat * width * lap_tiles.shape[2]
    rows = neighbours.T
    lists = send_blocks.transpose(0, 2, 1)

    field = shape((blocks, pixels, width), BF16)
    wide = shape((blocks, pixels, width), F32)
    scratch_field = pltpu.VMEM((blocks, pixels, width), BF16)
    *sends, value, keep, part, rows, lists, mix, mix_last, bias_row = call(
        pack_kernel,
        [shape((slots * 2 * pixels + 16, width), BF16)] * 4 + [field, field, wide]
        + [shape(rows.shape, jnp.int32), shape(lists.shape, jnp.int32)]
        + [shape((lanes, (terms - 1) * lanes), BF16), shape((lanes, lanes), BF16)]
        + [shape((1, lanes), F32)],
        [rows, lists, pixel_mask, features, cotangent, lap_tiles, cheb_weights]
        + [out_bias.reshape(1, chan_out)],
        [
            pltpu.VMEM((blocks, pixels), jnp.int32),
            pltpu.VMEM(lap_tiles.shape, BF16),
            pltpu.VMEM(cheb_weights.shape, BF16),
            pltpu.VMEM((1, chan_out), F32),
            pltpu.SemaphoreType.DMA((8,)),
        ],
        apply_flops,
        in_hbm=True,
    )
    gots = [exchange(send, k) for k, send in zip(ORDER, sends)]
    one, two, spread, *sends, sums = call(
        middle_kernel,
        [field, field, field]
        + [shape((slots * pixels, width), BF16)] * 4
        + [shape((lanes + 8, lanes), F32)],
        [rows, lists, features, cotangent, lap_tiles, value, keep, part, *gots],
        [scratch_field, scratch_field, pltpu.VMEM((blocks, pixels), F32)],
        2 * apply_flops,
    )
    gots = [exchange(send, k) for k, send in zip(ORDER, sends)]
    half_field = shape((blocks, pixels, lanes), F32)
    parts = call(
        partial_kernel,
        [half_field, half_field],
        [features, cotangent, mix, bias_row, one, two],
        [],
        4 * flat * lanes * lanes * (terms - 1),
    )
    count = lax.axis_size("pix")
    pair = lax.axis_size("dp")
    factor = 1.0 / math.sqrt(flat * (lanes // chan_in) * count * pair)
    other = lax.ppermute(sums, "dp", [(i ^ 1, i) for i in range(pair)])
    reach = 1
    while reach < count:
        sums = sums + other
        other = lax.ppermute(sums, "pix", [(i ^ reach, i) for i in range(count)])
        reach *= 2
    output_maps, grad_features = call(
        last_kernel,
        [shape(features.shape, BF16), shape(features.shape, BF16)],
        [rows, lap_tiles, keep, one, spread, *parts, mix_last, *gots],
        [scratch_field, scratch_field],
        2 * apply_flops,
    )
    grad_weights, grad_bias = call(
        functools.partial(finish_kernel, factor),
        [shape(cheb_weights.shape, F32), shape((1, chan_out), F32)],
        [sums, other],
        [],
        sums.size,
    )
    return output_maps, grad_features, grad_weights, grad_bias.reshape(chan_out)


def solution(mesh):
    return jax.shard_map(
        local,
        mesh=mesh,
        in_specs=(
            P("pix", None, ("groups", "dp")),
            P(),
            P(),
            P("pix", None, None),
            P("pix", None),
            P("pix", None, None),
            P("pix", None),
            P("pix", None, ("groups", "dp")),
        ),
        out_specs=(
            P("pix", None, ("groups", "dp")),
            P("pix", None, ("groups", "dp")),
            P("groups", None, None),
            P("groups"),
        ),
        check_vma=False,
    )
```

time: 46.2 us -> 41.2 us (0.89)
  local copies, waits for them, and re-layouts: 4.42 us -> 0.01 us
  waiting for transfers between devices: 15.9 us -> 14.8 us
    unnamed x18 -> x6, local copies, waits for them, and re-layouts: 4.42 us -> 0.01 us
    ppermute x3, starting transfers between devices: 2.96 us -> 4.67 us  [local(): other = lax.ppermute(sums, 'pix', [(i ^ reach, i) for i in range(count)])]
    ppermute x8, starting transfers between devices: 14.3 us -> 13 us  [exchange(): return lax.ppermute(block, 'pix', route)]
    ppermute x8, waiting for transfers between devices: 11.6 us -> 10.6 us  [exchange(): return lax.ppermute(block, 'pix', route)]
    pallas_call x4 -> x5, Pallas kernels: 7.55 us -> 7.71 us  [call(): pl.pallas_call(kernel, out_shape=outs, in_specs=[place(i, x) for i, x in...]
  transfers between devices with their start and end apart: 12 -> 12, of which waited for: 8 -> 8; matrix products, arithmetic and copies ran while one was open for 0% -> 0% of each run, Pallas kernels for 5% -> 6%
where the time goes in v2:
time: 41.2 us; the launch traced here: 41 us
  starting transfers between devices  17.7 us (43%)
  waiting for transfers between devices  14.8 us (36%)
  Pallas kernels  7.71 us (19%)
  between operations  0.71 us (2%)
    ppermute x8, starting transfers between devices, exchange(): return lax.ppermute(block, 'pix', route)  13 us
    ppermute x8, waiting for transfers between devices, exchange(): return lax.ppermute(block, 'pix', route)  10.6 us
    pallas_call x5, Pallas kernels, call(): pl.pallas_call(kernel, out_shape=outs, in_specs=[place(i, x) for i, x in...  7.71 us
    ppermute x3, starting transfers between devices, local(): other = lax.ppermute(sums, 'pix', [(i ^ reach, i) for i in range(count)])  4.67 us
    ppermute x3, waiting for transfers between devices, local(): other = lax.ppermute(sums, 'pix', [(i ^ reach, i) for i in range(count)])  2.98 us
    ppermute x1, waiting for transfers between devices, local(): other = lax.ppermute(sums, 'dp', [(i ^ 1, i) for i in range(pair)])  1.25 us
  transfers between devices with their start and end apart: 12, of which 8 were waited for; matrix products, arithmetic and copies ran while one was open for 0% of the time, Pallas kernels for 6%

profile of v2, /device:TPU:0, one launch (start us, length us, event | category | flops | bytes accessed | tf_op | source)
XLA Modules:
  0.0 41.0 jit_solution(3604523812800449376)
XLA Ops:
  0.6 0.0 copy-start
  0.6 0.0 copy-start.1
  0.7 0.0 copy-start.2
  0.7 2.6 %shard_map.111 = (bf16[272,256]{1,0:T(8,128)(2,1)S(1)}, bf16[272,256]{1,0:T(8,128)(2,1)S(1)}, bf16[272,256]{1,0:T(8,128)(2,1)S(1)}, bf16[272,256]{1,0:T(8,128)(2...) custom-call(s32[2,8]{1,0:T(2,128)} %bitcast.4, ...), custom_call_target="tpu_custom_call" | custom-call | flops 150994944 | bytes 2624448 | tf_op jit(solution)/shard_map/pallas_call | solution.py:259
  3.2 6.0 %collective-permute-start = (bf16[272,256]{1,0:T(8,128)(2,1)S(1)}, bf16[272,256]{1,0:T(8,128)(2,1)S(1)}, u32[]{:S(2)}, u32[]{:S(2)}) collective-permute-start(bf16[272,256]{1,0:T(8,128)(2,1)S(1)} %get-tuple-element.35), channel_id=1, source_target_pairs={{14,0},{4,2},{2,4},{8,6},{6,8},{12,10},{10,12},{0,14},{15,1},{5,3}... | collective-permute-start | bytes 417800 | tf_op jit(solution)/shard_map/ppermute | solution.py:30
  9.3 0.5 %collective-permute-start.1 = (bf16[272,256]{1,0:T(8,128)(2,1)S(1)}, bf16[272,256]{1,0:T(8,128)(2,1)S(1)}, u32[]{:S(2)}, u32[]{:S(2)}) collective-permute-start(bf16[272,256]{1,0:T(8,128)(2,1)S(1)} %get-tuple-element.36), channel_id=1, source_target_pairs={{12,0},{14,2},{8,4},{10,6},{4,8},{6,10},{0,12},{2,14},{13,1},{15,3... | collective-permute-start | bytes 417800 | tf_op jit(solution)/shard_map/ppermute | solution.py:30
  9.7 0.2 collective-permute-start.2
  9.9 1.0 %collective-permute-start.3 = (bf16[272,256]{1,0:T(8,128)(2,1)S(1)}, bf16[272,256]{1,0:T(8,128)(2,1)S(1)}, u32[]{:S(2)}, u32[]{:S(2)}) collective-permute-start(bf16[272,256]{1,0:T(8,128)(2,1)S(1)} %get-tuple-element.38), channel_id=1, source_target_pairs={{4,0},{6,2},{0,4},{2,6},{12,8},{14,10},{8,12},{10,14},{5,1},{7,3},... | collective-permute-start | bytes 417800 | tf_op jit(solution)/shard_map/ppermute | solution.py:30
  11.0 3.0 %collective-permute-done.refs_0_ = bf16[272,256]{1,0:T(8,128)(2,1)S(1)} collective-permute-done((bf16[272,256]{1,0:T(8,128)(2,1)S(1)}, bf16[272,256]{1,0:T(8,128)(2,1)S(1)}, u32[]{:S(2)}, u32[]{:S(2)}) %collective-permute-start) | collective-permute-done | bytes 139296 | tf_op jit(solution)/shard_map/ppermute | solution.py:30
  14.0 3.7 %collective-permute-done.1.refs_1_ = bf16[272,256]{1,0:T(8,128)(2,1)S(1)} collective-permute-done((bf16[272,256]{1,0:T(8,128)(2,1)S(1)}, bf16[272,256]{1,0:T(8,128)(2,1)S(1)}, u32[]{:S(2)}, u32[]{:S(2)}) %collective-permute-start.1) | collective-permute-done | bytes 139296 | tf_op jit(solution)/shard_map/ppermute | solution.py:30
  17.7 0.0 collective-permute-done.2.refs_2_
  17.7 0.6 %collective-permute-done.3.refs_3_ = bf16[272,256]{1,0:T(8,128)(2,1)S(1)} collective-permute-done((bf16[272,256]{1,0:T(8,128)(2,1)S(1)}, bf16[272,256]{1,0:T(8,128)(2,1)S(1)}, u32[]{:S(2)}, u32[]{:S(2)}) %collective-permute-start.3) | collective-permute-done | bytes 139296 | tf_op jit(solution)/shard_map/ppermute | solution.py:30
  18.3 2.1 %shard_map.112 = (bf16[8,64,256]{2,1,0:T(8,128)(2,1)S(1)}, bf16[8,64,256]{2,1,0:T(8,128)(2,1)S(1)}, bf16[8,64,256]{2,1,0:T(8,128)(2,1)S(1)}, bf16[128,256]{1,0:T...) custom-call(s32[2,8]{1,0:T(2,128)S(1)} %get-tuple-element.30.rows_re, ...), custom_call_target="tpu_custom_call" | custom-call | flops 301989888 | bytes 3575904 | tf_op jit(solution)/shard_map/pallas_call | solution.py:259
  20.4 0.1 collective-permute-start.8
  20.4 1.2 %collective-permute-done.8 = f32[136,128]{1,0:T(8,128)S(1)} collective-permute-done((f32[136,128]{1,0:T(8,128)S(1)}, f32[136,128]{1,0:T(8,128)S(1)}, u32[]{:S(2)}, u32[]{:S(2)}) %collective-permute-start.8) | collective-permute-done | bytes 69664 | tf_op jit(solution)/shard_map/ppermute | solution.py:325
  21.7 1.4 %collective-permute-start.9 = (f32[136,128]{1,0:T(8,128)S(1)}, f32[136,128]{1,0:T(8,128)S(1)}, u32[]{:S(2)}, u32[]{:S(2)}) collective-permute-start(f32[136,128]{1,0:T(8,128)S(1)} %add.9), channel_id=1, source_target_pairs={{2,0},{0,2},{6,4},{4,6},{10,8},{8,10},{14,12},{12,14},{3,1},{1,3},... | collective-permute-start | bytes 208904 | tf_op jit(solution)/shard_map/ppermute | solution.py:329
  23.1 3.0 %collective-permute-done.9 = f32[136,128]{1,0:T(8,128)S(1)} collective-permute-done((f32[136,128]{1,0:T(8,128)S(1)}, f32[136,128]{1,0:T(8,128)S(1)}, u32[]{:S(2)}, u32[]{:S(2)}) %collective-permute-start.9) | collective-permute-done | bytes 69664 | tf_op jit(solution)/shard_map/ppermute | solution.py:329
  26.1 2.6 %collective-permute-start.10 = (f32[136,128]{1,0:T(8,128)S(1)}, f32[136,128]{1,0:T(8,128)S(1)}, u32[]{:S(2)}, u32[]{:S(2)}) collective-permute-start(f32[136,128]{1,0:T(8,128)S(1)} %add.10), channel_id=1, source_target_pairs={{4,0},{6,2},{0,4},{2,6},{12,8},{14,10},{8,12},{10,14},{5,1},{7,3},... | collective-permute-start | bytes 208904 | tf_op jit(solution)/shard_map/ppermute | solution.py:329
  28.6 1.5 %collective-permute-start.4 = (bf16[128,256]{1,0:T(8,128)(2,1)S(1)}, bf16[128,256]{1,0:T(8,128)(2,1)S(1)}, u32[]{:S(2)}, u32[]{:S(2)}) collective-permute-start(bf16[128,256]{1,0:T(8,128)(2,1)S(1)} %get-tuple-element.47), channel_id=1, source_target_pairs={{14,0},{4,2},{2,4},{8,6},{6,8},{12,10},{10,12},{0,14},{15,1},{5,3}... | collective-permute-start | bytes 196616 | tf_op jit(solution)/shard_map/ppermute | solution.py:30
  30.2 1.9 %collective-permute-start.5 = (bf16[128,256]{1,0:T(8,128)(2,1)S(1)}, bf16[128,256]{1,0:T(8,128)(2,1)S(1)}, u32[]{:S(2)}, u32[]{:S(2)}) collective-permute-start(bf16[128,256]{1,0:T(8,128)(2,1)S(1)} %get-tuple-element.48), channel_id=1, source_target_pairs={{12,0},{14,2},{8,4},{10,6},{4,8},{6,10},{0,12},{2,14},{13,1},{15,3... | collective-permute-start | bytes 196616 | tf_op jit(solution)/shard_map/ppermute | solution.py:30
  32.1 1.8 %collective-permute-start.6 = (bf16[128,256]{1,0:T(8,128)(2,1)S(1)}, bf16[128,256]{1,0:T(8,128)(2,1)S(1)}, u32[]{:S(2)}, u32[]{:S(2)}) collective-permute-start(bf16[128,256]{1,0:T(8,128)(2,1)S(1)} %get-tuple-element.49), channel_id=1, source_target_pairs={{2,0},{0,2},{6,4},{4,6},{10,8},{8,10},{14,12},{12,14},{3,1},{1,3},... | collective-permute-start | bytes 196616 | tf_op jit(solution)/shard_map/ppermute | solution.py:30
  33.9 0.0 collective-permute-start.7
  33.9 0.0 collective-permute-done.10
  33.9 0.7 %collective-permute-start.11 = (f32[136,128]{1,0:T(8,128)S(1)}, f32[136,128]{1,0:T(8,128)S(1)}, u32[]{:S(2)}, u32[]{:S(2)}) collective-permute-start(f32[136,128]{1,0:T(8,128)S(1)} %add.11.mine), channel_id=1, source_target_pairs={{8,0},{10,2},{12,4},{14,6},{0,8},{2,10},{4,12},{6,14},{9,1},{11,3}... | collective-permute-start | bytes 208904 | tf_op jit(solution)/shard_map/ppermute | solution.py:329
  34.7 0.4 shard_map.113
  35.0 1.1 %collective-permute-done.4.refs_0_ = bf16[128,256]{1,0:T(8,128)(2,1)S(1)} collective-permute-done((bf16[128,256]{1,0:T(8,128)(2,1)S(1)}, bf16[128,256]{1,0:T(8,128)(2,1)S(1)}, u32[]{:S(2)}, u32[]{:S(2)}) %collective-permute-start.4) | collective-permute-done | bytes 65568 | tf_op jit(solution)/shard_map/ppermute | solution.py:30
  36.1 0.6 %collective-permute-done.5.refs_1_ = bf16[128,256]{1,0:T(8,128)(2,1)S(1)} collective-permute-done((bf16[128,256]{1,0:T(8,128)(2,1)S(1)}, bf16[128,256]{1,0:T(8,128)(2,1)S(1)}, u32[]{:S(2)}, u32[]{:S(2)}) %collective-permute-start.5) | collective-permute-done | bytes 65568 | tf_op jit(solution)/shard_map/ppermute | solution.py:30
  36.6 0.0 collective-permute-done.6.refs_2_
  36.6 1.6 %collective-permute-done.7.refs_3_ = bf16[128,256]{1,0:T(8,128)(2,1)S(1)} collective-permute-done((bf16[128,256]{1,0:T(8,128)(2,1)S(1)}, bf16[128,256]{1,0:T(8,128)(2,1)S(1)}, u32[]{:S(2)}, u32[]{:S(2)}) %collective-permute-start.7) | collective-permute-done | bytes 65568 | tf_op jit(solution)/shard_map/ppermute | solution.py:30
  38.3 2.0 %shard_map.114 = (bf16[8,64,128]{2,1,0:T(8,128)(2,1)}, bf16[8,64,128]{2,1,0:T(8,128)(2,1)}) custom-call(s32[2,8]{1,0:T(2,128)S(1)} %get-tuple-element.30.rows_ref, bf16[8,64,576]{2,1,0:T(8,128)(2,1)S(1)} %copy-done, bf16[8,64,256]{2,1,0:T(8,128)(2,1)S(1)} %get-tuple-element.31.keep, bf16[8,64,256]{2,1,0:T(8,128)(2,1)S(1)} %get-tuple-element.39.one, ...), custom_call_target="tpu_custom_call" | custom-call | flops 301989888 | bytes 2457664 | tf_op jit(solution)/shard_map/pallas_call | solution.py:259
  40.3 0.0 collective-permute-done.11.other
  40.3 0.7 %shard_map.115 = (f32[4,64,64]{2,1,0:T(8,128)}, f32[1,64]{1,0:T(1,128)}) custom-call(f32[136,128]{1,0:T(8,128)S(1)} %add.11.mine, f32[136,128]{1,0:T(8,128)S(1)} %collective-permute-done.11.other), custom_call_target="tpu_custom_call" | custom-call | flops 17408 | bytes 205056 | tf_op jit(solution)/shard_map/pallas_call | solution.py:259
  (6 shorter events, 0.0 us)
Async XLA Ops:
  0.6 17.6 %copy-start = (bf16[8,64,576]{2,1,0:T(8,128)(2,1)S(1)}, bf16[8,64,576]{2,1,0:T(8,128)(2,1)}, u32[]{:S(2)}) copy-start(bf16[8,64,576]{2,1,0:T(8,128)(2,1)} %lap.3) | copy-start | bytes 1769476
  0.6 17.6 %copy-start.1 = (bf16[8,64,128]{2,1,0:T(8,128)(2,1)S(1)}, bf16[8,64,128]{2,1,0:T(8,128)(2,1)}, u32[]{:S(2)}) copy-start(bf16[8,64,128]{2,1,0:T(8,128)(2,1)} %feat_ref.3) | copy-start | bytes 393220
  0.7 17.6 %copy-start.2 = (bf16[8,64,128]{2,1,0:T(8,128)(2,1)S(1)}, bf16[8,64,128]{2,1,0:T(8,128)(2,1)}, u32[]{:S(2)}) copy-start(bf16[8,64,128]{2,1,0:T(8,128)(2,1)} %cot_ref.3) | copy-start | bytes 393220
  3.2 10.7 %collective-permute-start = (bf16[272,256]{1,0:T(8,128)(2,1)S(1)}, bf16[272,256]{1,0:T(8,128)(2,1)S(1)}, u32[]{:S(2)}, u32[]{:S(2)}) collective-permute-start(bf16[272,256]{1,0:T(8,128)(2,1)S(1)} %get-tuple-element.35), channel_id=1, source_target_pairs={{14,0},{4,2},{2,4},{8,6},{6,8},{12,10},{10,12},{0,14},{15,1},{5,3}... | collective-permute-start | bytes 417800 | tf_op jit(solution)/shard_map/ppermute | solution.py:30
  9.3 8.4 %collective-permute-start.1 = (bf16[272,256]{1,0:T(8,128)(2,1)S(1)}, bf16[272,256]{1,0:T(8,128)(2,1)S(1)}, u32[]{:S(2)}, u32[]{:S(2)}) collective-permute-start(bf16[272,256]{1,0:T(8,128)(2,1)S(1)} %get-tuple-element.36), channel_id=1, source_target_pairs={{12,0},{14,2},{8,4},{10,6},{4,8},{6,10},{0,12},{2,14},{13,1},{15,3... | collective-permute-start | bytes 417800 | tf_op jit(solution)/shard_map/ppermute | solution.py:30
  9.7 7.9 %collective-permute-start.2 = (bf16[272,256]{1,0:T(8,128)(2,1)S(1)}, bf16[272,256]{1,0:T(8,128)(2,1)S(1)}, u32[]{:S(2)}, u32[]{:S(2)}) collective-permute-start(bf16[272,256]{1,0:T(8,128)(2,1)S(1)} %get-tuple-element.37), channel_id=1, source_target_pairs={{2,0},{0,2},{6,4},{4,6},{10,8},{8,10},{14,12},{12,14},{3,1},{1,3},... | collective-permute-start | bytes 417800 | tf_op jit(solution)/shard_map/ppermute | solution.py:30
  9.9 8.4 %collective-permute-start.3 = (bf16[272,256]{1,0:T(8,128)(2,1)S(1)}, bf16[272,256]{1,0:T(8,128)(2,1)S(1)}, u32[]{:S(2)}, u32[]{:S(2)}) collective-permute-start(bf16[272,256]{1,0:T(8,128)(2,1)S(1)} %get-tuple-element.38), channel_id=1, source_target_pairs={{4,0},{6,2},{0,4},{2,6},{12,8},{14,10},{8,12},{10,14},{5,1},{7,3},... | collective-permute-start | bytes 417800 | tf_op jit(solution)/shard_map/ppermute | solution.py:30
  20.4 1.3 %collective-permute-start.8 = (f32[136,128]{1,0:T(8,128)S(1)}, f32[136,128]{1,0:T(8,128)S(1)}, u32[]{:S(2)}, u32[]{:S(2)}) collective-permute-start(f32[136,128]{1,0:T(8,128)S(1)} %get-tuple-element.53), channel_id=1, source_target_pairs={{1,0},{0,1},{3,2},{2,3},{5,4},{4,5},{7,6},{6,7},{9,8},{8,9},{11,10... | collective-permute-start | bytes 208904 | tf_op jit(solution)/shard_map/ppermute | solution.py:325
  21.7 4.4 %collective-permute-start.9 = (f32[136,128]{1,0:T(8,128)S(1)}, f32[136,128]{1,0:T(8,128)S(1)}, u32[]{:S(2)}, u32[]{:S(2)}) collective-permute-start(f32[136,128]{1,0:T(8,128)S(1)} %add.9), channel_id=1, source_target_pairs={{2,0},{0,2},{6,4},{4,6},{10,8},{8,10},{14,12},{12,14},{3,1},{1,3},... | collective-permute-start | bytes 208904 | tf_op jit(solution)/shard_map/ppermute | solution.py:329
  26.1 7.9 %collective-permute-start.10 = (f32[136,128]{1,0:T(8,128)S(1)}, f32[136,128]{1,0:T(8,128)S(1)}, u32[]{:S(2)}, u32[]{:S(2)}) collective-permute-start(f32[136,128]{1,0:T(8,128)S(1)} %add.10), channel_id=1, source_target_pairs={{4,0},{6,2},{0,4},{2,6},{12,8},{14,10},{8,12},{10,14},{5,1},{7,3},... | collective-permute-start | bytes 208904 | tf_op jit(solution)/shard_map/ppermute | solution.py:329
  28.6 7.4 %collective-permute-start.4 = (bf16[128,256]{1,0:T(8,128)(2,1)S(1)}, bf16[128,256]{1,0:T(8,128)(2,1)S(1)}, u32[]{:S(2)}, u32[]{:S(2)}) collective-permute-start(bf16[128,256]{1,0:T(8,128)(2,1)S(1)} %get-tuple-element.47), channel_id=1, source_target_pairs={{14,0},{4,2},{2,4},{8,6},{6,8},{12,10},{10,12},{0,14},{15,1},{5,3}... | collective-permute-start | bytes 196616 | tf_op jit(solution)/shard_map/ppermute | solution.py:30
  30.2 6.5 %collective-permute-start.5 = (bf16[128,256]{1,0:T(8,128)(2,1)S(1)}, bf16[128,256]{1,0:T(8,128)(2,1)S(1)}, u32[]{:S(2)}, u32[]{:S(2)}) collective-permute-start(bf16[128,256]{1,0:T(8,128)(2,1)S(1)} %get-tuple-element.48), channel_id=1, source_target_pairs={{12,0},{14,2},{8,4},{10,6},{4,8},{6,10},{0,12},{2,14},{13,1},{15,3... | collective-permute-start | bytes 196616 | tf_op jit(solution)/shard_map/ppermute | solution.py:30
  32.1 4.5 %collective-permute-start.6 = (bf16[128,256]{1,0:T(8,128)(2,1)S(1)}, bf16[128,256]{1,0:T(8,128)(2,1)S(1)}, u32[]{:S(2)}, u32[]{:S(2)}) collective-permute-start(bf16[128,256]{1,0:T(8,128)(2,1)S(1)} %get-tuple-element.49), channel_id=1, source_target_pairs={{2,0},{0,2},{6,4},{4,6},{10,8},{8,10},{14,12},{12,14},{3,1},{1,3},... | collective-permute-start | bytes 196616 | tf_op jit(solution)/shard_map/ppermute | solution.py:30
  33.9 4.4 %collective-permute-start.7 = (bf16[128,256]{1,0:T(8,128)(2,1)S(1)}, bf16[128,256]{1,0:T(8,128)(2,1)S(1)}, u32[]{:S(2)}, u32[]{:S(2)}) collective-permute-start(bf16[128,256]{1,0:T(8,128)(2,1)S(1)} %get-tuple-element.50), channel_id=1, source_target_pairs={{4,0},{6,2},{0,4},{2,6},{12,8},{14,10},{8,12},{10,14},{5,1},{7,3},... | collective-permute-start | bytes 196616 | tf_op jit(solution)/shard_map/ppermute | solution.py:30
  33.9 6.3 %collective-permute-start.11 = (f32[136,128]{1,0:T(8,128)S(1)}, f32[136,128]{1,0:T(8,128)S(1)}, u32[]{:S(2)}, u32[]{:S(2)}) collective-permute-start(f32[136,128]{1,0:T(8,128)S(1)} %add.11.mine), channel_id=1, source_target_pairs={{8,0},{10,2},{12,4},{14,6},{0,8},{2,10},{4,12},{6,14},{9,1},{11,3}... | collective-permute-start | bytes 208904 | tf_op jit(solution)/shard_map/ppermute | solution.py:329

commit v3 on v2

--- a/solution.py
+++ b/solution.py
@@ -9,7 +9,10 @@
 from jax.sharding import PartitionSpec as P
 
 CYCLE_STEPS = (0, -1, 1, -2, 2, -3, 3)
-ORDER = (1, 3, 0, 2)
+ORDER = (3, 1, 2, 0)
+ORDER_TWO = (0, 1, 3, 2)
+TIES = {}
+STEPS = (0, 2, 4)
 F32 = jnp.float32
 BF16 = jnp.bfloat16
 
@@ -62,11 +65,11 @@
 
 
 def pack_kernel(
-    rows_hbm, lists_hbm, mask_hbm, feat_hbm, cot_hbm, lap_hbm, weight_hbm, bias_hbm,
+    rows_hbm, lists_hbm, mask_hbm, feat_hbm, cot_hbm, lap_hbm,
     *refs,
 ):
-    sends, (value, keep, part, rows_ref, lists_ref, mix, mix_last, bias_row) = refs[:4], refs[4:12]
-    mask, lap, weight, bias, sem = refs[12:]
+    sends, (value, keep, part, rows_ref, lists_ref) = refs[:4], refs[4:9]
+    mask, lap, sem = refs[9:]
     blocks, pixels, lanes = feat_hbm.shape
     slots = lists_hbm.shape[1]
     cycle = len(CYCLE_STEPS) * pixels
@@ -78,8 +81,6 @@
         pltpu.make_async_copy(lap_hbm, lap, sem.at[3]),
         pltpu.make_async_copy(rows_hbm, rows_ref, sem.at[4]),
         pltpu.make_async_copy(lists_hbm, lists_ref, sem.at[5]),
-        pltpu.make_async_copy(weight_hbm, weight, sem.at[6]),
-        pltpu.make_async_copy(bias_hbm, bias, sem.at[7]),
     ]
     for copy in copies:
         copy.start()
@@ -116,18 +117,6 @@
             flags = jnp.where(which == s, mask[pl.ds(b, 1), :].astype(F32), flags)
         send[tail:, :] = jnp.zeros((16, 2 * lanes), BF16)
         send[tail:, :pixels] = flags.astype(BF16)
-    copies[6].wait()
-    copies[7].wait()
-    terms, half, _ = weight.shape
-    mix[...] = jnp.zeros_like(mix)
-    mix_last[...] = jnp.zeros_like(mix_last)
-    for m in range(lanes // half):
-        spot = slice(m * half, (m + 1) * half)
-        for k in range(terms - 1):
-            shifted = slice(k * lanes + m * half, k * lanes + (m + 1) * half)
-            mix[spot, shifted] = weight[k]
-        mix_last[spot, spot] = weight[terms - 1]
-        bias_row[:, spot] = bias[...]
 
 
 def middle_kernel(
@@ -163,7 +152,7 @@
         fresh = (2.0 * total - base).astype(BF16)
         two[a] = fresh
         spread[a] = fresh * keep[a]
-    for pairing, send in zip(ORDER, sends):
+    for pairing, send in zip(ORDER_TWO, sends):
         heading = send_heading(pairing, device)
         for s in range(slots):
             send[s * pixels:(s + 1) * pixels, :] = spread[lists_ref[0, s, heading]]
@@ -184,17 +173,47 @@
 
     sum_zero = trace(low, 0)
     sum_one = trace(low, lanes)
-    sums[:half, :half] = sum_zero
-    sums[:half, half:] = sum_one
-    sums[half:lanes, :half] = 2.0 * trace(high, 0) - sum_zero
-    sums[half:lanes, half:] = 2.0 * trace(high, lanes) - sum_one
-    sums[lanes:, :] = jnp.broadcast_to(
-        jnp.sum(cot.astype(F32), axis=0, keepdims=True), (8, lanes)
-    )
-
-
-def partial_kernel(feat_ref, cot_ref, mix, bias_row, one, two, out_part, grad_part):
+    totals = jnp.concatenate(
+        [
+            jnp.concatenate([sum_zero, sum_one], axis=1),
+            jnp.concatenate(
+                [2.0 * trace(high, 0) - sum_zero, 2.0 * trace(high, lanes) - sum_one], axis=1
+            ),
+            jnp.broadcast_to(jnp.sum(cot.astype(F32), axis=0, keepdims=True), (16, lanes)),
+        ],
+        axis=0,
+    )
+    coarse = totals.astype(BF16)
+    fine = (totals - coarse.astype(F32)).astype(BF16)
+    send = sends[ORDER_TWO.index(0)]
+    send[slots * pixels:, :lanes] = coarse
+    send[slots * pixels:, lanes:] = fine
+    sums[...] = coarse.astype(F32) + fine.astype(F32)
+
+
+def partial_kernel(
+    feat_ref, cot_ref, one, two, weight_hbm, bias_hbm, out_part, grad_part, mix_last,
+    mix, bias_row, weight, bias, sem,
+):
     blocks, pixels, lanes = feat_ref.shape
+    copies = [
+        pltpu.make_async_copy(weight_hbm, weight, sem.at[0]),
+        pltpu.make_async_copy(bias_hbm, bias, sem.at[1]),
+    ]
+    for copy in copies:
+        copy.start()
+    for copy in copies:
+        copy.wait()
+    terms, half, _ = weight.shape
+    mix[...] = jnp.zeros_like(mix)
+    mix_last[...] = jnp.zeros_like(mix_last)
+    for m in range(lanes // half):
+        spot = slice(m * half, (m + 1) * half)
+        for k in range(terms - 1):
+            shifted = slice(k * lanes + m * half, k * lanes + (m + 1) * half)
+            mix[spot, shifted] = weight[k]
+        mix_last[spot, spot] = weight[terms - 1]
+        bias_row[:, spot] = bias[...]
     flat = blocks * pixels
     first = one[...].reshape(flat, 2 * lanes)
     second = two[...].reshape(flat, 2 * lanes)
@@ -214,8 +233,8 @@
     gots, (out_ref, grad_ref), (halo, three) = refs[:4], refs[4:6], refs[6:]
     blocks, pixels, lanes = out_part.shape
     device = lax.axis_index("pix")
-    slots = gots[0].shape[0] // pixels
-    for pairing, got in zip(ORDER, gots):
+    slots = 2 * blocks // len(gots) // 2
+    for pairing, got in zip(ORDER_TWO, gots):
         heading = send_heading(pairing, device) ^ 1
         for s in range(slots):
             row = row_of_slot(rows_ref, heading * slots + s)
@@ -243,16 +262,18 @@
     bias_ref[...] = bias[:, :half] + bias[:, half:]
 
 
-def call(kernel, outs, ins, scratch, flops, in_hbm=False):
+def call(kernel, outs, ins, scratch, flops, hbm_from=None):
     vmem = pl.BlockSpec(memory_space=pltpu.VMEM)
     smem = pl.BlockSpec(memory_space=pltpu.SMEM)
     hbm = pl.BlockSpec(memory_space=pltpu.MemorySpace.HBM)
     touched = sum(math.prod(x.shape) * x.dtype.itemsize for x in [*ins, *outs])
-    if in_hbm:
-        ins = [pltpu.with_memory_space_constraint(x, pltpu.MemorySpace.HBM) for x in ins]
+    hbm_from = len(ins) if hbm_from is None else hbm_from
+    ins = ins[:hbm_from] + [
+        pltpu.with_memory_space_constraint(x, pltpu.MemorySpace.HBM) for x in ins[hbm_from:]
+    ]
 
     def place(i, x):
-        if in_hbm:
+        if i >= hbm_from:
             return hbm
         return smem if i < 2 and x.dtype == jnp.int32 else vmem
 
@@ -282,52 +303,66 @@
     field = shape((blocks, pixels, width), BF16)
     wide = shape((blocks, pixels, width), F32)
     scratch_field = pltpu.VMEM((blocks, pixels, width), BF16)
-    *sends, value, keep, part, rows, lists, mix, mix_last, bias_row = call(
+    *sends, value, keep, part, rows, lists = call(
         pack_kernel,
         [shape((slots * 2 * pixels + 16, width), BF16)] * 4 + [field, field, wide]
-        + [shape(rows.shape, jnp.int32), shape(lists.shape, jnp.int32)]
-        + [shape((lanes, (terms - 1) * lanes), BF16), shape((lanes, lanes), BF16)]
-        + [shape((1, lanes), F32)],
-        [rows, lists, pixel_mask, features, cotangent, lap_tiles, cheb_weights]
-        + [out_bias.reshape(1, chan_out)],
+        + [shape(rows.shape, jnp.int32), shape(lists.shape, jnp.int32)],
+        [rows, lists, pixel_mask, features, cotangent, lap_tiles],
         [
             pltpu.VMEM((blocks, pixels), jnp.int32),
             pltpu.VMEM(lap_tiles.shape, BF16),
-            pltpu.VMEM(cheb_weights.shape, BF16),
-            pltpu.VMEM((1, chan_out), F32),
-            pltpu.SemaphoreType.DMA((8,)),
+            pltpu.SemaphoreType.DMA((6,)),
         ],
         apply_flops,
-        in_hbm=True,
+        hbm_from=0,
     )
     gots = [exchange(send, k) for k, send in zip(ORDER, sends)]
     one, two, spread, *sends, sums = call(
         middle_kernel,
         [field, field, field]
-        + [shape((slots * pixels, width), BF16)] * 4
-        + [shape((lanes + 8, lanes), F32)],
+        + [
+            shape((slots * pixels + (lanes + 16 if k == 0 else 0), width), BF16)
+            for k in ORDER_TWO
+        ]
+        + [shape((lanes + 16, lanes), F32)],
         [rows, lists, features, cotangent, lap_tiles, value, keep, part, *gots],
         [scratch_field, scratch_field, pltpu.VMEM((blocks, pixels), F32)],
         2 * apply_flops,
     )
-    gots = [exchange(send, k) for k, send in zip(ORDER, sends)]
+    gots = [exchange(send, k) for k, send in zip(ORDER_TWO, sends)]
     half_field = shape((blocks, pixels, lanes), F32)
-    parts = call(
+    *parts, mix_last = call(
         partial_kernel,
-        [half_field, half_field],
-        [features, cotangent, mix, bias_row, one, two],
-        [],
+        [half_field, half_field, shape((lanes, lanes), BF16)],
+        [features, cotangent, one, two, cheb_weights, out_bias.reshape(1, chan_out)],
+        [
+            pltpu.VMEM((lanes, (terms - 1) * lanes), BF16),
+            pltpu.VMEM((1, lanes), F32),
+            pltpu.VMEM(cheb_weights.shape, BF16),
+            pltpu.VMEM((1, chan_out), F32),
+            pltpu.SemaphoreType.DMA((2,)),
+        ],
         4 * flat * lanes * lanes * (terms - 1),
+        hbm_from=4,
     )
     count = lax.axis_size("pix")
     pair = lax.axis_size("dp")
     factor = 1.0 / math.sqrt(flat * (lanes // chan_in) * count * pair)
-    other = lax.ppermute(sums, "dp", [(i ^ 1, i) for i in range(pair)])
-    reach = 1
-    while reach < count:
+    def swap(block, step):
+        if step == 0:
+            return lax.ppermute(block, "dp", [(i ^ 1, i) for i in range(pair)])
+        return lax.ppermute(block, "pix", [(i ^ step, i) for i in range(count)])
+
+    tail = gots[ORDER_TWO.index(0)][slots * pixels:].astype(F32)
+    other = tail[:, :lanes] + tail[:, lanes:]
+    for step in STEPS:
         sums = sums + other
-        other = lax.ppermute(sums, "pix", [(i ^ reach, i) for i in range(count)])
-        reach *= 2
+        if step in TIES:
+            spots = [ORDER_TWO.index(k) for k in TIES[step]]
+            sums, *held = lax.optimization_barrier((sums, *[gots[i] for i in spots]))
+            for i, block in zip(spots, held):
+                gots[i] = block
+        other = swap(sums, step)
     output_maps, grad_features = call(
         last_kernel,
         [shape(features.shape, BF16), shape(features.shape, BF16)],

time: 41.2 us -> 40.2 us (0.976)
  starting transfers between devices: 17.7 us -> 15.7 us
  Pallas kernels: 7.71 us -> 8.26 us
  waiting for transfers between devices: 14.8 us -> 15.3 us
    ppermute x8, waiting for transfers between devices: 10.6 us -> 13.1 us  [exchange(): return lax.ppermute(block, 'pix', route)]
    ppermute x4 -> x3, waiting for transfers between devices: 4.23 us -> 2.24 us  [the longest x1 1.25 us: swap(): return lax.ppermute(block, 'dp', [(i ^ 1, i) for i in range(pair)])]
    ppermute x4 -> x3, starting transfers between devices: 4.74 us -> 2.98 us  [the longest x2 2.91 us: swap(): return lax.ppermute(block, 'pix', [(i ^ step, i) for i in range(count)])]
    pallas_call x5, Pallas kernels: 7.71 us -> 8.26 us  [call(): pl.pallas_call(kernel, out_shape=outs, in_specs=[place(i, x) for i, x in...]
  transfers between devices with their start and end apart: 12 -> 11, of which waited for: 8 -> 10; matrix products, arithmetic and copies ran while one was open for 0% -> 0% of each run, Pallas kernels for 6% -> 8%
where the time goes in v3:
time: 40.2 us; the launch traced here: 40.1 us
  starting transfers between devices  15.7 us (39%)
  waiting for transfers between devices  15.3 us (38%)
  Pallas kernels  8.26 us (21%)
  between operations  0.72 us (2%)
    ppermute x8, waiting for transfers between devices, exchange(): return lax.ppermute(block, 'pix', route)  13.1 us
    ppermute x8, starting transfers between devices, exchange(): return lax.ppermute(block, 'pix', route)  12.7 us
    pallas_call x5, Pallas kernels, call(): pl.pallas_call(kernel, out_shape=outs, in_specs=[place(i, x) for i, x in...  8.26 us
    ppermute x2, starting transfers between devices, swap(): return lax.ppermute(block, 'pix', [(i ^ step, i) for i in range(count)])  2.91 us
    ppermute x1, waiting for transfers between devices, swap(): return lax.ppermute(block, 'dp', [(i ^ 1, i) for i in range(pair)])  1.25 us
    ppermute x2, waiting for transfers between devices, swap(): return lax.ppermute(block, 'pix', [(i ^ step, i) for i in range(count)])  0.98 us
  transfers between devices with their start and end apart: 11, of which 10 were waited for; matrix products, arithmetic and copies ran while one was open for 0% of the time, Pallas kernels for 8%

profile of v3, /device:TPU:0, one launch (start us, length us, event | category | flops | bytes accessed | tf_op | source)
XLA Modules:
  0.0 40.1 jit_solution(11155614758893416368)
XLA Ops:
  0.6 0.0 copy-start
  0.6 0.0 copy-start.1
  0.7 0.0 copy-start.2
  0.7 2.2 %shard_map.111 = (bf16[272,256]{1,0:T(8,128)(2,1)S(1)}, bf16[272,256]{1,0:T(8,128)(2,1)S(1)}, bf16[272,256]{1,0:T(8,128)(2,1)S(1)}, bf16[272,256]{1,0:T(8,128)(2...) custom-call(s32[2,8]{1,0:T(2,128)} %bitcast.4, ...), custom_call_target="tpu_custom_call" | custom-call | flops 150994944 | bytes 2459840 | tf_op jit(solution)/shard_map/pallas_call | solution.py:280
  2.8 5.1 %collective-permute-start = (bf16[272,256]{1,0:T(8,128)(2,1)S(1)}, bf16[272,256]{1,0:T(8,128)(2,1)S(1)}, u32[]{:S(2)}, u32[]{:S(2)}) collective-permute-start(bf16[272,256]{1,0:T(8,128)(2,1)S(1)} %get-tuple-element.33), channel_id=1, source_target_pairs={{12,0},{14,2},{8,4},{10,6},{4,8},{6,10},{0,12},{2,14},{13,1},{15,3... | collective-permute-start | bytes 417800 | tf_op jit(solution)/shard_map/ppermute | solution.py:33
  8.0 1.1 %collective-permute-start.1 = (bf16[272,256]{1,0:T(8,128)(2,1)S(1)}, bf16[272,256]{1,0:T(8,128)(2,1)S(1)}, u32[]{:S(2)}, u32[]{:S(2)}) collective-permute-start(bf16[272,256]{1,0:T(8,128)(2,1)S(1)} %get-tuple-element.34), channel_id=1, source_target_pairs={{14,0},{4,2},{2,4},{8,6},{6,8},{12,10},{10,12},{0,14},{15,1},{5,3}... | collective-permute-start | bytes 417800 | tf_op jit(solution)/shard_map/ppermute | solution.py:33
  9.1 1.8 %collective-permute-start.2 = (bf16[272,256]{1,0:T(8,128)(2,1)S(1)}, bf16[272,256]{1,0:T(8,128)(2,1)S(1)}, u32[]{:S(2)}, u32[]{:S(2)}) collective-permute-start(bf16[272,256]{1,0:T(8,128)(2,1)S(1)} %get-tuple-element.35), channel_id=1, source_target_pairs={{4,0},{6,2},{0,4},{2,6},{12,8},{14,10},{8,12},{10,14},{5,1},{7,3},... | collective-permute-start | bytes 417800 | tf_op jit(solution)/shard_map/ppermute | solution.py:33
  10.9 0.0 collective-permute-start.3
  10.9 1.6 %collective-permute-done.refs_0_ = bf16[272,256]{1,0:T(8,128)(2,1)S(1)} collective-permute-done((bf16[272,256]{1,0:T(8,128)(2,1)S(1)}, bf16[272,256]{1,0:T(8,128)(2,1)S(1)}, u32[]{:S(2)}, u32[]{:S(2)}) %collective-permute-start) | collective-permute-done | bytes 139296 | tf_op jit(solution)/shard_map/ppermute | solution.py:33
  12.5 4.8 %collective-permute-done.1.refs_1_ = bf16[272,256]{1,0:T(8,128)(2,1)S(1)} collective-permute-done((bf16[272,256]{1,0:T(8,128)(2,1)S(1)}, bf16[272,256]{1,0:T(8,128)(2,1)S(1)}, u32[]{:S(2)}, u32[]{:S(2)}) %collective-permute-start.1) | collective-permute-done | bytes 139296 | tf_op jit(solution)/shard_map/ppermute | solution.py:33
  17.3 0.5 %collective-permute-done.2.refs_2_ = bf16[272,256]{1,0:T(8,128)(2,1)S(1)} collective-permute-done((bf16[272,256]{1,0:T(8,128)(2,1)S(1)}, bf16[272,256]{1,0:T(8,128)(2,1)S(1)}, u32[]{:S(2)}, u32[]{:S(2)}) %collective-permute-start.2) | collective-permute-done | bytes 139296 | tf_op jit(solution)/shard_map/ppermute | solution.py:33
  17.8 0.7 %collective-permute-done.3.refs_3_ = bf16[272,256]{1,0:T(8,128)(2,1)S(1)} collective-permute-done((bf16[272,256]{1,0:T(8,128)(2,1)S(1)}, bf16[272,256]{1,0:T(8,128)(2,1)S(1)}, u32[]{:S(2)}, u32[]{:S(2)}) %collective-permute-start.3) | collective-permute-done | bytes 139296 | tf_op jit(solution)/shard_map/ppermute | solution.py:33
  18.5 0.0 copy-done
  18.5 0.0 copy-done.2
  18.5 2.1 %shard_map.112 = (bf16[8,64,256]{2,1,0:T(8,128)(2,1)S(1)}, bf16[8,64,256]{2,1,0:T(8,128)(2,1)S(1)}, bf16[8,64,256]{2,1,0:T(8,128)(2,1)S(1)}, bf16[272,256]{1,0:T...) custom-call(s32[2,8]{1,0:T(2,128)S(1)} %get-tuple-element.28.rows_re, ...), custom_call_target="tpu_custom_call" | custom-call | flops 301989888 | bytes 3653728 | tf_op jit(solution)/shard_map/pallas_call | solution.py:280
  20.6 0.8 %collective-permute-start.4 = (bf16[272,256]{1,0:T(8,128)(2,1)S(1)}, bf16[272,256]{1,0:T(8,128)(2,1)S(1)}, u32[]{:S(2)}, u32[]{:S(2)}) collective-permute-start(bf16[272,256]{1,0:T(8,128)(2,1)S(1)} %get-tuple-element.43), channel_id=1, source_target_pairs={{2,0},{0,2},{6,4},{4,6},{10,8},{8,10},{14,12},{12,14},{3,1},{1,3},... | collective-permute-start | bytes 417800 | tf_op jit(solution)/shard_map/ppermute | solution.py:33
  21.4 4.4 %collective-permute-done.4.refs_0_ = bf16[272,256]{1,0:T(8,128)(2,1)S(1)} collective-permute-done((bf16[272,256]{1,0:T(8,128)(2,1)S(1)}, bf16[272,256]{1,0:T(8,128)(2,1)S(1)}, u32[]{:S(2)}, u32[]{:S(2)}) %collective-permute-start.4) | collective-permute-done | bytes 139296 | tf_op jit(solution)/shard_map/ppermute | solution.py:33
  25.8 0.1 collective-permute-start.8
  25.9 1.3 %collective-permute-done.8 = f32[144,128]{1,0:T(8,128)S(1)} collective-permute-done((f32[144,128]{1,0:T(8,128)S(1)}, f32[144,128]{1,0:T(8,128)S(1)}, u32[]{:S(2)}, u32[]{:S(2)}) %collective-permute-start.8) | collective-permute-done | bytes 73760 | tf_op jit(solution)/shard_map/ppermute | solution.py:353
  27.2 0.9 %collective-permute-start.9 = (f32[144,128]{1,0:T(8,128)S(1)}, f32[144,128]{1,0:T(8,128)S(1)}, u32[]{:S(2)}, u32[]{:S(2)}) collective-permute-start(f32[144,128]{1,0:T(8,128)S(1)} %add.14), channel_id=1, source_target_pairs={{4,0},{6,2},{0,4},{2,6},{12,8},{14,10},{8,12},{10,14},{5,1},{7,3},... | collective-permute-start | bytes 221192 | tf_op jit(solution)/shard_map/ppermute | solution.py:354
  28.1 1.4 %collective-permute-start.5 = (bf16[128,256]{1,0:T(8,128)(2,1)S(1)}, bf16[128,256]{1,0:T(8,128)(2,1)S(1)}, u32[]{:S(2)}, u32[]{:S(2)}) collective-permute-start(bf16[128,256]{1,0:T(8,128)(2,1)S(1)} %get-tuple-element.44), channel_id=1, source_target_pairs={{14,0},{4,2},{2,4},{8,6},{6,8},{12,10},{10,12},{0,14},{15,1},{5,3}... | collective-permute-start | bytes 196616 | tf_op jit(solution)/shard_map/ppermute | solution.py:33
  29.5 1.7 %collective-permute-start.6 = (bf16[128,256]{1,0:T(8,128)(2,1)S(1)}, bf16[128,256]{1,0:T(8,128)(2,1)S(1)}, u32[]{:S(2)}, u32[]{:S(2)}) collective-permute-start(bf16[128,256]{1,0:T(8,128)(2,1)S(1)} %get-tuple-element.45), channel_id=1, source_target_pairs={{12,0},{14,2},{8,4},{10,6},{4,8},{6,10},{0,12},{2,14},{13,1},{15,3... | collective-permute-start | bytes 196616 | tf_op jit(solution)/shard_map/ppermute | solution.py:33
  31.2 0.7 %collective-permute-start.7 = (bf16[128,256]{1,0:T(8,128)(2,1)S(1)}, bf16[128,256]{1,0:T(8,128)(2,1)S(1)}, u32[]{:S(2)}, u32[]{:S(2)}) collective-permute-start(bf16[128,256]{1,0:T(8,128)(2,1)S(1)} %get-tuple-element.46), channel_id=1, source_target_pairs={{4,0},{6,2},{0,4},{2,6},{12,8},{14,10},{8,12},{10,14},{5,1},{7,3},... | collective-permute-start | bytes 196616 | tf_op jit(solution)/shard_map/ppermute | solution.py:33
  31.9 0.0 collective-permute-done.9
  31.9 2.0 %collective-permute-start.10 = (f32[144,128]{1,0:T(8,128)S(1)}, f32[144,128]{1,0:T(8,128)S(1)}, u32[]{:S(2)}, u32[]{:S(2)}) collective-permute-start(f32[144,128]{1,0:T(8,128)S(1)} %add.15.mine), channel_id=1, source_target_pairs={{8,0},{10,2},{12,4},{14,6},{0,8},{2,10},{4,12},{6,14},{9,1},{11,3}... | collective-permute-start | bytes 221192 | tf_op jit(solution)/shard_map/ppermute | solution.py:354
  33.9 1.3 %shard_map.113 = (f32[8,64,128]{2,1,0:T(8,128)S(1)}, f32[8,64,128]{2,1,0:T(8,128)S(1)}, bf16[128,128]{1,0:T(8,128)(2,1)S(1)}) custom-call(bf16[8,64,128]{2,1,0:T(8,128)(2,1)S(1)} %copy-done.1, bf16[8,64,128]{2,1,0:T(8,128)(2,1)S(1)} %copy-done.2, bf16[8,64,256]{2,1,0:T(8,128)(2,1)S(1)} %get-tuple-element.37.one, ...), custom_call_target="tpu_custom_call" | custom-call | flops 100663296 | bytes 1376512 | tf_op jit(solution)/shard_map/pallas_call | solution.py:280
  35.2 0.5 %collective-permute-done.5.refs_1_ = bf16[128,256]{1,0:T(8,128)(2,1)S(1)} collective-permute-done((bf16[128,256]{1,0:T(8,128)(2,1)S(1)}, bf16[128,256]{1,0:T(8,128)(2,1)S(1)}, u32[]{:S(2)}, u32[]{:S(2)}) %collective-permute-start.5) | collective-permute-done | bytes 65568 | tf_op jit(solution)/shard_map/ppermute | solution.py:33
  35.7 0.5 %collective-permute-done.6.refs_2_ = bf16[128,256]{1,0:T(8,128)(2,1)S(1)} collective-permute-done((bf16[128,256]{1,0:T(8,128)(2,1)S(1)}, bf16[128,256]{1,0:T(8,128)(2,1)S(1)}, u32[]{:S(2)}, u32[]{:S(2)}) %collective-permute-start.6) | collective-permute-done | bytes 65568 | tf_op jit(solution)/shard_map/ppermute | solution.py:33
  36.2 0.2 collective-permute-done.7.refs_3_
  36.3 2.0 %shard_map.114 = (bf16[8,64,128]{2,1,0:T(8,128)(2,1)}, bf16[8,64,128]{2,1,0:T(8,128)(2,1)}) custom-call(s32[2,8]{1,0:T(2,128)S(1)} %get-tuple-element.28.rows_ref, bf16[8,64,576]{2,1,0:T(8,128)(2,1)S(1)} %copy-done, bf16[8,64,256]{2,1,0:T(8,128)(2,1)S(1)} %get-tuple-element.29.keep, bf16[8,64,256]{2,1,0:T(8,128)(2,1)S(1)} %get-tuple-element.37.one, ...), custom_call_target="tpu_custom_call" | custom-call | flops 301989888 | bytes 2531392 | tf_op jit(solution)/shard_map/pallas_call | solution.py:280
  38.3 1.0 %collective-permute-done.10.other = f32[144,128]{1,0:T(8,128)S(1)} collective-permute-done((f32[144,128]{1,0:T(8,128)S(1)}, f32[144,128]{1,0:T(8,128)S(1)}, u32[]{:S(2)}, u32[]{:S(2)}) %collective-permute-start.10) | collective-permute-done | bytes 73760 | tf_op jit(solution)/shard_map/ppermute | solution.py:354
  39.3 0.7 %shard_map.115 = (f32[4,64,64]{2,1,0:T(8,128)}, f32[1,64]{1,0:T(1,128)}) custom-call(f32[144,128]{1,0:T(8,128)S(1)} %add.15.mine, f32[144,128]{1,0:T(8,128)S(1)} %collective-permute-done.10.other), custom_call_target="tpu_custom_call" | custom-call | flops 18432 | bytes 213248 | tf_op jit(solution)/shard_map/pallas_call | solution.py:280
  (5 shorter events, 0.1 us)
Async XLA Ops:
  0.6 17.8 %copy-start = (bf16[8,64,576]{2,1,0:T(8,128)(2,1)S(1)}, bf16[8,64,576]{2,1,0:T(8,128)(2,1)}, u32[]{:S(2)}) copy-start(bf16[8,64,576]{2,1,0:T(8,128)(2,1)} %lap.3) | copy-start | bytes 1769476
  0.6 17.8 %copy-start.1 = (bf16[8,64,128]{2,1,0:T(8,128)(2,1)S(1)}, bf16[8,64,128]{2,1,0:T(8,128)(2,1)}, u32[]{:S(2)}) copy-start(bf16[8,64,128]{2,1,0:T(8,128)(2,1)} %feat_ref.3) | copy-start | bytes 393220
  0.7 17.8 %copy-start.2 = (bf16[8,64,128]{2,1,0:T(8,128)(2,1)S(1)}, bf16[8,64,128]{2,1,0:T(8,128)(2,1)}, u32[]{:S(2)}) copy-start(bf16[8,64,128]{2,1,0:T(8,128)(2,1)} %cot_ref.3) | copy-start | bytes 393220
  2.8 9.7 %collective-permute-start = (bf16[272,256]{1,0:T(8,128)(2,1)S(1)}, bf16[272,256]{1,0:T(8,128)(2,1)S(1)}, u32[]{:S(2)}, u32[]{:S(2)}) collective-permute-start(bf16[272,256]{1,0:T(8,128)(2,1)S(1)} %get-tuple-element.33), channel_id=1, source_target_pairs={{12,0},{14,2},{8,4},{10,6},{4,8},{6,10},{0,12},{2,14},{13,1},{15,3... | collective-permute-start | bytes 417800 | tf_op jit(solution)/shard_map/ppermute | solution.py:33
  8.0 9.3 %collective-permute-start.1 = (bf16[272,256]{1,0:T(8,128)(2,1)S(1)}, bf16[272,256]{1,0:T(8,128)(2,1)S(1)}, u32[]{:S(2)}, u32[]{:S(2)}) collective-permute-start(bf16[272,256]{1,0:T(8,128)(2,1)S(1)} %get-tuple-element.34), channel_id=1, source_target_pairs={{14,0},{4,2},{2,4},{8,6},{6,8},{12,10},{10,12},{0,14},{15,1},{5,3}... | collective-permute-start | bytes 417800 | tf_op jit(solution)/shard_map/ppermute | solution.py:33
  9.1 8.7 %collective-permute-start.2 = (bf16[272,256]{1,0:T(8,128)(2,1)S(1)}, bf16[272,256]{1,0:T(8,128)(2,1)S(1)}, u32[]{:S(2)}, u32[]{:S(2)}) collective-permute-start(bf16[272,256]{1,0:T(8,128)(2,1)S(1)} %get-tuple-element.35), channel_id=1, source_target_pairs={{4,0},{6,2},{0,4},{2,6},{12,8},{14,10},{8,12},{10,14},{5,1},{7,3},... | collective-permute-start | bytes 417800 | tf_op jit(solution)/shard_map/ppermute | solution.py:33
  10.9 7.6 %collective-permute-start.3 = (bf16[272,256]{1,0:T(8,128)(2,1)S(1)}, bf16[272,256]{1,0:T(8,128)(2,1)S(1)}, u32[]{:S(2)}, u32[]{:S(2)}) collective-permute-start(bf16[272,256]{1,0:T(8,128)(2,1)S(1)} %get-tuple-element.36), channel_id=1, source_target_pairs={{2,0},{0,2},{6,4},{4,6},{10,8},{8,10},{14,12},{12,14},{3,1},{1,3},... | collective-permute-start | bytes 417800 | tf_op jit(solution)/shard_map/ppermute | solution.py:33
  20.6 5.2 %collective-permute-start.4 = (bf16[272,256]{1,0:T(8,128)(2,1)S(1)}, bf16[272,256]{1,0:T(8,128)(2,1)S(1)}, u32[]{:S(2)}, u32[]{:S(2)}) collective-permute-start(bf16[272,256]{1,0:T(8,128)(2,1)S(1)} %get-tuple-element.43), channel_id=1, source_target_pairs={{2,0},{0,2},{6,4},{4,6},{10,8},{8,10},{14,12},{12,14},{3,1},{1,3},... | collective-permute-start | bytes 417800 | tf_op jit(solution)/shard_map/ppermute | solution.py:33
  25.8 1.3 %collective-permute-start.8 = (f32[144,128]{1,0:T(8,128)S(1)}, f32[144,128]{1,0:T(8,128)S(1)}, u32[]{:S(2)}, u32[]{:S(2)}) collective-permute-start(f32[144,128]{1,0:T(8,128)S(1)} %fusion), channel_id=1, source_target_pairs={{1,0},{0,1},{3,2},{2,3},{5,4},{4,5},{7,6},{6,7},{9,8},{8,9},{11,10... | collective-permute-start | bytes 221192 | tf_op jit(solution)/shard_map/ppermute | solution.py:353
  27.2 4.7 %collective-permute-start.9 = (f32[144,128]{1,0:T(8,128)S(1)}, f32[144,128]{1,0:T(8,128)S(1)}, u32[]{:S(2)}, u32[]{:S(2)}) collective-permute-start(f32[144,128]{1,0:T(8,128)S(1)} %add.14), channel_id=1, source_target_pairs={{4,0},{6,2},{0,4},{2,6},{12,8},{14,10},{8,12},{10,14},{5,1},{7,3},... | collective-permute-start | bytes 221192 | tf_op jit(solution)/shard_map/ppermute | solution.py:354
  28.1 7.7 %collective-permute-start.5 = (bf16[128,256]{1,0:T(8,128)(2,1)S(1)}, bf16[128,256]{1,0:T(8,128)(2,1)S(1)}, u32[]{:S(2)}, u32[]{:S(2)}) collective-permute-start(bf16[128,256]{1,0:T(8,128)(2,1)S(1)} %get-tuple-element.44), channel_id=1, source_target_pairs={{14,0},{4,2},{2,4},{8,6},{6,8},{12,10},{10,12},{0,14},{15,1},{5,3}... | collective-permute-start | bytes 196616 | tf_op jit(solution)/shard_map/ppermute | solution.py:33
  29.5 6.7 %collective-permute-start.6 = (bf16[128,256]{1,0:T(8,128)(2,1)S(1)}, bf16[128,256]{1,0:T(8,128)(2,1)S(1)}, u32[]{:S(2)}, u32[]{:S(2)}) collective-permute-start(bf16[128,256]{1,0:T(8,128)(2,1)S(1)} %get-tuple-element.45), channel_id=1, source_target_pairs={{12,0},{14,2},{8,4},{10,6},{4,8},{6,10},{0,12},{2,14},{13,1},{15,3... | collective-permute-start | bytes 196616 | tf_op jit(solution)/shard_map/ppermute | solution.py:33
  31.2 5.1 %collective-permute-start.7 = (bf16[128,256]{1,0:T(8,128)(2,1)S(1)}, bf16[128,256]{1,0:T(8,128)(2,1)S(1)}, u32[]{:S(2)}, u32[]{:S(2)}) collective-permute-start(bf16[128,256]{1,0:T(8,128)(2,1)S(1)} %get-tuple-element.46), channel_id=1, source_target_pairs={{4,0},{6,2},{0,4},{2,6},{12,8},{14,10},{8,12},{10,14},{5,1},{7,3},... | collective-permute-start | bytes 196616 | tf_op jit(solution)/shard_map/ppermute | solution.py:33
  31.9 7.4 %collective-permute-start.10 = (f32[144,128]{1,0:T(8,128)S(1)}, f32[144,128]{1,0:T(8,128)S(1)}, u32[]{:S(2)}, u32[]{:S(2)}) collective-permute-start(f32[144,128]{1,0:T(8,128)S(1)} %add.15.mine), channel_id=1, source_target_pairs={{8,0},{10,2},{12,4},{14,6},{0,8},{2,10},{4,12},{6,14},{9,1},{11,3}... | collective-permute-start | bytes 221192 | tf_op jit(solution)/shard_map/ppermute | solution.py:354

commit v4 on v3

--- a/solution.py
+++ b/solution.py
@@ -10,9 +10,9 @@
 
 CYCLE_STEPS = (0, -1, 1, -2, 2, -3, 3)
 ORDER = (3, 1, 2, 0)
-ORDER_TWO = (0, 1, 3, 2)
-TIES = {}
-STEPS = (0, 2, 4)
+ORDER_TWO = (3, 1, 2, 0)
+SPLIT = 2
+OUTSIDE = 16
 F32 = jnp.float32
 BF16 = jnp.bfloat16
 
@@ -104,19 +104,13 @@
         total = matmul(lap[a, :, :cycle], jnp.concatenate(ring_rows(value, a), axis=0))
         total = total + matmul(lap[a, :, cycle + pixels:], value[rows_ref[1, a]])
         part[a] = total * keep[a].astype(F32)
-    tail = slots * 2 * pixels
-    which = lax.broadcasted_iota(jnp.int32, (16, pixels), 0)
     for pairing, send in zip(ORDER, sends):
         heading = send_heading(pairing, device)
-        flags = jnp.zeros((16, pixels), F32)
         for s in range(slots):
             b = lists_ref[0, s, heading]
             base = s * 2 * pixels
-            send[base:base + pixels, :] = value[b]
+            send[base:base + pixels, :] = value[b] + (1 - keep[b]) * OUTSIDE
             send[base + pixels:base + 2 * pixels, :] = part[b].astype(BF16)
-            flags = jnp.where(which == s, mask[pl.ds(b, 1), :].astype(F32), flags)
-        send[tail:, :] = jnp.zeros((16, 2 * lanes), BF16)
-        send[tail:, :pixels] = flags.astype(BF16)
 
 
 def middle_kernel(
@@ -129,21 +123,21 @@
     cycle = len(CYCLE_STEPS) * pixels
     flat, width = blocks * pixels, 2 * lanes
     device = lax.axis_index("pix")
-    tail = slots * 2 * pixels
     for pairing, got in zip(ORDER, gots):
         heading = send_heading(pairing, device) ^ 1
-        flags = got[tail:, :pixels].astype(F32)
         for s in range(slots):
             row = row_of_slot(rows_ref, heading * slots + s)
             base = s * 2 * pixels
-            halo[row] = got[base:base + pixels, :]
+            arrived = got[base:base + pixels, :].astype(F32)
+            outside = arrived > OUTSIDE / 2
+            halo[row] = jnp.where(outside, 0.0, arrived).astype(BF16)
+            keep_far[row] = jnp.where(outside, 0.0, 1.0).astype(BF16)
             halo_part[row] = got[base + pixels:base + 2 * pixels, :]
-            keep_far[pl.ds(row, 1), :] = flags[s:s + 1, :]
-    for a in range(blocks):
-        cross = lap[a, :, cycle:cycle + pixels] * keep_far[a:a + 1, :].astype(BF16)
+    for a in range(blocks):
+        cross = lap[a, :, cycle:cycle + pixels]
         total = part[a] + matmul(cross, halo[a]) * keep[a].astype(F32)
         one[a] = total.astype(BF16)
-        total = halo_part[a].astype(F32) + matmul_tn(cross, value[a])
+        total = halo_part[a].astype(F32) + matmul_tn(cross, value[a]) * keep_far[a].astype(F32)
         halo[a] = total.astype(BF16)
     for a in range(blocks):
         near = ring_rows(one, a) + [halo[a], one[rows_ref[1, a]]]
@@ -179,16 +173,11 @@
             jnp.concatenate(
                 [2.0 * trace(high, 0) - sum_zero, 2.0 * trace(high, lanes) - sum_one], axis=1
             ),
-            jnp.broadcast_to(jnp.sum(cot.astype(F32), axis=0, keepdims=True), (16, lanes)),
+            jnp.broadcast_to(jnp.sum(cot.astype(F32), axis=0, keepdims=True), (8, lanes)),
         ],
         axis=0,
     )
-    coarse = totals.astype(BF16)
-    fine = (totals - coarse.astype(F32)).astype(BF16)
-    send = sends[ORDER_TWO.index(0)]
-    send[slots * pixels:, :lanes] = coarse
-    send[slots * pixels:, lanes:] = fine
-    sums[...] = coarse.astype(F32) + fine.astype(F32)
+    sums[...] = totals
 
 
 def partial_kernel(
@@ -230,25 +219,36 @@
 def last_kernel(
     rows_ref, lap, keep, one, spread, out_part, grad_part, mix_last, *refs,
 ):
-    gots, (out_ref, grad_ref), (halo, three) = refs[:4], refs[4:6], refs[6:]
+    gots, (out_hbm, grad_hbm), (halo, three, out_ref, grad_ref, sem) = refs[:4], refs[4:6], refs[6:]
     blocks, pixels, lanes = out_part.shape
     device = lax.axis_index("pix")
-    slots = 2 * blocks // len(gots) // 2
+    slots = gots[0].shape[0] // pixels
     for pairing, got in zip(ORDER_TWO, gots):
         heading = send_heading(pairing, device) ^ 1
         for s in range(slots):
             row = row_of_slot(rows_ref, heading * slots + s)
             halo[row] = got[s * pixels:(s + 1) * pixels, :]
-    for a in range(blocks):
-        near = ring_rows(spread, a) + [halo[a], spread[rows_ref[1, a]]]
-        total = matmul(lap[a], jnp.concatenate(near, axis=0)) * keep[a].astype(F32)
-        three[a] = (2.0 * total - one[a].astype(F32)).astype(BF16)
-    flat = blocks * pixels
-    last = three[...].reshape(flat, 2 * lanes)
-    total = out_part[...].reshape(flat, lanes) + matmul(last[:, :lanes], mix_last[...])
-    out_ref[...] = total.astype(BF16).reshape(blocks, pixels, lanes)
-    total = grad_part[...].reshape(flat, lanes) + matmul_nt(last[:, lanes:], mix_last[...])
-    grad_ref[...] = total.astype(BF16).reshape(blocks, pixels, lanes)
+    group = blocks // SPLIT
+    size = group * pixels
+    copies = []
+    for start in range(0, blocks, group):
+        for a in range(start, start + group):
+            near = ring_rows(spread, a) + [halo[a], spread[rows_ref[1, a]]]
+            total = matmul(lap[a], jnp.concatenate(near, axis=0)) * keep[a].astype(F32)
+            three[a] = (2.0 * total - one[a].astype(F32)).astype(BF16)
+        mine = pl.ds(start, group)
+        last = three[mine].reshape(size, 2 * lanes)
+        total = out_part[mine].reshape(size, lanes) + matmul(last[:, :lanes], mix_last[...])
+        out_ref[mine] = total.astype(BF16).reshape(group, pixels, lanes)
+        total = grad_part[mine].reshape(size, lanes) + matmul_nt(last[:, lanes:], mix_last[...])
+        grad_ref[mine] = total.astype(BF16).reshape(group, pixels, lanes)
+        for source, target in ((out_ref, out_hbm), (grad_ref, grad_hbm)):
+            copies.append(
+                pltpu.make_async_copy(source.at[mine], target.at[mine], sem.at[len(copies)])
+            )
+            copies[-1].start()
+    for copy in copies:
+        copy.wait()
 
 
 def finish_kernel(factor, mine, other, weight_ref, bias_ref):
@@ -262,7 +262,7 @@
     bias_ref[...] = bias[:, :half] + bias[:, half:]
 
 
-def call(kernel, outs, ins, scratch, flops, hbm_from=None):
+def call(kernel, outs, ins, scratch, flops, hbm_from=None, out_hbm=False):
     vmem = pl.BlockSpec(memory_space=pltpu.VMEM)
     smem = pl.BlockSpec(memory_space=pltpu.SMEM)
     hbm = pl.BlockSpec(memory_space=pltpu.MemorySpace.HBM)
@@ -281,7 +281,7 @@
         kernel,
         out_shape=outs,
         in_specs=[place(i, x) for i, x in enumerate(ins)],
-        out_specs=[smem if x.dtype == jnp.int32 else vmem for x in outs],
+        out_specs=[hbm if out_hbm else smem if x.dtype == jnp.int32 else vmem for x in outs],
         scratch_shapes=scratch,
         cost_estimate=pl.CostEstimate(flops=flops, transcendentals=0, bytes_accessed=touched),
         compiler_params=pltpu.CompilerParams(vmem_limit_bytes=32 << 20),
@@ -305,7 +305,7 @@
     scratch_field = pltpu.VMEM((blocks, pixels, width), BF16)
     *sends, value, keep, part, rows, lists = call(
         pack_kernel,
-        [shape((slots * 2 * pixels + 16, width), BF16)] * 4 + [field, field, wide]
+        [shape((slots * 2 * pixels, width), BF16)] * 4 + [field, field, wide]
         + [shape(rows.shape, jnp.int32), shape(lists.shape, jnp.int32)],
         [rows, lists, pixel_mask, features, cotangent, lap_tiles],
         [
@@ -320,13 +320,10 @@
     one, two, spread, *sends, sums = call(
         middle_kernel,
         [field, field, field]
-        + [
-            shape((slots * pixels + (lanes + 16 if k == 0 else 0), width), BF16)
-            for k in ORDER_TWO
-        ]
-        + [shape((lanes + 16, lanes), F32)],
+        + [shape((slots * pixels, width), BF16)] * 4
+        + [shape((lanes + 8, lanes), F32)],
         [rows, lists, features, cotangent, lap_tiles, value, keep, part, *gots],
-        [scratch_field, scratch_field, pltpu.VMEM((blocks, pixels), F32)],
+        [scratch_field, scratch_field, scratch_field],
         2 * apply_flops,
     )
     gots = [exchange(send, k) for k, send in zip(ORDER_TWO, sends)]
@@ -348,27 +345,30 @@
     count = lax.axis_size("pix")
     pair = lax.axis_size("dp")
     factor = 1.0 / math.sqrt(flat * (lanes // chan_in) * count * pair)
-    def swap(block, step):
-        if step == 0:
-            return lax.ppermute(block, "dp", [(i ^ 1, i) for i in range(pair)])
-        return lax.ppermute(block, "pix", [(i ^ step, i) for i in range(count)])
-
-    tail = gots[ORDER_TWO.index(0)][slots * pixels:].astype(F32)
-    other = tail[:, :lanes] + tail[:, lanes:]
-    for step in STEPS:
+
+    def swap(block, reach):
+        return lax.ppermute(block, "pix", [(i ^ reach, i) for i in range(count)])
+
+    beside = lax.ppermute(sums, "dp", [(i ^ 1, i) for i in range(pair)])
+    across = lax.ppermute(
+        sums, ("pix", "dp"), [(i ^ (pair + 1), i) for i in range(count * pair)]
+    )
+    other = swap(sums, 1) + across
+    sums = sums + beside
+    reach = 2
+    while reach < count:
         sums = sums + other
-        if step in TIES:
-            spots = [ORDER_TWO.index(k) for k in TIES[step]]
-            sums, *held = lax.optimization_barrier((sums, *[gots[i] for i in spots]))
-            for i, block in zip(spots, held):
-                gots[i] = block
-        other = swap(sums, step)
+        other = swap(sums, reach)
+        reach *= 2
     output_maps, grad_features = call(
         last_kernel,
         [shape(features.shape, BF16), shape(features.shape, BF16)],
         [rows, lap_tiles, keep, one, spread, *parts, mix_last, *gots],
-        [scratch_field, scratch_field],
+        [scratch_field, scratch_field]
+        + [pltpu.VMEM(features.shape, BF16)] * 2
+        + [pltpu.SemaphoreType.DMA((2 * SPLIT,))],
         2 * apply_flops,
+        out_hbm=True,
     )
     grad_weights, grad_bias = call(
         functools.partial(finish_kernel, factor),

time: 40.2 us -> 38.8 us (0.965)
  waiting for transfers between devices: 15.3 us -> 11.5 us
  starting transfers between devices: 15.7 us -> 18 us
    ppermute x8, waiting for transfers between devices: 13.1 us -> 7.88 us  [exchange(): return lax.ppermute(block, 'pix', route)]
    ppermute x3 -> x5, starting transfers between devices: 2.98 us -> 5.72 us  [the longest x3 4.81 us: swap(): return lax.ppermute(block, 'pix', [(i ^ reach, i) for i in range(count)])]
    ppermute x3 -> x5, waiting for transfers between devices: 2.24 us -> 3.61 us  [the longest x1 2.62 us: local(): lax.ppermute(sums, ('pix', 'dp'), [(i ^ pair + 1, i) for i in range(count...]
  transfers between devices with their start and end apart: 11 -> 13, of which waited for: 10 -> 8; matrix products, arithmetic and copies ran while one was open for 0% -> 0% of each run, Pallas kernels for 8% -> 9%
where the time goes in v4:
time: 38.8 us; the launch traced here: 38.6 us
  starting transfers between devices  18 us (46%)
  waiting for transfers between devices  11.5 us (30%)
  Pallas kernels  8.32 us (21%)
  between operations  0.73 us (2%)
    ppermute x8, starting transfers between devices, exchange(): return lax.ppermute(block, 'pix', route)  12.3 us
    pallas_call x5, Pallas kernels, call(): pl.pallas_call(kernel, out_shape=outs, in_specs=[place(i, x) for i, x in...  8.32 us
    ppermute x8, waiting for transfers between devices, exchange(): return lax.ppermute(block, 'pix', route)  7.88 us
    ppermute x3, starting transfers between devices, swap(): return lax.ppermute(block, 'pix', [(i ^ reach, i) for i in range(count)])  4.81 us
    ppermute x1, waiting for transfers between devices, local(): lax.ppermute(sums, ('pix', 'dp'), [(i ^ pair + 1, i) for i in range(count...  2.62 us
    ppermute x3, waiting for transfers between devices, swap(): return lax.ppermute(block, 'pix', [(i ^ reach, i) for i in range(count)])  0.99 us
  transfers between devices with their start and end apart: 13, of which 8 were waited for; matrix products, arithmetic and copies ran while one was open for 0% of the time, Pallas kernels for 9%

profile of v4, /device:TPU:0, one launch (start us, length us, event | category | flops | bytes accessed | tf_op | source)
XLA Modules:
  0.0 38.6 jit_solution(4595533261652653419)
XLA Ops:
  0.7 2.3 %shard_map.111 = (bf16[256,256]{1,0:T(8,128)(2,1)S(1)}, bf16[256,256]{1,0:T(8,128)(2,1)S(1)}, bf16[256,256]{1,0:T(8,128)(2,1)S(1)}, bf16[256,256]{1,0:T(8,128)(2...) custom-call(s32[2,8]{1,0:T(2,128)} %bitcast.4, ...), custom_call_target="tpu_custom_call" | custom-call | flops 150994944 | bytes 2427072 | tf_op jit(solution)/shard_map/pallas_call | solution.py:280
  3.0 5.1 %collective-permute-start = (bf16[256,256]{1,0:T(8,128)(2,1)S(1)}, bf16[256,256]{1,0:T(8,128)(2,1)S(1)}, u32[]{:S(2)}, u32[]{:S(2)}) collective-permute-start(bf16[256,256]{1,0:T(8,128)(2,1)S(1)} %get-tuple-element.33), channel_id=1, source_target_pairs={{12,0},{14,2},{8,4},{10,6},{4,8},{6,10},{0,12},{2,14},{13,1},{15,3... | collective-permute-start | bytes 393224 | tf_op jit(solution)/shard_map/ppermute | solution.py:33
  8.1 1.2 %collective-permute-start.1 = (bf16[256,256]{1,0:T(8,128)(2,1)S(1)}, bf16[256,256]{1,0:T(8,128)(2,1)S(1)}, u32[]{:S(2)}, u32[]{:S(2)}) collective-permute-start(bf16[256,256]{1,0:T(8,128)(2,1)S(1)} %get-tuple-element.34), channel_id=1, source_target_pairs={{14,0},{4,2},{2,4},{8,6},{6,8},{12,10},{10,12},{0,14},{15,1},{5,3}... | collective-permute-start | bytes 393224 | tf_op jit(solution)/shard_map/ppermute | solution.py:33
  9.2 1.8 %collective-permute-start.2 = (bf16[256,256]{1,0:T(8,128)(2,1)S(1)}, bf16[256,256]{1,0:T(8,128)(2,1)S(1)}, u32[]{:S(2)}, u32[]{:S(2)}) collective-permute-start(bf16[256,256]{1,0:T(8,128)(2,1)S(1)} %get-tuple-element.35), channel_id=1, source_target_pairs={{4,0},{6,2},{0,4},{2,6},{12,8},{14,10},{8,12},{10,14},{5,1},{7,3},... | collective-permute-start | bytes 393224 | tf_op jit(solution)/shard_map/ppermute | solution.py:33
  11.0 0.0 collective-permute-start.3
  11.0 1.4 %collective-permute-done.refs_0_ = bf16[256,256]{1,0:T(8,128)(2,1)S(1)} collective-permute-done((bf16[256,256]{1,0:T(8,128)(2,1)S(1)}, bf16[256,256]{1,0:T(8,128)(2,1)S(1)}, u32[]{:S(2)}, u32[]{:S(2)}) %collective-permute-start) | collective-permute-done | bytes 131104 | tf_op jit(solution)/shard_map/ppermute | solution.py:33
  12.5 4.7 %collective-permute-done.1.refs_1_ = bf16[256,256]{1,0:T(8,128)(2,1)S(1)} collective-permute-done((bf16[256,256]{1,0:T(8,128)(2,1)S(1)}, bf16[256,256]{1,0:T(8,128)(2,1)S(1)}, u32[]{:S(2)}, u32[]{:S(2)}) %collective-permute-start.1) | collective-permute-done | bytes 131104 | tf_op jit(solution)/shard_map/ppermute | solution.py:33
  17.2 0.3 collective-permute-done.2.refs_2_
  17.5 0.8 %collective-permute-done.3.refs_3_ = bf16[256,256]{1,0:T(8,128)(2,1)S(1)} collective-permute-done((bf16[256,256]{1,0:T(8,128)(2,1)S(1)}, bf16[256,256]{1,0:T(8,128)(2,1)S(1)}, u32[]{:S(2)}, u32[]{:S(2)}) %collective-permute-start.3) | collective-permute-done | bytes 131104 | tf_op jit(solution)/shard_map/ppermute | solution.py:33
  18.2 0.0 copy-done
  18.3 1.9 %shard_map.112 = (bf16[8,64,256]{2,1,0:T(8,128)(2,1)S(1)}, bf16[8,64,256]{2,1,0:T(8,128)(2,1)S(1)}, bf16[8,64,256]{2,1,0:T(8,128)(2,1)S(1)}, bf16[128,256]{1,0:T...) custom-call(s32[2,8]{1,0:T(2,128)S(1)} %get-tuple-element.28.rows_re, ...), custom_call_target="tpu_custom_call" | custom-call | flops 301989888 | bytes 3543136 | tf_op jit(solution)/shard_map/pallas_call | solution.py:280
  20.2 0.2 collective-permute-start.10
  20.4 1.0 %collective-permute-start.9 = (f32[136,128]{1,0:T(8,128)S(1)}, f32[136,128]{1,0:T(8,128)S(1)}, u32[]{:S(2)}, u32[]{:S(2)}) collective-permute-start(f32[136,128]{1,0:T(8,128)S(1)} %get-tuple-element.49), channel_id=1, source_target_pairs={{2,0},{0,2},{6,4},{4,6},{10,8},{8,10},{14,12},{12,14},{3,1},{1,3},... | collective-permute-start | bytes 208904 | tf_op jit(solution)/shard_map/ppermute | solution.py:350
  21.4 0.7 %collective-permute-start.8 = (f32[136,128]{1,0:T(8,128)S(1)}, f32[136,128]{1,0:T(8,128)S(1)}, u32[]{:S(2)}, u32[]{:S(2)}) collective-permute-start(f32[136,128]{1,0:T(8,128)S(1)} %get-tuple-element.49), channel_id=1, source_target_pairs={{1,0},{0,1},{3,2},{2,3},{5,4},{4,5},{7,6},{6,7},{9,8},{8,9},{11,10... | collective-permute-start | bytes 208904 | tf_op jit(solution)/shard_map/ppermute | solution.py:352
  22.1 2.6 %collective-permute-done.10 = f32[136,128]{1,0:T(8,128)S(1)} collective-permute-done((f32[136,128]{1,0:T(8,128)S(1)}, f32[136,128]{1,0:T(8,128)S(1)}, u32[]{:S(2)}, u32[]{:S(2)}) %collective-permute-start.10) | collective-permute-done | bytes 69664 | tf_op jit(solution)/shard_map/ppermute | solution.py:353
  24.7 1.0 %collective-permute-done.9 = f32[136,128]{1,0:T(8,128)S(1)} collective-permute-done((f32[136,128]{1,0:T(8,128)S(1)}, f32[136,128]{1,0:T(8,128)S(1)}, u32[]{:S(2)}, u32[]{:S(2)}) %collective-permute-start.9) | collective-permute-done | bytes 69664 | tf_op jit(solution)/shard_map/ppermute | solution.py:350
  25.7 0.0 collective-permute-done.8
  25.7 1.3 %collective-permute-start.11 = (f32[136,128]{1,0:T(8,128)S(1)}, f32[136,128]{1,0:T(8,128)S(1)}, u32[]{:S(2)}, u32[]{:S(2)}) collective-permute-start(f32[136,128]{1,0:T(8,128)S(1)} %add_add_fusion), channel_id=1, source_target_pairs={{4,0},{6,2},{0,4},{2,6},{12,8},{14,10},{8,12},{10,14},{5,1},{7,3},... | collective-permute-start | bytes 208904 | tf_op jit(solution)/shard_map/ppermute | solution.py:350
  27.1 0.8 %collective-permute-start.4 = (bf16[128,256]{1,0:T(8,128)(2,1)S(1)}, bf16[128,256]{1,0:T(8,128)(2,1)S(1)}, u32[]{:S(2)}, u32[]{:S(2)}) collective-permute-start(bf16[128,256]{1,0:T(8,128)(2,1)S(1)} %get-tuple-element.43), channel_id=1, source_target_pairs={{12,0},{14,2},{8,4},{10,6},{4,8},{6,10},{0,12},{2,14},{13,1},{15,3... | collective-permute-start | bytes 196616 | tf_op jit(solution)/shard_map/ppermute | solution.py:33
  27.9 3.1 %collective-permute-start.5 = (bf16[128,256]{1,0:T(8,128)(2,1)S(1)}, bf16[128,256]{1,0:T(8,128)(2,1)S(1)}, u32[]{:S(2)}, u32[]{:S(2)}) collective-permute-start(bf16[128,256]{1,0:T(8,128)(2,1)S(1)} %get-tuple-element.44), channel_id=1, source_target_pairs={{14,0},{4,2},{2,4},{8,6},{6,8},{12,10},{10,12},{0,14},{15,1},{5,3}... | collective-permute-start | bytes 196616 | tf_op jit(solution)/shard_map/ppermute | solution.py:33
  30.9 0.0 collective-permute-start.6
  30.9 0.4 %collective-permute-start.7 = (bf16[128,256]{1,0:T(8,128)(2,1)S(1)}, bf16[128,256]{1,0:T(8,128)(2,1)S(1)}, u32[]{:S(2)}, u32[]{:S(2)}) collective-permute-start(bf16[128,256]{1,0:T(8,128)(2,1)S(1)} %get-tuple-element.46), channel_id=1, source_target_pairs={{2,0},{0,2},{6,4},{4,6},{10,8},{8,10},{14,12},{12,14},{3,1},{1,3},... | collective-permute-start | bytes 196616 | tf_op jit(solution)/shard_map/ppermute | solution.py:33
  31.3 0.0 collective-permute-done.11
  31.3 2.5 %collective-permute-start.12 = (f32[136,128]{1,0:T(8,128)S(1)}, f32[136,128]{1,0:T(8,128)S(1)}, u32[]{:S(2)}, u32[]{:S(2)}) collective-permute-start(f32[136,128]{1,0:T(8,128)S(1)} %add.15.mine), channel_id=1, source_target_pairs={{8,0},{10,2},{12,4},{14,6},{0,8},{2,10},{4,12},{6,14},{9,1},{11,3}... | collective-permute-start | bytes 208904 | tf_op jit(solution)/shard_map/ppermute | solution.py:350
  33.8 1.3 %shard_map.113 = (f32[8,64,128]{2,1,0:T(8,128)S(1)}, f32[8,64,128]{2,1,0:T(8,128)S(1)}, bf16[128,128]{1,0:T(8,128)(2,1)S(1)}) custom-call(bf16[8,64,128]{2,1,0:T(8,128)(2,1)S(1)} %copy-done.1, bf16[8,64,128]{2,1,0:T(8,128)(2,1)S(1)} %copy-done.2, bf16[8,64,256]{2,1,0:T(8,128)(2,1)S(1)} %get-tuple-element.37.one, ...), custom_call_target="tpu_custom_call" | custom-call | flops 100663296 | bytes 1376512 | tf_op jit(solution)/shard_map/pallas_call | solution.py:280
  35.1 0.0 collective-permute-done.4.refs_0_
  35.1 0.2 collective-permute-done.5.refs_1_
  35.3 0.5 %collective-permute-done.6.refs_2_ = bf16[128,256]{1,0:T(8,128)(2,1)S(1)} collective-permute-done((bf16[128,256]{1,0:T(8,128)(2,1)S(1)}, bf16[128,256]{1,0:T(8,128)(2,1)S(1)}, u32[]{:S(2)}, u32[]{:S(2)}) %collective-permute-start.6) | collective-permute-done | bytes 65568 | tf_op jit(solution)/shard_map/ppermute | solution.py:33
  35.8 0.0 collective-permute-done.7.refs_3_
  35.8 2.1 %shard_map.114 = (bf16[8,64,128]{2,1,0:T(8,128)(2,1)}, bf16[8,64,128]{2,1,0:T(8,128)(2,1)}) custom-call(s32[2,8]{1,0:T(2,128)S(1)} %get-tuple-element.28.rows_ref, bf16[8,64,576]{2,1,0:T(8,128)(2,1)S(1)} %copy-done, bf16[8,64,256]{2,1,0:T(8,128)(2,1)S(1)} %get-tuple-element.29.keep, bf16[8,64,256]{2,1,0:T(8,128)(2,1)S(1)} %get-tuple-element.37.one, ...), custom_call_target="tpu_custom_call" | custom-call | flops 301989888 | bytes 2457664 | tf_op jit(solution)/shard_map/pallas_call | solution.py:280
  37.9 0.0 collective-permute-done.12.other
  37.9 0.7 %shard_map.115 = (f32[4,64,64]{2,1,0:T(8,128)}, f32[1,64]{1,0:T(1,128)}) custom-call(f32[136,128]{1,0:T(8,128)S(1)} %add.15.mine, f32[136,128]{1,0:T(8,128)S(1)} %collective-permute-done.12.other), custom_call_target="tpu_custom_call" | custom-call | flops 17408 | bytes 205056 | tf_op jit(solution)/shard_map/pallas_call | solution.py:280
  (7 shorter events, 0.0 us)
Async XLA Ops:
  0.6 17.6 %copy-start = (bf16[8,64,576]{2,1,0:T(8,128)(2,1)S(1)}, bf16[8,64,576]{2,1,0:T(8,128)(2,1)}, u32[]{:S(2)}) copy-start(bf16[8,64,576]{2,1,0:T(8,128)(2,1)} %lap.3) | copy-start | bytes 1769476
  0.6 17.6 %copy-start.1 = (bf16[8,64,128]{2,1,0:T(8,128)(2,1)S(1)}, bf16[8,64,128]{2,1,0:T(8,128)(2,1)}, u32[]{:S(2)}) copy-start(bf16[8,64,128]{2,1,0:T(8,128)(2,1)} %feat_ref.3) | copy-start | bytes 393220
  0.7 17.6 %copy-start.2 = (bf16[8,64,128]{2,1,0:T(8,128)(2,1)S(1)}, bf16[8,64,128]{2,1,0:T(8,128)(2,1)}, u32[]{:S(2)}) copy-start(bf16[8,64,128]{2,1,0:T(8,128)(2,1)} %cot_ref.3) | copy-start | bytes 393220
  3.0 9.5 %collective-permute-start = (bf16[256,256]{1,0:T(8,128)(2,1)S(1)}, bf16[256,256]{1,0:T(8,128)(2,1)S(1)}, u32[]{:S(2)}, u32[]{:S(2)}) collective-permute-start(bf16[256,256]{1,0:T(8,128)(2,1)S(1)} %get-tuple-element.33), channel_id=1, source_target_pairs={{12,0},{14,2},{8,4},{10,6},{4,8},{6,10},{0,12},{2,14},{13,1},{15,3... | collective-permute-start | bytes 393224 | tf_op jit(solution)/shard_map/ppermute | solution.py:33
  8.1 9.1 %collective-permute-start.1 = (bf16[256,256]{1,0:T(8,128)(2,1)S(1)}, bf16[256,256]{1,0:T(8,128)(2,1)S(1)}, u32[]{:S(2)}, u32[]{:S(2)}) collective-permute-start(bf16[256,256]{1,0:T(8,128)(2,1)S(1)} %get-tuple-element.34), channel_id=1, source_target_pairs={{14,0},{4,2},{2,4},{8,6},{6,8},{12,10},{10,12},{0,14},{15,1},{5,3}... | collective-permute-start | bytes 393224 | tf_op jit(solution)/shard_map/ppermute | solution.py:33
  9.2 8.2 %collective-permute-start.2 = (bf16[256,256]{1,0:T(8,128)(2,1)S(1)}, bf16[256,256]{1,0:T(8,128)(2,1)S(1)}, u32[]{:S(2)}, u32[]{:S(2)}) collective-permute-start(bf16[256,256]{1,0:T(8,128)(2,1)S(1)} %get-tuple-element.35), channel_id=1, source_target_pairs={{4,0},{6,2},{0,4},{2,6},{12,8},{14,10},{8,12},{10,14},{5,1},{7,3},... | collective-permute-start | bytes 393224 | tf_op jit(solution)/shard_map/ppermute | solution.py:33
  11.0 7.2 %collective-permute-start.3 = (bf16[256,256]{1,0:T(8,128)(2,1)S(1)}, bf16[256,256]{1,0:T(8,128)(2,1)S(1)}, u32[]{:S(2)}, u32[]{:S(2)}) collective-permute-start(bf16[256,256]{1,0:T(8,128)(2,1)S(1)} %get-tuple-element.36), channel_id=1, source_target_pairs={{2,0},{0,2},{6,4},{4,6},{10,8},{8,10},{14,12},{12,14},{3,1},{1,3},... | collective-permute-start | bytes 393224 | tf_op jit(solution)/shard_map/ppermute | solution.py:33
  20.2 4.5 %collective-permute-start.10 = (f32[136,128]{1,0:T(8,128)S(1)}, f32[136,128]{1,0:T(8,128)S(1)}, u32[]{:S(2)}, u32[]{:S(2)}) collective-permute-start(f32[136,128]{1,0:T(8,128)S(1)} %get-tuple-element.49), channel_id=1, source_target_pairs={{3,0},{2,1},{1,2},{0,3},{7,4},{6,5},{5,6},{4,7},{11,8},{10,9},{9,1... | collective-permute-start | bytes 208904 | tf_op jit(solution)/shard_map/ppermute | solution.py:353
  20.4 5.3 %collective-permute-start.9 = (f32[136,128]{1,0:T(8,128)S(1)}, f32[136,128]{1,0:T(8,128)S(1)}, u32[]{:S(2)}, u32[]{:S(2)}) collective-permute-start(f32[136,128]{1,0:T(8,128)S(1)} %get-tuple-element.49), channel_id=1, source_target_pairs={{2,0},{0,2},{6,4},{4,6},{10,8},{8,10},{14,12},{12,14},{3,1},{1,3},... | collective-permute-start | bytes 208904 | tf_op jit(solution)/shard_map/ppermute | solution.py:350
  21.4 4.3 %collective-permute-start.8 = (f32[136,128]{1,0:T(8,128)S(1)}, f32[136,128]{1,0:T(8,128)S(1)}, u32[]{:S(2)}, u32[]{:S(2)}) collective-permute-start(f32[136,128]{1,0:T(8,128)S(1)} %get-tuple-element.49), channel_id=1, source_target_pairs={{1,0},{0,1},{3,2},{2,3},{5,4},{4,5},{7,6},{6,7},{9,8},{8,9},{11,10... | collective-permute-start | bytes 208904 | tf_op jit(solution)/shard_map/ppermute | solution.py:352
  25.7 5.6 %collective-permute-start.11 = (f32[136,128]{1,0:T(8,128)S(1)}, f32[136,128]{1,0:T(8,128)S(1)}, u32[]{:S(2)}, u32[]{:S(2)}) collective-permute-start(f32[136,128]{1,0:T(8,128)S(1)} %add_add_fusion), channel_id=1, source_target_pairs={{4,0},{6,2},{0,4},{2,6},{12,8},{14,10},{8,12},{10,14},{5,1},{7,3},... | collective-permute-start | bytes 208904 | tf_op jit(solution)/shard_map/ppermute | solution.py:350
  27.1 8.0 %collective-permute-start.4 = (bf16[128,256]{1,0:T(8,128)(2,1)S(1)}, bf16[128,256]{1,0:T(8,128)(2,1)S(1)}, u32[]{:S(2)}, u32[]{:S(2)}) collective-permute-start(bf16[128,256]{1,0:T(8,128)(2,1)S(1)} %get-tuple-element.43), channel_id=1, source_target_pairs={{12,0},{14,2},{8,4},{10,6},{4,8},{6,10},{0,12},{2,14},{13,1},{15,3... | collective-permute-start | bytes 196616 | tf_op jit(solution)/shard_map/ppermute | solution.py:33
  27.9 7.4 %collective-permute-start.5 = (bf16[128,256]{1,0:T(8,128)(2,1)S(1)}, bf16[128,256]{1,0:T(8,128)(2,1)S(1)}, u32[]{:S(2)}, u32[]{:S(2)}) collective-permute-start(bf16[128,256]{1,0:T(8,128)(2,1)S(1)} %get-tuple-element.44), channel_id=1, source_target_pairs={{14,0},{4,2},{2,4},{8,6},{6,8},{12,10},{10,12},{0,14},{15,1},{5,3}... | collective-permute-start | bytes 196616 | tf_op jit(solution)/shard_map/ppermute | solution.py:33
  30.9 4.8 %collective-permute-start.6 = (bf16[128,256]{1,0:T(8,128)(2,1)S(1)}, bf16[128,256]{1,0:T(8,128)(2,1)S(1)}, u32[]{:S(2)}, u32[]{:S(2)}) collective-permute-start(bf16[128,256]{1,0:T(8,128)(2,1)S(1)} %get-tuple-element.45), channel_id=1, source_target_pairs={{4,0},{6,2},{0,4},{2,6},{12,8},{14,10},{8,12},{10,14},{5,1},{7,3},... | collective-permute-start | bytes 196616 | tf_op jit(solution)/shard_map/ppermute | solution.py:33
  30.9 4.8 %collective-permute-start.7 = (bf16[128,256]{1,0:T(8,128)(2,1)S(1)}, bf16[128,256]{1,0:T(8,128)(2,1)S(1)}, u32[]{:S(2)}, u32[]{:S(2)}) collective-permute-start(bf16[128,256]{1,0:T(8,128)(2,1)S(1)} %get-tuple-element.46), channel_id=1, source_target_pairs={{2,0},{0,2},{6,4},{4,6},{10,8},{8,10},{14,12},{12,14},{3,1},{1,3},... | collective-permute-start | bytes 196616 | tf_op jit(solution)/shard_map/ppermute | solution.py:33
  31.3 6.5 %collective-permute-start.12 = (f32[136,128]{1,0:T(8,128)S(1)}, f32[136,128]{1,0:T(8,128)S(1)}, u32[]{:S(2)}, u32[]{:S(2)}) collective-permute-start(f32[136,128]{1,0:T(8,128)S(1)} %add.15.mine), channel_id=1, source_target_pairs={{8,0},{10,2},{12,4},{14,6},{0,8},{2,10},{4,12},{6,14},{9,1},{11,3}... | collective-permute-start | bytes 208904 | tf_op jit(solution)/shard_map/ppermute | solution.py:350

commit v5 on v4

--- a/solution.py
+++ b/solution.py
@@ -113,8 +113,43 @@
             send[base + pixels:base + 2 * pixels, :] = part[b].astype(BF16)
 
 
+def early_kernel(
+    feat_ref, cot_ref, lap, value, weight_hbm, bias_hbm,
+    turned, zero_sums, mix, mix_last, bias_row,
+    weight, bias, sem,
+):
+    blocks, pixels, lanes = feat_ref.shape
+    cycle = len(CYCLE_STEPS) * pixels
+    copies = [
+        pltpu.make_async_copy(weight_hbm, weight, sem.at[0]),
+        pltpu.make_async_copy(bias_hbm, bias, sem.at[1]),
+    ]
+    for copy in copies:
+        copy.start()
+    for a in range(blocks):
+        turned[a] = matmul_tn(lap[a, :, cycle:cycle + pixels], value[a])
+    feat = feat_ref[...].reshape(blocks * pixels, lanes)
+    cot = cot_ref[...].reshape(blocks * pixels, lanes)
+    zero_sums[:lanes, :] = matmul_tn(feat, cot)
+    zero_sums[lanes:, :] = jnp.broadcast_to(
+        jnp.sum(cot.astype(F32), axis=0, keepdims=True), (8, lanes)
+    )
+    for copy in copies:
+        copy.wait()
+    terms, half, _ = weight.shape
+    mix[...] = jnp.zeros_like(mix)
+    mix_last[...] = jnp.zeros_like(mix_last)
+    for m in range(lanes // half):
+        spot = slice(m * half, (m + 1) * half)
+        for k in range(terms - 1):
+            shifted = slice(k * lanes + m * half, k * lanes + (m + 1) * half)
+            mix[spot, shifted] = weight[k]
+        mix_last[spot, spot] = weight[terms - 1]
+        bias_row[:, spot] = bias[...]
+
+
 def middle_kernel(
-    rows_ref, lists_ref, feat_ref, cot_ref, lap, value, keep, part, *refs,
+    rows_ref, lists_ref, feat_ref, cot_ref, lap, keep, part, turned, zero_sums, *refs,
 ):
     gots, (one, two, spread), sends, (sums,) = refs[:4], refs[4:7], refs[7:11], refs[11:12]
     halo, halo_part, keep_far = refs[12:]
@@ -137,7 +172,7 @@
         cross = lap[a, :, cycle:cycle + pixels]
         total = part[a] + matmul(cross, halo[a]) * keep[a].astype(F32)
         one[a] = total.astype(BF16)
-        total = halo_part[a].astype(F32) + matmul_tn(cross, value[a]) * keep_far[a].astype(F32)
+        total = halo_part[a].astype(F32) + turned[a] * keep_far[a].astype(F32)
         halo[a] = total.astype(BF16)
     for a in range(blocks):
         near = ring_rows(one, a) + [halo[a], one[rows_ref[1, a]]]
@@ -150,12 +185,11 @@
         heading = send_heading(pairing, device)
         for s in range(slots):
             send[s * pixels:(s + 1) * pixels, :] = spread[lists_ref[0, s, heading]]
-    feat = feat_ref[...].reshape(flat, lanes)
     cot = cot_ref[...].reshape(flat, lanes)
     first = one[...].reshape(flat, width)
     second = two[...].reshape(flat, width)
     half = lanes // 2
-    low = matmul_tn(jnp.concatenate([feat, first[:, :lanes]], axis=1), cot)
+    low = matmul_tn(first[:, :lanes], cot)
     high = matmul_tn(
         jnp.concatenate([first[:, :lanes], second[:, :lanes]], axis=1), first[:, lanes:]
     )
@@ -165,15 +199,15 @@
             product[start:start + half, :half] + product[start + half:start + lanes, half:]
         )
 
-    sum_zero = trace(low, 0)
-    sum_one = trace(low, lanes)
+    sum_zero = trace(zero_sums, 0)
+    sum_one = trace(low, 0)
     totals = jnp.concatenate(
         [
             jnp.concatenate([sum_zero, sum_one], axis=1),
             jnp.concatenate(
                 [2.0 * trace(high, 0) - sum_zero, 2.0 * trace(high, lanes) - sum_one], axis=1
             ),
-            jnp.broadcast_to(jnp.sum(cot.astype(F32), axis=0, keepdims=True), (8, lanes)),
+            zero_sums[lanes:, :],
         ],
         axis=0,
     )
@@ -181,28 +215,15 @@
 
 
 def partial_kernel(
-    feat_ref, cot_ref, one, two, weight_hbm, bias_hbm, out_part, grad_part, mix_last,
-    mix, bias_row, weight, bias, sem,
+    rows_ref, feat_ref, cot_ref, lap, keep, one, two, spread, mix, bias_row,
+    out_part, grad_part, three_part,
 ):
     blocks, pixels, lanes = feat_ref.shape
-    copies = [
-        pltpu.make_async_copy(weight_hbm, weight, sem.at[0]),
-        pltpu.make_async_copy(bias_hbm, bias, sem.at[1]),
-    ]
-    for copy in copies:
-        copy.start()
-    for copy in copies:
-        copy.wait()
-    terms, half, _ = weight.shape
-    mix[...] = jnp.zeros_like(mix)
-    mix_last[...] = jnp.zeros_like(mix_last)
-    for m in range(lanes // half):
-        spot = slice(m * half, (m + 1) * half)
-        for k in range(terms - 1):
-            shifted = slice(k * lanes + m * half, k * lanes + (m + 1) * half)
-            mix[spot, shifted] = weight[k]
-        mix_last[spot, spot] = weight[terms - 1]
-        bias_row[:, spot] = bias[...]
+    cycle = len(CYCLE_STEPS) * pixels
+    for a in range(blocks):
+        total = matmul(lap[a, :, :cycle], jnp.concatenate(ring_rows(spread, a), axis=0))
+        total = total + matmul(lap[a, :, cycle + pixels:], spread[rows_ref[1, a]])
+        three_part[a] = 2.0 * total * keep[a].astype(F32) - one[a].astype(F32)
     flat = blocks * pixels
     first = one[...].reshape(flat, 2 * lanes)
     second = two[...].reshape(flat, 2 * lanes)
@@ -217,7 +238,7 @@
 
 
 def last_kernel(
-    rows_ref, lap, keep, one, spread, out_part, grad_part, mix_last, *refs,
+    rows_ref, lap, keep, out_part, grad_part, three_part, mix_last, *refs,
 ):
     gots, (out_hbm, grad_hbm), (halo, three, out_ref, grad_ref, sem) = refs[:4], refs[4:6], refs[6:]
     blocks, pixels, lanes = out_part.shape
@@ -228,14 +249,14 @@
         for s in range(slots):
             row = row_of_slot(rows_ref, heading * slots + s)
             halo[row] = got[s * pixels:(s + 1) * pixels, :]
+    cycle = len(CYCLE_STEPS) * pixels
     group = blocks // SPLIT
     size = group * pixels
     copies = []
     for start in range(0, blocks, group):
         for a in range(start, start + group):
-            near = ring_rows(spread, a) + [halo[a], spread[rows_ref[1, a]]]
-            total = matmul(lap[a], jnp.concatenate(near, axis=0)) * keep[a].astype(F32)
-            three[a] = (2.0 * total - one[a].astype(F32)).astype(BF16)
+            total = matmul(lap[a, :, cycle:cycle + pixels], halo[a]) * keep[a].astype(F32)
+            three[a] = (three_part[a] + 2.0 * total).astype(BF16)
         mine = pl.ds(start, group)
         last = three[mine].reshape(size, 2 * lanes)
         total = out_part[mine].reshape(size, lanes) + matmul(last[:, :lanes], mix_last[...])
@@ -317,30 +338,38 @@
         hbm_from=0,
     )
     gots = [exchange(send, k) for k, send in zip(ORDER, sends)]
+    *early, mix, mix_last, bias_row = call(
+        early_kernel,
+        [wide, shape((lanes + 8, lanes), F32)]
+        + [shape((lanes, (terms - 1) * lanes), BF16), shape((lanes, lanes), BF16)]
+        + [shape((1, lanes), F32)],
+        [features, cotangent, lap_tiles, value, cheb_weights, out_bias.reshape(1, chan_out)],
+        [
+            pltpu.VMEM(cheb_weights.shape, BF16),
+            pltpu.VMEM((1, chan_out), F32),
+            pltpu.SemaphoreType.DMA((2,)),
+        ],
+        2 * flat * (width * pixels + lanes * lanes),
+        hbm_from=4,
+    )
     one, two, spread, *sends, sums = call(
         middle_kernel,
         [field, field, field]
         + [shape((slots * pixels, width), BF16)] * 4
         + [shape((lanes + 8, lanes), F32)],
-        [rows, lists, features, cotangent, lap_tiles, value, keep, part, *gots],
+        [rows, lists, features, cotangent, lap_tiles, keep, part, *early, *gots],
         [scratch_field, scratch_field, scratch_field],
         2 * apply_flops,
     )
     gots = [exchange(send, k) for k, send in zip(ORDER_TWO, sends)]
     half_field = shape((blocks, pixels, lanes), F32)
-    *parts, mix_last = call(
+    parts = call(
         partial_kernel,
-        [half_field, half_field, shape((lanes, lanes), BF16)],
-        [features, cotangent, one, two, cheb_weights, out_bias.reshape(1, chan_out)],
-        [
-            pltpu.VMEM((lanes, (terms - 1) * lanes), BF16),
-            pltpu.VMEM((1, lanes), F32),
-            pltpu.VMEM(cheb_weights.shape, BF16),
-            pltpu.VMEM((1, chan_out), F32),
-            pltpu.SemaphoreType.DMA((2,)),
-        ],
-        4 * flat * lanes * lanes * (terms - 1),
-        hbm_from=4,
+        [half_field, half_field, wide],
+        [rows, features, cotangent, lap_tiles, keep, one, two, spread]
+        + [mix, bias_row],
+        [],
+        apply_flops + 4 * flat * lanes * lanes * (terms - 1),
     )
     count = lax.axis_size("pix")
     pair = lax.axis_size("dp")
@@ -363,11 +392,11 @@
     output_maps, grad_features = call(
         last_kernel,
         [shape(features.shape, BF16), shape(features.shape, BF16)],
-        [rows, lap_tiles, keep, one, spread, *parts, mix_last, *gots],
+        [rows, lap_tiles, keep, *parts, mix_last, *gots],
         [scratch_field, scratch_field]
         + [pltpu.VMEM(features.shape, BF16)] * 2
         + [pltpu.SemaphoreType.DMA((2 * SPLIT,))],
-        2 * apply_flops,
+        apply_flops,
         out_hbm=True,
     )
     grad_weights, grad_bias = call(

time: 38.8 us -> 38.3 us (0.987)
  waiting for transfers between devices: 11.5 us -> 10.4 us
  Pallas kernels: 8.32 us -> 8.87 us
    ppermute x8, waiting for transfers between devices: 7.88 us -> 6.82 us  [exchange(): return lax.ppermute(block, 'pix', route)]
    pallas_call x5 -> x6, Pallas kernels: 8.32 us -> 8.87 us  [call(): pl.pallas_call(kernel, out_shape=outs, in_specs=[place(i, x) for i, x in...]
  transfers between devices with their start and end apart: 13 -> 13, of which waited for: 8 -> 8; matrix products, arithmetic and copies ran while one was open for 0% -> 0% of each run, Pallas kernels for 9% -> 11%
where the time goes in v5:
time: 38.3 us; the launch traced here: 38.1 us
  starting transfers between devices  18 us (47%)
  waiting for transfers between devices  10.4 us (27%)
  Pallas kernels  8.87 us (23%)
  between operations  0.74 us (2%)
    ppermute x8, starting transfers between devices, exchange(): return lax.ppermute(block, 'pix', route)  12.3 us
    pallas_call x6, Pallas kernels, call(): pl.pallas_call(kernel, out_shape=outs, in_specs=[place(i, x) for i, x in...  8.87 us
    ppermute x8, waiting for transfers between devices, exchange(): return lax.ppermute(block, 'pix', route)  6.82 us
    ppermute x3, starting transfers between devices, swap(): return lax.ppermute(block, 'pix', [(i ^ reach, i) for i in range(count)])  4.81 us
    ppermute x1, waiting for transfers between devices, local(): lax.ppermute(sums, ('pix', 'dp'), [(i ^ pair + 1, i) for i in range(count...  2.62 us
    ppermute x3, waiting for transfers between devices, swap(): return lax.ppermute(block, 'pix', [(i ^ reach, i) for i in range(count)])  0.99 us
  transfers between devices with their start and end apart: 13, of which 8 were waited for; matrix products, arithmetic and copies ran while one was open for 0% of the time, Pallas kernels for 11%

profile of v5, /device:TPU:0, one launch (start us, length us, event | category | flops | bytes accessed | tf_op | source)
XLA Modules:
  0.0 38.1 jit_solution(4182507975557240901)
XLA Ops:
  0.7 2.3 %shard_map.111 = (bf16[256,256]{1,0:T(8,128)(2,1)S(1)}, bf16[256,256]{1,0:T(8,128)(2,1)S(1)}, bf16[256,256]{1,0:T(8,128)(2,1)S(1)}, bf16[256,256]{1,0:T(8,128)(2...) custom-call(s32[2,8]{1,0:T(2,128)} %bitcast.4, ...), custom_call_target="tpu_custom_call" | custom-call | flops 150994944 | bytes 2427072 | tf_op jit(solution)/shard_map/pallas_call | solution.py:301
  2.9 5.1 %collective-permute-start = (bf16[256,256]{1,0:T(8,128)(2,1)S(1)}, bf16[256,256]{1,0:T(8,128)(2,1)S(1)}, u32[]{:S(2)}, u32[]{:S(2)}) collective-permute-start(bf16[256,256]{1,0:T(8,128)(2,1)S(1)} %get-tuple-element.40), channel_id=1, source_target_pairs={{12,0},{14,2},{8,4},{10,6},{4,8},{6,10},{0,12},{2,14},{13,1},{15,3... | collective-permute-start | bytes 393224 | tf_op jit(solution)/shard_map/ppermute | solution.py:33
  8.1 1.2 %collective-permute-start.1 = (bf16[256,256]{1,0:T(8,128)(2,1)S(1)}, bf16[256,256]{1,0:T(8,128)(2,1)S(1)}, u32[]{:S(2)}, u32[]{:S(2)}) collective-permute-start(bf16[256,256]{1,0:T(8,128)(2,1)S(1)} %get-tuple-element.41), channel_id=1, source_target_pairs={{14,0},{4,2},{2,4},{8,6},{6,8},{12,10},{10,12},{0,14},{15,1},{5,3}... | collective-permute-start | bytes 393224 | tf_op jit(solution)/shard_map/ppermute | solution.py:33
  9.2 1.8 %collective-permute-start.2 = (bf16[256,256]{1,0:T(8,128)(2,1)S(1)}, bf16[256,256]{1,0:T(8,128)(2,1)S(1)}, u32[]{:S(2)}, u32[]{:S(2)}) collective-permute-start(bf16[256,256]{1,0:T(8,128)(2,1)S(1)} %get-tuple-element.42), channel_id=1, source_target_pairs={{4,0},{6,2},{0,4},{2,6},{12,8},{14,10},{8,12},{10,14},{5,1},{7,3},... | collective-permute-start | bytes 393224 | tf_op jit(solution)/shard_map/ppermute | solution.py:33
  11.0 0.0 collective-permute-start.3
  11.0 1.0 %shard_map.112 = (f32[8,64,256]{2,1,0:T(8,128)S(1)}, f32[136,128]{1,0:T(8,128)S(1)}, bf16[128,384]{1,0:T(8,128)(2,1)S(1)}, bf16[128,128]{1,0:T(8,128)(2,1)S(1)}, f32[1,128]{1,0:T(1,128)S(1)}) custom-call(bf16[8,64,128]{2,1,0:T(8,128)(2,1)S(1)} %copy-done.1, bf16[8,64,128]{2,1,0:T(8,128)(2,1)S(1)} %copy-done.2, bf16[8,64,576]{2,1,0:T(8,128)(2,1)S(1)} %copy-done, ...), custom_call_target="tpu_custom_call" | custom-call | flops 33554432 | bytes 1872640 | tf_op jit(solution)/shard_map/pallas_call | solution.py:301
  12.0 0.4 %collective-permute-done.refs_0_ = bf16[256,256]{1,0:T(8,128)(2,1)S(1)} collective-permute-done((bf16[256,256]{1,0:T(8,128)(2,1)S(1)}, bf16[256,256]{1,0:T(8,128)(2,1)S(1)}, u32[]{:S(2)}, u32[]{:S(2)}) %collective-permute-start) | collective-permute-done | bytes 131104 | tf_op jit(solution)/shard_map/ppermute | solution.py:33
  12.4 4.7 %collective-permute-done.1.refs_1_ = bf16[256,256]{1,0:T(8,128)(2,1)S(1)} collective-permute-done((bf16[256,256]{1,0:T(8,128)(2,1)S(1)}, bf16[256,256]{1,0:T(8,128)(2,1)S(1)}, u32[]{:S(2)}, u32[]{:S(2)}) %collective-permute-start.1) | collective-permute-done | bytes 131104 | tf_op jit(solution)/shard_map/ppermute | solution.py:33
  17.1 0.3 collective-permute-done.2.refs_2_
  17.4 0.8 %collective-permute-done.3.refs_3_ = bf16[256,256]{1,0:T(8,128)(2,1)S(1)} collective-permute-done((bf16[256,256]{1,0:T(8,128)(2,1)S(1)}, bf16[256,256]{1,0:T(8,128)(2,1)S(1)}, u32[]{:S(2)}, u32[]{:S(2)}) %collective-permute-start.3) | collective-permute-done | bytes 131104 | tf_op jit(solution)/shard_map/ppermute | solution.py:33
  18.2 1.7 %shard_map.113 = (bf16[8,64,256]{2,1,0:T(8,128)(2,1)S(1)}, bf16[8,64,256]{2,1,0:T(8,128)(2,1)S(1)}, bf16[8,64,256]{2,1,0:T(8,128)(2,1)S(1)}, bf16[128,256]{1,0:T...) custom-call(s32[2,8]{1,0:T(2,128)S(1)} %get-tuple-element.33.rows_re, ...), custom_call_target="tpu_custom_call" | custom-call | flops 301989888 | bytes 3874912 | tf_op jit(solution)/shard_map/pallas_call | solution.py:301
  20.0 0.2 collective-permute-start.10
  20.2 1.0 %collective-permute-start.9 = (f32[136,128]{1,0:T(8,128)S(1)}, f32[136,128]{1,0:T(8,128)S(1)}, u32[]{:S(2)}, u32[]{:S(2)}) collective-permute-start(f32[136,128]{1,0:T(8,128)S(1)} %get-tuple-element.59), channel_id=1, source_target_pairs={{2,0},{0,2},{6,4},{4,6},{10,8},{8,10},{14,12},{12,14},{3,1},{1,3},... | collective-permute-start | bytes 208904 | tf_op jit(solution)/shard_map/ppermute | solution.py:379
  21.2 0.7 %collective-permute-start.8 = (f32[136,128]{1,0:T(8,128)S(1)}, f32[136,128]{1,0:T(8,128)S(1)}, u32[]{:S(2)}, u32[]{:S(2)}) collective-permute-start(f32[136,128]{1,0:T(8,128)S(1)} %get-tuple-element.59), channel_id=1, source_target_pairs={{1,0},{0,1},{3,2},{2,3},{5,4},{4,5},{7,6},{6,7},{9,8},{8,9},{11,10... | collective-permute-start | bytes 208904 | tf_op jit(solution)/shard_map/ppermute | solution.py:381
  21.9 2.6 %collective-permute-done.10 = f32[136,128]{1,0:T(8,128)S(1)} collective-permute-done((f32[136,128]{1,0:T(8,128)S(1)}, f32[136,128]{1,0:T(8,128)S(1)}, u32[]{:S(2)}, u32[]{:S(2)}) %collective-permute-start.10) | collective-permute-done | bytes 69664 | tf_op jit(solution)/shard_map/ppermute | solution.py:382
  24.5 1.0 %collective-permute-done.9 = f32[136,128]{1,0:T(8,128)S(1)} collective-permute-done((f32[136,128]{1,0:T(8,128)S(1)}, f32[136,128]{1,0:T(8,128)S(1)}, u32[]{:S(2)}, u32[]{:S(2)}) %collective-permute-start.9) | collective-permute-done | bytes 69664 | tf_op jit(solution)/shard_map/ppermute | solution.py:379
  25.5 0.0 collective-permute-done.8
  25.5 1.3 %collective-permute-start.11 = (f32[136,128]{1,0:T(8,128)S(1)}, f32[136,128]{1,0:T(8,128)S(1)}, u32[]{:S(2)}, u32[]{:S(2)}) collective-permute-start(f32[136,128]{1,0:T(8,128)S(1)} %add_add_fusion), channel_id=1, source_target_pairs={{4,0},{6,2},{0,4},{2,6},{12,8},{14,10},{8,12},{10,14},{5,1},{7,3},... | collective-permute-start | bytes 208904 | tf_op jit(solution)/shard_map/ppermute | solution.py:379
  26.8 0.8 %collective-permute-start.4 = (bf16[128,256]{1,0:T(8,128)(2,1)S(1)}, bf16[128,256]{1,0:T(8,128)(2,1)S(1)}, u32[]{:S(2)}, u32[]{:S(2)}) collective-permute-start(bf16[128,256]{1,0:T(8,128)(2,1)S(1)} %get-tuple-element.53), channel_id=1, source_target_pairs={{12,0},{14,2},{8,4},{10,6},{4,8},{6,10},{0,12},{2,14},{13,1},{15,3... | collective-permute-start | bytes 196616 | tf_op jit(solution)/shard_map/ppermute | solution.py:33
  27.6 3.1 %collective-permute-start.5 = (bf16[128,256]{1,0:T(8,128)(2,1)S(1)}, bf16[128,256]{1,0:T(8,128)(2,1)S(1)}, u32[]{:S(2)}, u32[]{:S(2)}) collective-permute-start(bf16[128,256]{1,0:T(8,128)(2,1)S(1)} %get-tuple-element.54), channel_id=1, source_target_pairs={{14,0},{4,2},{2,4},{8,6},{6,8},{12,10},{10,12},{0,14},{15,1},{5,3}... | collective-permute-start | bytes 196616 | tf_op jit(solution)/shard_map/ppermute | solution.py:33
  30.7 0.0 collective-permute-start.6
  30.7 0.4 %collective-permute-start.7 = (bf16[128,256]{1,0:T(8,128)(2,1)S(1)}, bf16[128,256]{1,0:T(8,128)(2,1)S(1)}, u32[]{:S(2)}, u32[]{:S(2)}) collective-permute-start(bf16[128,256]{1,0:T(8,128)(2,1)S(1)} %get-tuple-element.56), channel_id=1, source_target_pairs={{2,0},{0,2},{6,4},{4,6},{10,8},{8,10},{14,12},{12,14},{3,1},{1,3},... | collective-permute-start | bytes 196616 | tf_op jit(solution)/shard_map/ppermute | solution.py:33
  31.1 0.0 collective-permute-done.11
  31.1 2.5 %collective-permute-start.12 = (f32[136,128]{1,0:T(8,128)S(1)}, f32[136,128]{1,0:T(8,128)S(1)}, u32[]{:S(2)}, u32[]{:S(2)}) collective-permute-start(f32[136,128]{1,0:T(8,128)S(1)} %add.15.mine), channel_id=1, source_target_pairs={{8,0},{10,2},{12,4},{14,6},{0,8},{2,10},{4,12},{6,14},{9,1},{11,3}... | collective-permute-start | bytes 208904 | tf_op jit(solution)/shard_map/ppermute | solution.py:379
  33.6 1.3 %shard_map.114 = (f32[8,64,128]{2,1,0:T(8,128)S(1)}, f32[8,64,128]{2,1,0:T(8,128)S(1)}, f32[8,64,256]{2,1,0:T(8,128)S(1)}) custom-call(s32[2,8]{1,0:T(2,128)S(1)} %get-tuple-element.33.rows_ref, bf16[8,64,128]{2,1,0:T(8,128)(2,1)S(1)} %copy-done.1, bf16[8,64,128]{2,1,0:T(8,128)(2,1)S(1)} %copy-done.2, bf16[8,64,576]{2,1,0:T(8,128)(2,1)S(1)} %copy-done, ...), custom_call_target="tpu_custom_call" | custom-call | flops 251658240 | bytes 3048000 | tf_op jit(solution)/shard_map/pallas_call | solution.py:301
  34.9 0.0 collective-permute-done.4.refs_0_
  34.9 0.2 collective-permute-done.5.refs_1_
  35.1 0.5 %collective-permute-done.6.refs_2_ = bf16[128,256]{1,0:T(8,128)(2,1)S(1)} collective-permute-done((bf16[128,256]{1,0:T(8,128)(2,1)S(1)}, bf16[128,256]{1,0:T(8,128)(2,1)S(1)}, u32[]{:S(2)}, u32[]{:S(2)}) %collective-permute-start.6) | collective-permute-done | bytes 65568 | tf_op jit(solution)/shard_map/ppermute | solution.py:33
  35.5 0.0 collective-permute-done.7.refs_3_
  35.6 1.8 %shard_map.115 = (bf16[8,64,128]{2,1,0:T(8,128)(2,1)}, bf16[8,64,128]{2,1,0:T(8,128)(2,1)}) custom-call(s32[2,8]{1,0:T(2,128)S(1)} %get-tuple-element.33.rows_ref, bf16[8,64,576]{2,1,0:T(8,128)(2,1)S(1)} %copy-done, bf16[8,64,256]{2,1,0:T(8,128)(2,1)S(1)} %get-tuple-element.34.keep, f32[8,64,128]{2,1,0:T(8,128)S(1)} %get-tuple-element.49.out_part, ...), custom_call_target="tpu_custom_call" | custom-call | flops 150994944 | bytes 2457664 | tf_op jit(solution)/shard_map/pallas_call | solution.py:301
  37.4 0.0 collective-permute-done.12.other
  37.4 0.7 %shard_map.116 = (f32[4,64,64]{2,1,0:T(8,128)}, f32[1,64]{1,0:T(1,128)}) custom-call(f32[136,128]{1,0:T(8,128)S(1)} %add.15.mine, f32[136,128]{1,0:T(8,128)S(1)} %collective-permute-done.12.other), custom_call_target="tpu_custom_call" | custom-call | flops 17408 | bytes 205056 | tf_op jit(solution)/shard_map/pallas_call | solution.py:301
  (8 shorter events, 0.0 us)
Async XLA Ops:
  0.6 10.4 %copy-start = (bf16[8,64,576]{2,1,0:T(8,128)(2,1)S(1)}, bf16[8,64,576]{2,1,0:T(8,128)(2,1)}, u32[]{:S(2)}) copy-start(bf16[8,64,576]{2,1,0:T(8,128)(2,1)} %lap.7) | copy-start | bytes 1769476
  0.6 10.4 %copy-start.1 = (bf16[8,64,128]{2,1,0:T(8,128)(2,1)S(1)}, bf16[8,64,128]{2,1,0:T(8,128)(2,1)}, u32[]{:S(2)}) copy-start(bf16[8,64,128]{2,1,0:T(8,128)(2,1)} %feat_ref.5) | copy-start | bytes 393220
  0.7 10.4 %copy-start.2 = (bf16[8,64,128]{2,1,0:T(8,128)(2,1)S(1)}, bf16[8,64,128]{2,1,0:T(8,128)(2,1)}, u32[]{:S(2)}) copy-start(bf16[8,64,128]{2,1,0:T(8,128)(2,1)} %cot_ref.5) | copy-start | bytes 393220
  2.9 9.5 %collective-permute-start = (bf16[256,256]{1,0:T(8,128)(2,1)S(1)}, bf16[256,256]{1,0:T(8,128)(2,1)S(1)}, u32[]{:S(2)}, u32[]{:S(2)}) collective-permute-start(bf16[256,256]{1,0:T(8,128)(2,1)S(1)} %get-tuple-element.40), channel_id=1, source_target_pairs={{12,0},{14,2},{8,4},{10,6},{4,8},{6,10},{0,12},{2,14},{13,1},{15,3... | collective-permute-start | bytes 393224 | tf_op jit(solution)/shard_map/ppermute | solution.py:33
  8.1 9.1 %collective-permute-start.1 = (bf16[256,256]{1,0:T(8,128)(2,1)S(1)}, bf16[256,256]{1,0:T(8,128)(2,1)S(1)}, u32[]{:S(2)}, u32[]{:S(2)}) collective-permute-start(bf16[256,256]{1,0:T(8,128)(2,1)S(1)} %get-tuple-element.41), channel_id=1, source_target_pairs={{14,0},{4,2},{2,4},{8,6},{6,8},{12,10},{10,12},{0,14},{15,1},{5,3}... | collective-permute-start | bytes 393224 | tf_op jit(solution)/shard_map/ppermute | solution.py:33
  9.2 8.2 %collective-permute-start.2 = (bf16[256,256]{1,0:T(8,128)(2,1)S(1)}, bf16[256,256]{1,0:T(8,128)(2,1)S(1)}, u32[]{:S(2)}, u32[]{:S(2)}) collective-permute-start(bf16[256,256]{1,0:T(8,128)(2,1)S(1)} %get-tuple-element.42), channel_id=1, source_target_pairs={{4,0},{6,2},{0,4},{2,6},{12,8},{14,10},{8,12},{10,14},{5,1},{7,3},... | collective-permute-start | bytes 393224 | tf_op jit(solution)/shard_map/ppermute | solution.py:33
  11.0 7.2 %collective-permute-start.3 = (bf16[256,256]{1,0:T(8,128)(2,1)S(1)}, bf16[256,256]{1,0:T(8,128)(2,1)S(1)}, u32[]{:S(2)}, u32[]{:S(2)}) collective-permute-start(bf16[256,256]{1,0:T(8,128)(2,1)S(1)} %get-tuple-element.43), channel_id=1, source_target_pairs={{2,0},{0,2},{6,4},{4,6},{10,8},{8,10},{14,12},{12,14},{3,1},{1,3},... | collective-permute-start | bytes 393224 | tf_op jit(solution)/shard_map/ppermute | solution.py:33
  20.0 4.5 %collective-permute-start.10 = (f32[136,128]{1,0:T(8,128)S(1)}, f32[136,128]{1,0:T(8,128)S(1)}, u32[]{:S(2)}, u32[]{:S(2)}) collective-permute-start(f32[136,128]{1,0:T(8,128)S(1)} %get-tuple-element.59), channel_id=1, source_target_pairs={{3,0},{2,1},{1,2},{0,3},{7,4},{6,5},{5,6},{4,7},{11,8},{10,9},{9,1... | collective-permute-start | bytes 208904 | tf_op jit(solution)/shard_map/ppermute | solution.py:382
  20.2 5.3 %collective-permute-start.9 = (f32[136,128]{1,0:T(8,128)S(1)}, f32[136,128]{1,0:T(8,128)S(1)}, u32[]{:S(2)}, u32[]{:S(2)}) collective-permute-start(f32[136,128]{1,0:T(8,128)S(1)} %get-tuple-element.59), channel_id=1, source_target_pairs={{2,0},{0,2},{6,4},{4,6},{10,8},{8,10},{14,12},{12,14},{3,1},{1,3},... | collective-permute-start | bytes 208904 | tf_op jit(solution)/shard_map/ppermute | solution.py:379
  21.2 4.3 %collective-permute-start.8 = (f32[136,128]{1,0:T(8,128)S(1)}, f32[136,128]{1,0:T(8,128)S(1)}, u32[]{:S(2)}, u32[]{:S(2)}) collective-permute-start(f32[136,128]{1,0:T(8,128)S(1)} %get-tuple-element.59), channel_id=1, source_target_pairs={{1,0},{0,1},{3,2},{2,3},{5,4},{4,5},{7,6},{6,7},{9,8},{8,9},{11,10... | collective-permute-start | bytes 208904 | tf_op jit(solution)/shard_map/ppermute | solution.py:381
  25.5 5.6 %collective-permute-start.11 = (f32[136,128]{1,0:T(8,128)S(1)}, f32[136,128]{1,0:T(8,128)S(1)}, u32[]{:S(2)}, u32[]{:S(2)}) collective-permute-start(f32[136,128]{1,0:T(8,128)S(1)} %add_add_fusion), channel_id=1, source_target_pairs={{4,0},{6,2},{0,4},{2,6},{12,8},{14,10},{8,12},{10,14},{5,1},{7,3},... | collective-permute-start | bytes 208904 | tf_op jit(solution)/shard_map/ppermute | solution.py:379
  26.8 8.1 %collective-permute-start.4 = (bf16[128,256]{1,0:T(8,128)(2,1)S(1)}, bf16[128,256]{1,0:T(8,128)(2,1)S(1)}, u32[]{:S(2)}, u32[]{:S(2)}) collective-permute-start(bf16[128,256]{1,0:T(8,128)(2,1)S(1)} %get-tuple-element.53), channel_id=1, source_target_pairs={{12,0},{14,2},{8,4},{10,6},{4,8},{6,10},{0,12},{2,14},{13,1},{15,3... | collective-permute-start | bytes 196616 | tf_op jit(solution)/shard_map/ppermute | solution.py:33
  27.6 7.4 %collective-permute-start.5 = (bf16[128,256]{1,0:T(8,128)(2,1)S(1)}, bf16[128,256]{1,0:T(8,128)(2,1)S(1)}, u32[]{:S(2)}, u32[]{:S(2)}) collective-permute-start(bf16[128,256]{1,0:T(8,128)(2,1)S(1)} %get-tuple-element.54), channel_id=1, source_target_pairs={{14,0},{4,2},{2,4},{8,6},{6,8},{12,10},{10,12},{0,14},{15,1},{5,3}... | collective-permute-start | bytes 196616 | tf_op jit(solution)/shard_map/ppermute | solution.py:33
  30.7 4.8 %collective-permute-start.6 = (bf16[128,256]{1,0:T(8,128)(2,1)S(1)}, bf16[128,256]{1,0:T(8,128)(2,1)S(1)}, u32[]{:S(2)}, u32[]{:S(2)}) collective-permute-start(bf16[128,256]{1,0:T(8,128)(2,1)S(1)} %get-tuple-element.55), channel_id=1, source_target_pairs={{4,0},{6,2},{0,4},{2,6},{12,8},{14,10},{8,12},{10,14},{5,1},{7,3},... | collective-permute-start | bytes 196616 | tf_op jit(solution)/shard_map/ppermute | solution.py:33
  30.7 4.8 %collective-permute-start.7 = (bf16[128,256]{1,0:T(8,128)(2,1)S(1)}, bf16[128,256]{1,0:T(8,128)(2,1)S(1)}, u32[]{:S(2)}, u32[]{:S(2)}) collective-permute-start(bf16[128,256]{1,0:T(8,128)(2,1)S(1)} %get-tuple-element.56), channel_id=1, source_target_pairs={{2,0},{0,2},{6,4},{4,6},{10,8},{8,10},{14,12},{12,14},{3,1},{1,3},... | collective-permute-start | bytes 196616 | tf_op jit(solution)/shard_map/ppermute | solution.py:33
  31.1 6.2 %collective-permute-start.12 = (f32[136,128]{1,0:T(8,128)S(1)}, f32[136,128]{1,0:T(8,128)S(1)}, u32[]{:S(2)}, u32[]{:S(2)}) collective-permute-start(f32[136,128]{1,0:T(8,128)S(1)} %add.15.mine), channel_id=1, source_target_pairs={{8,0},{10,2},{12,4},{14,6},{0,8},{2,10},{4,12},{6,14},{9,1},{11,3}... | collective-permute-start | bytes 208904 | tf_op jit(solution)/shard_map/ppermute | solution.py:379

commit v6 on v5

--- a/solution.py
+++ b/solution.py
@@ -11,7 +11,7 @@
 CYCLE_STEPS = (0, -1, 1, -2, 2, -3, 3)
 ORDER = (3, 1, 2, 0)
 ORDER_TWO = (3, 1, 2, 0)
-SPLIT = 2
+SPLIT = 1
 OUTSIDE = 16
 F32 = jnp.float32
 BF16 = jnp.bfloat16

time: 38.3 us -> 38.2 us (level)
  no operation moved by 1% of the time
where the time goes in v6:
time: 38.2 us; the launch traced here: 38 us
  starting transfers between devices  18 us (47%)
  waiting for transfers between devices  10.4 us (27%)
  Pallas kernels  8.76 us (23%)
  between operations  0.74 us (2%)
    ppermute x8, starting transfers between devices, exchange(): return lax.ppermute(block, 'pix', route)  12.3 us
    pallas_call x6, Pallas kernels, call(): pl.pallas_call(kernel, out_shape=outs, in_specs=[place(i, x) for i, x in...  8.76 us
    ppermute x8, waiting for transfers between devices, exchange(): return lax.ppermute(block, 'pix', route)  6.83 us
    ppermute x3, starting transfers between devices, swap(): return lax.ppermute(block, 'pix', [(i ^ reach, i) for i in range(count)])  4.81 us
    ppermute x1, waiting for transfers between devices, local(): lax.ppermute(sums, ('pix', 'dp'), [(i ^ pair + 1, i) for i in range(count...  2.62 us
    ppermute x3, waiting for transfers between devices, swap(): return lax.ppermute(block, 'pix', [(i ^ reach, i) for i in range(count)])  0.99 us
  transfers between devices with their start and end apart: 13, of which 8 were waited for; matrix products, arithmetic and copies ran while one was open for 0% of the time, Pallas kernels for 11%

profile of v6, /device:TPU:0, one launch (start us, length us, event | category | flops | bytes accessed | tf_op | source)
XLA Modules:
  0.0 38.0 jit_solution(13757918255002244996)
XLA Ops:
  0.7 2.3 %shard_map.111 = (bf16[256,256]{1,0:T(8,128)(2,1)S(1)}, bf16[256,256]{1,0:T(8,128)(2,1)S(1)}, bf16[256,256]{1,0:T(8,128)(2,1)S(1)}, bf16[256,256]{1,0:T(8,128)(2...) custom-call(s32[2,8]{1,0:T(2,128)} %bitcast.4, ...), custom_call_target="tpu_custom_call" | custom-call | flops 150994944 | bytes 2427072 | tf_op jit(solution)/shard_map/pallas_call | solution.py:301
  2.9 5.1 %collective-permute-start = (bf16[256,256]{1,0:T(8,128)(2,1)S(1)}, bf16[256,256]{1,0:T(8,128)(2,1)S(1)}, u32[]{:S(2)}, u32[]{:S(2)}) collective-permute-start(bf16[256,256]{1,0:T(8,128)(2,1)S(1)} %get-tuple-element.40), channel_id=1, source_target_pairs={{12,0},{14,2},{8,4},{10,6},{4,8},{6,10},{0,12},{2,14},{13,1},{15,3... | collective-permute-start | bytes 393224 | tf_op jit(solution)/shard_map/ppermute | solution.py:33
  8.1 1.2 %collective-permute-start.1 = (bf16[256,256]{1,0:T(8,128)(2,1)S(1)}, bf16[256,256]{1,0:T(8,128)(2,1)S(1)}, u32[]{:S(2)}, u32[]{:S(2)}) collective-permute-start(bf16[256,256]{1,0:T(8,128)(2,1)S(1)} %get-tuple-element.41), channel_id=1, source_target_pairs={{14,0},{4,2},{2,4},{8,6},{6,8},{12,10},{10,12},{0,14},{15,1},{5,3}... | collective-permute-start | bytes 393224 | tf_op jit(solution)/shard_map/ppermute | solution.py:33
  9.2 1.8 %collective-permute-start.2 = (bf16[256,256]{1,0:T(8,128)(2,1)S(1)}, bf16[256,256]{1,0:T(8,128)(2,1)S(1)}, u32[]{:S(2)}, u32[]{:S(2)}) collective-permute-start(bf16[256,256]{1,0:T(8,128)(2,1)S(1)} %get-tuple-element.42), channel_id=1, source_target_pairs={{4,0},{6,2},{0,4},{2,6},{12,8},{14,10},{8,12},{10,14},{5,1},{7,3},... | collective-permute-start | bytes 393224 | tf_op jit(solution)/shard_map/ppermute | solution.py:33
  11.0 0.0 collective-permute-start.3
  11.0 1.0 %shard_map.112 = (f32[8,64,256]{2,1,0:T(8,128)S(1)}, f32[136,128]{1,0:T(8,128)S(1)}, bf16[128,384]{1,0:T(8,128)(2,1)S(1)}, bf16[128,128]{1,0:T(8,128)(2,1)S(1)}, f32[1,128]{1,0:T(1,128)S(1)}) custom-call(bf16[8,64,128]{2,1,0:T(8,128)(2,1)S(1)} %copy-done.1, bf16[8,64,128]{2,1,0:T(8,128)(2,1)S(1)} %copy-done.2, bf16[8,64,576]{2,1,0:T(8,128)(2,1)S(1)} %copy-done, ...), custom_call_target="tpu_custom_call" | custom-call | flops 33554432 | bytes 1872640 | tf_op jit(solution)/shard_map/pallas_call | solution.py:301
  12.0 0.4 %collective-permute-done.refs_0_ = bf16[256,256]{1,0:T(8,128)(2,1)S(1)} collective-permute-done((bf16[256,256]{1,0:T(8,128)(2,1)S(1)}, bf16[256,256]{1,0:T(8,128)(2,1)S(1)}, u32[]{:S(2)}, u32[]{:S(2)}) %collective-permute-start) | collective-permute-done | bytes 131104 | tf_op jit(solution)/shard_map/ppermute | solution.py:33
  12.4 4.7 %collective-permute-done.1.refs_1_ = bf16[256,256]{1,0:T(8,128)(2,1)S(1)} collective-permute-done((bf16[256,256]{1,0:T(8,128)(2,1)S(1)}, bf16[256,256]{1,0:T(8,128)(2,1)S(1)}, u32[]{:S(2)}, u32[]{:S(2)}) %collective-permute-start.1) | collective-permute-done | bytes 131104 | tf_op jit(solution)/shard_map/ppermute | solution.py:33
  17.1 0.3 collective-permute-done.2.refs_2_
  17.4 0.8 %collective-permute-done.3.refs_3_ = bf16[256,256]{1,0:T(8,128)(2,1)S(1)} collective-permute-done((bf16[256,256]{1,0:T(8,128)(2,1)S(1)}, bf16[256,256]{1,0:T(8,128)(2,1)S(1)}, u32[]{:S(2)}, u32[]{:S(2)}) %collective-permute-start.3) | collective-permute-done | bytes 131104 | tf_op jit(solution)/shard_map/ppermute | solution.py:33
  18.2 1.7 %shard_map.113 = (bf16[8,64,256]{2,1,0:T(8,128)(2,1)S(1)}, bf16[8,64,256]{2,1,0:T(8,128)(2,1)S(1)}, bf16[8,64,256]{2,1,0:T(8,128)(2,1)S(1)}, bf16[128,256]{1,0:T...) custom-call(s32[2,8]{1,0:T(2,128)S(1)} %get-tuple-element.33.rows_re, ...), custom_call_target="tpu_custom_call" | custom-call | flops 301989888 | bytes 3874912 | tf_op jit(solution)/shard_map/pallas_call | solution.py:301
  20.0 0.2 collective-permute-start.10
  20.2 1.0 %collective-permute-start.9 = (f32[136,128]{1,0:T(8,128)S(1)}, f32[136,128]{1,0:T(8,128)S(1)}, u32[]{:S(2)}, u32[]{:S(2)}) collective-permute-start(f32[136,128]{1,0:T(8,128)S(1)} %get-tuple-element.59), channel_id=1, source_target_pairs={{2,0},{0,2},{6,4},{4,6},{10,8},{8,10},{14,12},{12,14},{3,1},{1,3},... | collective-permute-start | bytes 208904 | tf_op jit(solution)/shard_map/ppermute | solution.py:379
  21.2 0.7 %collective-permute-start.8 = (f32[136,128]{1,0:T(8,128)S(1)}, f32[136,128]{1,0:T(8,128)S(1)}, u32[]{:S(2)}, u32[]{:S(2)}) collective-permute-start(f32[136,128]{1,0:T(8,128)S(1)} %get-tuple-element.59), channel_id=1, source_target_pairs={{1,0},{0,1},{3,2},{2,3},{5,4},{4,5},{7,6},{6,7},{9,8},{8,9},{11,10... | collective-permute-start | bytes 208904 | tf_op jit(solution)/shard_map/ppermute | solution.py:381
  21.9 2.6 %collective-permute-done.10 = f32[136,128]{1,0:T(8,128)S(1)} collective-permute-done((f32[136,128]{1,0:T(8,128)S(1)}, f32[136,128]{1,0:T(8,128)S(1)}, u32[]{:S(2)}, u32[]{:S(2)}) %collective-permute-start.10) | collective-permute-done | bytes 69664 | tf_op jit(solution)/shard_map/ppermute | solution.py:382
  24.5 1.0 %collective-permute-done.9 = f32[136,128]{1,0:T(8,128)S(1)} collective-permute-done((f32[136,128]{1,0:T(8,128)S(1)}, f32[136,128]{1,0:T(8,128)S(1)}, u32[]{:S(2)}, u32[]{:S(2)}) %collective-permute-start.9) | collective-permute-done | bytes 69664 | tf_op jit(solution)/shard_map/ppermute | solution.py:379
  25.5 0.0 collective-permute-done.8
  25.5 1.3 %collective-permute-start.11 = (f32[136,128]{1,0:T(8,128)S(1)}, f32[136,128]{1,0:T(8,128)S(1)}, u32[]{:S(2)}, u32[]{:S(2)}) collective-permute-start(f32[136,128]{1,0:T(8,128)S(1)} %add_add_fusion), channel_id=1, source_target_pairs={{4,0},{6,2},{0,4},{2,6},{12,8},{14,10},{8,12},{10,14},{5,1},{7,3},... | collective-permute-start | bytes 208904 | tf_op jit(solution)/shard_map/ppermute | solution.py:379
  26.8 0.8 %collective-permute-start.4 = (bf16[128,256]{1,0:T(8,128)(2,1)S(1)}, bf16[128,256]{1,0:T(8,128)(2,1)S(1)}, u32[]{:S(2)}, u32[]{:S(2)}) collective-permute-start(bf16[128,256]{1,0:T(8,128)(2,1)S(1)} %get-tuple-element.53), channel_id=1, source_target_pairs={{12,0},{14,2},{8,4},{10,6},{4,8},{6,10},{0,12},{2,14},{13,1},{15,3... | collective-permute-start | bytes 196616 | tf_op jit(solution)/shard_map/ppermute | solution.py:33
  27.6 3.1 %collective-permute-start.5 = (bf16[128,256]{1,0:T(8,128)(2,1)S(1)}, bf16[128,256]{1,0:T(8,128)(2,1)S(1)}, u32[]{:S(2)}, u32[]{:S(2)}) collective-permute-start(bf16[128,256]{1,0:T(8,128)(2,1)S(1)} %get-tuple-element.54), channel_id=1, source_target_pairs={{14,0},{4,2},{2,4},{8,6},{6,8},{12,10},{10,12},{0,14},{15,1},{5,3}... | collective-permute-start | bytes 196616 | tf_op jit(solution)/shard_map/ppermute | solution.py:33
  30.7 0.0 collective-permute-start.6
  30.7 0.4 %collective-permute-start.7 = (bf16[128,256]{1,0:T(8,128)(2,1)S(1)}, bf16[128,256]{1,0:T(8,128)(2,1)S(1)}, u32[]{:S(2)}, u32[]{:S(2)}) collective-permute-start(bf16[128,256]{1,0:T(8,128)(2,1)S(1)} %get-tuple-element.56), channel_id=1, source_target_pairs={{2,0},{0,2},{6,4},{4,6},{10,8},{8,10},{14,12},{12,14},{3,1},{1,3},... | collective-permute-start | bytes 196616 | tf_op jit(solution)/shard_map/ppermute | solution.py:33
  31.1 0.0 collective-permute-done.11
  31.1 2.5 %collective-permute-start.12 = (f32[136,128]{1,0:T(8,128)S(1)}, f32[136,128]{1,0:T(8,128)S(1)}, u32[]{:S(2)}, u32[]{:S(2)}) collective-permute-start(f32[136,128]{1,0:T(8,128)S(1)} %add.15.mine), channel_id=1, source_target_pairs={{8,0},{10,2},{12,4},{14,6},{0,8},{2,10},{4,12},{6,14},{9,1},{11,3}... | collective-permute-start | bytes 208904 | tf_op jit(solution)/shard_map/ppermute | solution.py:379
  33.6 1.3 %shard_map.114 = (f32[8,64,128]{2,1,0:T(8,128)S(1)}, f32[8,64,128]{2,1,0:T(8,128)S(1)}, f32[8,64,256]{2,1,0:T(8,128)S(1)}) custom-call(s32[2,8]{1,0:T(2,128)S(1)} %get-tuple-element.33.rows_ref, bf16[8,64,128]{2,1,0:T(8,128)(2,1)S(1)} %copy-done.1, bf16[8,64,128]{2,1,0:T(8,128)(2,1)S(1)} %copy-done.2, bf16[8,64,576]{2,1,0:T(8,128)(2,1)S(1)} %copy-done, ...), custom_call_target="tpu_custom_call" | custom-call | flops 251658240 | bytes 3048000 | tf_op jit(solution)/shard_map/pallas_call | solution.py:301
  34.9 0.0 collective-permute-done.4.refs_0_
  34.9 0.2 collective-permute-done.5.refs_1_
  35.1 0.5 %collective-permute-done.6.refs_2_ = bf16[128,256]{1,0:T(8,128)(2,1)S(1)} collective-permute-done((bf16[128,256]{1,0:T(8,128)(2,1)S(1)}, bf16[128,256]{1,0:T(8,128)(2,1)S(1)}, u32[]{:S(2)}, u32[]{:S(2)}) %collective-permute-start.6) | collective-permute-done | bytes 65568 | tf_op jit(solution)/shard_map/ppermute | solution.py:33
  35.5 0.0 collective-permute-done.7.refs_3_
  35.6 1.7 %shard_map.115 = (bf16[8,64,128]{2,1,0:T(8,128)(2,1)}, bf16[8,64,128]{2,1,0:T(8,128)(2,1)}) custom-call(s32[2,8]{1,0:T(2,128)S(1)} %get-tuple-element.33.rows_ref, bf16[8,64,576]{2,1,0:T(8,128)(2,1)S(1)} %copy-done, bf16[8,64,256]{2,1,0:T(8,128)(2,1)S(1)} %get-tuple-element.34.keep, f32[8,64,128]{2,1,0:T(8,128)S(1)} %get-tuple-element.49.out_part, ...), custom_call_target="tpu_custom_call" | custom-call | flops 150994944 | bytes 2457664 | tf_op jit(solution)/shard_map/pallas_call | solution.py:301
  37.3 0.0 collective-permute-done.12.other
  37.3 0.7 %shard_map.116 = (f32[4,64,64]{2,1,0:T(8,128)}, f32[1,64]{1,0:T(1,128)}) custom-call(f32[136,128]{1,0:T(8,128)S(1)} %add.15.mine, f32[136,128]{1,0:T(8,128)S(1)} %collective-permute-done.12.other), custom_call_target="tpu_custom_call" | custom-call | flops 17408 | bytes 205056 | tf_op jit(solution)/shard_map/pallas_call | solution.py:301
  (8 shorter events, 0.0 us)
Async XLA Ops:
  0.6 10.4 %copy-start = (bf16[8,64,576]{2,1,0:T(8,128)(2,1)S(1)}, bf16[8,64,576]{2,1,0:T(8,128)(2,1)}, u32[]{:S(2)}) copy-start(bf16[8,64,576]{2,1,0:T(8,128)(2,1)} %lap.7) | copy-start | bytes 1769476
  0.6 10.4 %copy-start.1 = (bf16[8,64,128]{2,1,0:T(8,128)(2,1)S(1)}, bf16[8,64,128]{2,1,0:T(8,128)(2,1)}, u32[]{:S(2)}) copy-start(bf16[8,64,128]{2,1,0:T(8,128)(2,1)} %feat_ref.5) | copy-start | bytes 393220
  0.7 10.4 %copy-start.2 = (bf16[8,64,128]{2,1,0:T(8,128)(2,1)S(1)}, bf16[8,64,128]{2,1,0:T(8,128)(2,1)}, u32[]{:S(2)}) copy-start(bf16[8,64,128]{2,1,0:T(8,128)(2,1)} %cot_ref.5) | copy-start | bytes 393220
  2.9 9.5 %collective-permute-start = (bf16[256,256]{1,0:T(8,128)(2,1)S(1)}, bf16[256,256]{1,0:T(8,128)(2,1)S(1)}, u32[]{:S(2)}, u32[]{:S(2)}) collective-permute-start(bf16[256,256]{1,0:T(8,128)(2,1)S(1)} %get-tuple-element.40), channel_id=1, source_target_pairs={{12,0},{14,2},{8,4},{10,6},{4,8},{6,10},{0,12},{2,14},{13,1},{15,3... | collective-permute-start | bytes 393224 | tf_op jit(solution)/shard_map/ppermute | solution.py:33
  8.1 9.1 %collective-permute-start.1 = (bf16[256,256]{1,0:T(8,128)(2,1)S(1)}, bf16[256,256]{1,0:T(8,128)(2,1)S(1)}, u32[]{:S(2)}, u32[]{:S(2)}) collective-permute-start(bf16[256,256]{1,0:T(8,128)(2,1)S(1)} %get-tuple-element.41), channel_id=1, source_target_pairs={{14,0},{4,2},{2,4},{8,6},{6,8},{12,10},{10,12},{0,14},{15,1},{5,3}... | collective-permute-start | bytes 393224 | tf_op jit(solution)/shard_map/ppermute | solution.py:33
  9.2 8.2 %collective-permute-start.2 = (bf16[256,256]{1,0:T(8,128)(2,1)S(1)}, bf16[256,256]{1,0:T(8,128)(2,1)S(1)}, u32[]{:S(2)}, u32[]{:S(2)}) collective-permute-start(bf16[256,256]{1,0:T(8,128)(2,1)S(1)} %get-tuple-element.42), channel_id=1, source_target_pairs={{4,0},{6,2},{0,4},{2,6},{12,8},{14,10},{8,12},{10,14},{5,1},{7,3},... | collective-permute-start | bytes 393224 | tf_op jit(solution)/shard_map/ppermute | solution.py:33
  11.0 7.2 %collective-permute-start.3 = (bf16[256,256]{1,0:T(8,128)(2,1)S(1)}, bf16[256,256]{1,0:T(8,128)(2,1)S(1)}, u32[]{:S(2)}, u32[]{:S(2)}) collective-permute-start(bf16[256,256]{1,0:T(8,128)(2,1)S(1)} %get-tuple-element.43), channel_id=1, source_target_pairs={{2,0},{0,2},{6,4},{4,6},{10,8},{8,10},{14,12},{12,14},{3,1},{1,3},... | collective-permute-start | bytes 393224 | tf_op jit(solution)/shard_map/ppermute | solution.py:33
  20.0 4.5 %collective-permute-start.10 = (f32[136,128]{1,0:T(8,128)S(1)}, f32[136,128]{1,0:T(8,128)S(1)}, u32[]{:S(2)}, u32[]{:S(2)}) collective-permute-start(f32[136,128]{1,0:T(8,128)S(1)} %get-tuple-element.59), channel_id=1, source_target_pairs={{3,0},{2,1},{1,2},{0,3},{7,4},{6,5},{5,6},{4,7},{11,8},{10,9},{9,1... | collective-permute-start | bytes 208904 | tf_op jit(solution)/shard_map/ppermute | solution.py:382
  20.2 5.3 %collective-permute-start.9 = (f32[136,128]{1,0:T(8,128)S(1)}, f32[136,128]{1,0:T(8,128)S(1)}, u32[]{:S(2)}, u32[]{:S(2)}) collective-permute-start(f32[136,128]{1,0:T(8,128)S(1)} %get-tuple-element.59), channel_id=1, source_target_pairs={{2,0},{0,2},{6,4},{4,6},{10,8},{8,10},{14,12},{12,14},{3,1},{1,3},... | collective-permute-start | bytes 208904 | tf_op jit(solution)/shard_map/ppermute | solution.py:379
  21.2 4.3 %collective-permute-start.8 = (f32[136,128]{1,0:T(8,128)S(1)}, f32[136,128]{1,0:T(8,128)S(1)}, u32[]{:S(2)}, u32[]{:S(2)}) collective-permute-start(f32[136,128]{1,0:T(8,128)S(1)} %get-tuple-element.59), channel_id=1, source_target_pairs={{1,0},{0,1},{3,2},{2,3},{5,4},{4,5},{7,6},{6,7},{9,8},{8,9},{11,10... | collective-permute-start | bytes 208904 | tf_op jit(solution)/shard_map/ppermute | solution.py:381
  25.5 5.6 %collective-permute-start.11 = (f32[136,128]{1,0:T(8,128)S(1)}, f32[136,128]{1,0:T(8,128)S(1)}, u32[]{:S(2)}, u32[]{:S(2)}) collective-permute-start(f32[136,128]{1,0:T(8,128)S(1)} %add_add_fusion), channel_id=1, source_target_pairs={{4,0},{6,2},{0,4},{2,6},{12,8},{14,10},{8,12},{10,14},{5,1},{7,3},... | collective-permute-start | bytes 208904 | tf_op jit(solution)/shard_map/ppermute | solution.py:379
  26.8 8.1 %collective-permute-start.4 = (bf16[128,256]{1,0:T(8,128)(2,1)S(1)}, bf16[128,256]{1,0:T(8,128)(2,1)S(1)}, u32[]{:S(2)}, u32[]{:S(2)}) collective-permute-start(bf16[128,256]{1,0:T(8,128)(2,1)S(1)} %get-tuple-element.53), channel_id=1, source_target_pairs={{12,0},{14,2},{8,4},{10,6},{4,8},{6,10},{0,12},{2,14},{13,1},{15,3... | collective-permute-start | bytes 196616 | tf_op jit(solution)/shard_map/ppermute | solution.py:33
  27.6 7.4 %collective-permute-start.5 = (bf16[128,256]{1,0:T(8,128)(2,1)S(1)}, bf16[128,256]{1,0:T(8,128)(2,1)S(1)}, u32[]{:S(2)}, u32[]{:S(2)}) collective-permute-start(bf16[128,256]{1,0:T(8,128)(2,1)S(1)} %get-tuple-element.54), channel_id=1, source_target_pairs={{14,0},{4,2},{2,4},{8,6},{6,8},{12,10},{10,12},{0,14},{15,1},{5,3}... | collective-permute-start | bytes 196616 | tf_op jit(solution)/shard_map/ppermute | solution.py:33
  30.7 4.8 %collective-permute-start.6 = (bf16[128,256]{1,0:T(8,128)(2,1)S(1)}, bf16[128,256]{1,0:T(8,128)(2,1)S(1)}, u32[]{:S(2)}, u32[]{:S(2)}) collective-permute-start(bf16[128,256]{1,0:T(8,128)(2,1)S(1)} %get-tuple-element.55), channel_id=1, source_target_pairs={{4,0},{6,2},{0,4},{2,6},{12,8},{14,10},{8,12},{10,14},{5,1},{7,3},... | collective-permute-start | bytes 196616 | tf_op jit(solution)/shard_map/ppermute | solution.py:33
  30.7 4.8 %collective-permute-start.7 = (bf16[128,256]{1,0:T(8,128)(2,1)S(1)}, bf16[128,256]{1,0:T(8,128)(2,1)S(1)}, u32[]{:S(2)}, u32[]{:S(2)}) collective-permute-start(bf16[128,256]{1,0:T(8,128)(2,1)S(1)} %get-tuple-element.56), channel_id=1, source_target_pairs={{2,0},{0,2},{6,4},{4,6},{10,8},{8,10},{14,12},{12,14},{3,1},{1,3},... | collective-permute-start | bytes 196616 | tf_op jit(solution)/shard_map/ppermute | solution.py:33
  31.1 6.1 %collective-permute-start.12 = (f32[136,128]{1,0:T(8,128)S(1)}, f32[136,128]{1,0:T(8,128)S(1)}, u32[]{:S(2)}, u32[]{:S(2)}) collective-permute-start(f32[136,128]{1,0:T(8,128)S(1)} %add.15.mine), channel_id=1, source_target_pairs={{8,0},{10,2},{12,4},{14,6},{0,8},{2,10},{4,12},{6,14},{9,1},{11,3}... | collective-permute-start | bytes 208904 | tf_op jit(solution)/shard_map/ppermute | solution.py:379

commit v7 on v6

--- a/solution.py
+++ b/solution.py
@@ -82,8 +82,8 @@
         pltpu.make_async_copy(rows_hbm, rows_ref, sem.at[4]),
         pltpu.make_async_copy(lists_hbm, lists_ref, sem.at[5]),
     ]
-    for copy in copies:
-        copy.start()
+    for first in (3, 0, 1, 2, 4, 5):
+        copies[first].start()
     diagonal = lax.broadcasted_iota(jnp.int32, (pixels, pixels), 0) == lax.broadcasted_iota(
         jnp.int32, (pixels, pixels), 1
     )

time: 38.2 us -> 38.2 us (level)
  no operation moved by 1% of the time
where the time goes in v7:
time: 38.2 us; the launch traced here: 38 us
  starting transfers between devices  18 us (47%)
  waiting for transfers between devices  10.4 us (27%)
  Pallas kernels  8.75 us (23%)
  between operations  0.74 us (2%)
    ppermute x8, starting transfers between devices, exchange(): return lax.ppermute(block, 'pix', route)  12.3 us
    pallas_call x6, Pallas kernels, call(): pl.pallas_call(kernel, out_shape=outs, in_specs=[place(i, x) for i, x in...  8.75 us
    ppermute x8, waiting for transfers between devices, exchange(): return lax.ppermute(block, 'pix', route)  6.83 us
    ppermute x3, starting transfers between devices, swap(): return lax.ppermute(block, 'pix', [(i ^ reach, i) for i in range(count)])  4.79 us
    ppermute x1, waiting for transfers between devices, local(): lax.ppermute(sums, ('pix', 'dp'), [(i ^ pair + 1, i) for i in range(count...  2.62 us
    ppermute x3, waiting for transfers between devices, swap(): return lax.ppermute(block, 'pix', [(i ^ reach, i) for i in range(count)])  1 us
  transfers between devices with their start and end apart: 13, of which 8 were waited for; matrix products, arithmetic and copies ran while one was open for 0% of the time, Pallas kernels for 11%

profile of v7, /device:TPU:0, one launch (start us, length us, event | category | flops | bytes accessed | tf_op | source)
XLA Modules:
  0.0 38.0 jit_solution(12454071123667686702)
XLA Ops:
  0.7 2.3 %shard_map.111 = (bf16[256,256]{1,0:T(8,128)(2,1)S(1)}, bf16[256,256]{1,0:T(8,128)(2,1)S(1)}, bf16[256,256]{1,0:T(8,128)(2,1)S(1)}, bf16[256,256]{1,0:T(8,128)(2...) custom-call(s32[2,8]{1,0:T(2,128)} %bitcast.4, ...), custom_call_target="tpu_custom_call" | custom-call | flops 150994944 | bytes 2427072 | tf_op jit(solution)/shard_map/pallas_call | solution.py:301
  2.9 5.1 %collective-permute-start = (bf16[256,256]{1,0:T(8,128)(2,1)S(1)}, bf16[256,256]{1,0:T(8,128)(2,1)S(1)}, u32[]{:S(2)}, u32[]{:S(2)}) collective-permute-start(bf16[256,256]{1,0:T(8,128)(2,1)S(1)} %get-tuple-element.40), channel_id=1, source_target_pairs={{12,0},{14,2},{8,4},{10,6},{4,8},{6,10},{0,12},{2,14},{13,1},{15,3... | collective-permute-start | bytes 393224 | tf_op jit(solution)/shard_map/ppermute | solution.py:33
  8.0 1.1 %collective-permute-start.1 = (bf16[256,256]{1,0:T(8,128)(2,1)S(1)}, bf16[256,256]{1,0:T(8,128)(2,1)S(1)}, u32[]{:S(2)}, u32[]{:S(2)}) collective-permute-start(bf16[256,256]{1,0:T(8,128)(2,1)S(1)} %get-tuple-element.41), channel_id=1, source_target_pairs={{14,0},{4,2},{2,4},{8,6},{6,8},{12,10},{10,12},{0,14},{15,1},{5,3}... | collective-permute-start | bytes 393224 | tf_op jit(solution)/shard_map/ppermute | solution.py:33
  9.2 1.8 %collective-permute-start.2 = (bf16[256,256]{1,0:T(8,128)(2,1)S(1)}, bf16[256,256]{1,0:T(8,128)(2,1)S(1)}, u32[]{:S(2)}, u32[]{:S(2)}) collective-permute-start(bf16[256,256]{1,0:T(8,128)(2,1)S(1)} %get-tuple-element.42), channel_id=1, source_target_pairs={{4,0},{6,2},{0,4},{2,6},{12,8},{14,10},{8,12},{10,14},{5,1},{7,3},... | collective-permute-start | bytes 393224 | tf_op jit(solution)/shard_map/ppermute | solution.py:33
  11.0 0.0 collective-permute-start.3
  11.0 1.0 %shard_map.112 = (f32[8,64,256]{2,1,0:T(8,128)S(1)}, f32[136,128]{1,0:T(8,128)S(1)}, bf16[128,384]{1,0:T(8,128)(2,1)S(1)}, bf16[128,128]{1,0:T(8,128)(2,1)S(1)}, f32[1,128]{1,0:T(1,128)S(1)}) custom-call(bf16[8,64,128]{2,1,0:T(8,128)(2,1)S(1)} %copy-done.1, bf16[8,64,128]{2,1,0:T(8,128)(2,1)S(1)} %copy-done.2, bf16[8,64,576]{2,1,0:T(8,128)(2,1)S(1)} %copy-done, ...), custom_call_target="tpu_custom_call" | custom-call | flops 33554432 | bytes 1872640 | tf_op jit(solution)/shard_map/pallas_call | solution.py:301
  12.0 0.4 %collective-permute-done.refs_0_ = bf16[256,256]{1,0:T(8,128)(2,1)S(1)} collective-permute-done((bf16[256,256]{1,0:T(8,128)(2,1)S(1)}, bf16[256,256]{1,0:T(8,128)(2,1)S(1)}, u32[]{:S(2)}, u32[]{:S(2)}) %collective-permute-start) | collective-permute-done | bytes 131104 | tf_op jit(solution)/shard_map/ppermute | solution.py:33
  12.4 4.7 %collective-permute-done.1.refs_1_ = bf16[256,256]{1,0:T(8,128)(2,1)S(1)} collective-permute-done((bf16[256,256]{1,0:T(8,128)(2,1)S(1)}, bf16[256,256]{1,0:T(8,128)(2,1)S(1)}, u32[]{:S(2)}, u32[]{:S(2)}) %collective-permute-start.1) | collective-permute-done | bytes 131104 | tf_op jit(solution)/shard_map/ppermute | solution.py:33
  17.1 0.3 collective-permute-done.2.refs_2_
  17.4 0.8 %collective-permute-done.3.refs_3_ = bf16[256,256]{1,0:T(8,128)(2,1)S(1)} collective-permute-done((bf16[256,256]{1,0:T(8,128)(2,1)S(1)}, bf16[256,256]{1,0:T(8,128)(2,1)S(1)}, u32[]{:S(2)}, u32[]{:S(2)}) %collective-permute-start.3) | collective-permute-done | bytes 131104 | tf_op jit(solution)/shard_map/ppermute | solution.py:33
  18.2 1.7 %shard_map.113 = (bf16[8,64,256]{2,1,0:T(8,128)(2,1)S(1)}, bf16[8,64,256]{2,1,0:T(8,128)(2,1)S(1)}, bf16[8,64,256]{2,1,0:T(8,128)(2,1)S(1)}, bf16[128,256]{1,0:T...) custom-call(s32[2,8]{1,0:T(2,128)S(1)} %get-tuple-element.33.rows_re, ...), custom_call_target="tpu_custom_call" | custom-call | flops 301989888 | bytes 3874912 | tf_op jit(solution)/shard_map/pallas_call | solution.py:301
  20.0 0.2 collective-permute-start.10
  20.2 1.0 %collective-permute-start.9 = (f32[136,128]{1,0:T(8,128)S(1)}, f32[136,128]{1,0:T(8,128)S(1)}, u32[]{:S(2)}, u32[]{:S(2)}) collective-permute-start(f32[136,128]{1,0:T(8,128)S(1)} %get-tuple-element.59), channel_id=1, source_target_pairs={{2,0},{0,2},{6,4},{4,6},{10,8},{8,10},{14,12},{12,14},{3,1},{1,3},... | collective-permute-start | bytes 208904 | tf_op jit(solution)/shard_map/ppermute | solution.py:379
  21.2 0.7 %collective-permute-start.8 = (f32[136,128]{1,0:T(8,128)S(1)}, f32[136,128]{1,0:T(8,128)S(1)}, u32[]{:S(2)}, u32[]{:S(2)}) collective-permute-start(f32[136,128]{1,0:T(8,128)S(1)} %get-tuple-element.59), channel_id=1, source_target_pairs={{1,0},{0,1},{3,2},{2,3},{5,4},{4,5},{7,6},{6,7},{9,8},{8,9},{11,10... | collective-permute-start | bytes 208904 | tf_op jit(solution)/shard_map/ppermute | solution.py:381
  21.9 2.6 %collective-permute-done.10 = f32[136,128]{1,0:T(8,128)S(1)} collective-permute-done((f32[136,128]{1,0:T(8,128)S(1)}, f32[136,128]{1,0:T(8,128)S(1)}, u32[]{:S(2)}, u32[]{:S(2)}) %collective-permute-start.10) | collective-permute-done | bytes 69664 | tf_op jit(solution)/shard_map/ppermute | solution.py:382
  24.5 1.0 %collective-permute-done.9 = f32[136,128]{1,0:T(8,128)S(1)} collective-permute-done((f32[136,128]{1,0:T(8,128)S(1)}, f32[136,128]{1,0:T(8,128)S(1)}, u32[]{:S(2)}, u32[]{:S(2)}) %collective-permute-start.9) | collective-permute-done | bytes 69664 | tf_op jit(solution)/shard_map/ppermute | solution.py:379
  25.5 0.0 collective-permute-done.8
  25.5 1.3 %collective-permute-start.11 = (f32[136,128]{1,0:T(8,128)S(1)}, f32[136,128]{1,0:T(8,128)S(1)}, u32[]{:S(2)}, u32[]{:S(2)}) collective-permute-start(f32[136,128]{1,0:T(8,128)S(1)} %add_add_fusion), channel_id=1, source_target_pairs={{4,0},{6,2},{0,4},{2,6},{12,8},{14,10},{8,12},{10,14},{5,1},{7,3},... | collective-permute-start | bytes 208904 | tf_op jit(solution)/shard_map/ppermute | solution.py:379
  26.8 0.8 %collective-permute-start.4 = (bf16[128,256]{1,0:T(8,128)(2,1)S(1)}, bf16[128,256]{1,0:T(8,128)(2,1)S(1)}, u32[]{:S(2)}, u32[]{:S(2)}) collective-permute-start(bf16[128,256]{1,0:T(8,128)(2,1)S(1)} %get-tuple-element.53), channel_id=1, source_target_pairs={{12,0},{14,2},{8,4},{10,6},{4,8},{6,10},{0,12},{2,14},{13,1},{15,3... | collective-permute-start | bytes 196616 | tf_op jit(solution)/shard_map/ppermute | solution.py:33
  27.6 3.1 %collective-permute-start.5 = (bf16[128,256]{1,0:T(8,128)(2,1)S(1)}, bf16[128,256]{1,0:T(8,128)(2,1)S(1)}, u32[]{:S(2)}, u32[]{:S(2)}) collective-permute-start(bf16[128,256]{1,0:T(8,128)(2,1)S(1)} %get-tuple-element.54), channel_id=1, source_target_pairs={{14,0},{4,2},{2,4},{8,6},{6,8},{12,10},{10,12},{0,14},{15,1},{5,3}... | collective-permute-start | bytes 196616 | tf_op jit(solution)/shard_map/ppermute | solution.py:33
  30.7 0.0 collective-permute-start.6
  30.7 0.4 %collective-permute-start.7 = (bf16[128,256]{1,0:T(8,128)(2,1)S(1)}, bf16[128,256]{1,0:T(8,128)(2,1)S(1)}, u32[]{:S(2)}, u32[]{:S(2)}) collective-permute-start(bf16[128,256]{1,0:T(8,128)(2,1)S(1)} %get-tuple-element.56), channel_id=1, source_target_pairs={{2,0},{0,2},{6,4},{4,6},{10,8},{8,10},{14,12},{12,14},{3,1},{1,3},... | collective-permute-start | bytes 196616 | tf_op jit(solution)/shard_map/ppermute | solution.py:33
  31.1 0.0 collective-permute-done.11
  31.1 2.5 %collective-permute-start.12 = (f32[136,128]{1,0:T(8,128)S(1)}, f32[136,128]{1,0:T(8,128)S(1)}, u32[]{:S(2)}, u32[]{:S(2)}) collective-permute-start(f32[136,128]{1,0:T(8,128)S(1)} %add.15.mine), channel_id=1, source_target_pairs={{8,0},{10,2},{12,4},{14,6},{0,8},{2,10},{4,12},{6,14},{9,1},{11,3}... | collective-permute-start | bytes 208904 | tf_op jit(solution)/shard_map/ppermute | solution.py:379
  33.6 1.3 %shard_map.114 = (f32[8,64,128]{2,1,0:T(8,128)S(1)}, f32[8,64,128]{2,1,0:T(8,128)S(1)}, f32[8,64,256]{2,1,0:T(8,128)S(1)}) custom-call(s32[2,8]{1,0:T(2,128)S(1)} %get-tuple-element.33.rows_ref, bf16[8,64,128]{2,1,0:T(8,128)(2,1)S(1)} %copy-done.1, bf16[8,64,128]{2,1,0:T(8,128)(2,1)S(1)} %copy-done.2, bf16[8,64,576]{2,1,0:T(8,128)(2,1)S(1)} %copy-done, ...), custom_call_target="tpu_custom_call" | custom-call | flops 251658240 | bytes 3048000 | tf_op jit(solution)/shard_map/pallas_call | solution.py:301
  34.9 0.0 collective-permute-done.4.refs_0_
  34.9 0.2 collective-permute-done.5.refs_1_
  35.1 0.5 %collective-permute-done.6.refs_2_ = bf16[128,256]{1,0:T(8,128)(2,1)S(1)} collective-permute-done((bf16[128,256]{1,0:T(8,128)(2,1)S(1)}, bf16[128,256]{1,0:T(8,128)(2,1)S(1)}, u32[]{:S(2)}, u32[]{:S(2)}) %collective-permute-start.6) | collective-permute-done | bytes 65568 | tf_op jit(solution)/shard_map/ppermute | solution.py:33
  35.5 0.0 collective-permute-done.7.refs_3_
  35.5 1.7 %shard_map.115 = (bf16[8,64,128]{2,1,0:T(8,128)(2,1)}, bf16[8,64,128]{2,1,0:T(8,128)(2,1)}) custom-call(s32[2,8]{1,0:T(2,128)S(1)} %get-tuple-element.33.rows_ref, bf16[8,64,576]{2,1,0:T(8,128)(2,1)S(1)} %copy-done, bf16[8,64,256]{2,1,0:T(8,128)(2,1)S(1)} %get-tuple-element.34.keep, f32[8,64,128]{2,1,0:T(8,128)S(1)} %get-tuple-element.49.out_part, ...), custom_call_target="tpu_custom_call" | custom-call | flops 150994944 | bytes 2457664 | tf_op jit(solution)/shard_map/pallas_call | solution.py:301
  37.2 0.0 collective-permute-done.12.other
  37.3 0.7 %shard_map.116 = (f32[4,64,64]{2,1,0:T(8,128)}, f32[1,64]{1,0:T(1,128)}) custom-call(f32[136,128]{1,0:T(8,128)S(1)} %add.15.mine, f32[136,128]{1,0:T(8,128)S(1)} %collective-permute-done.12.other), custom_call_target="tpu_custom_call" | custom-call | flops 17408 | bytes 205056 | tf_op jit(solution)/shard_map/pallas_call | solution.py:301
  (8 shorter events, 0.0 us)
Async XLA Ops:
  0.6 10.4 %copy-start = (bf16[8,64,576]{2,1,0:T(8,128)(2,1)S(1)}, bf16[8,64,576]{2,1,0:T(8,128)(2,1)}, u32[]{:S(2)}) copy-start(bf16[8,64,576]{2,1,0:T(8,128)(2,1)} %lap.7) | copy-start | bytes 1769476
  0.6 10.4 %copy-start.1 = (bf16[8,64,128]{2,1,0:T(8,128)(2,1)S(1)}, bf16[8,64,128]{2,1,0:T(8,128)(2,1)}, u32[]{:S(2)}) copy-start(bf16[8,64,128]{2,1,0:T(8,128)(2,1)} %feat_ref.5) | copy-start | bytes 393220
  0.7 10.4 %copy-start.2 = (bf16[8,64,128]{2,1,0:T(8,128)(2,1)S(1)}, bf16[8,64,128]{2,1,0:T(8,128)(2,1)}, u32[]{:S(2)}) copy-start(bf16[8,64,128]{2,1,0:T(8,128)(2,1)} %cot_ref.5) | copy-start | bytes 393220
  2.9 9.5 %collective-permute-start = (bf16[256,256]{1,0:T(8,128)(2,1)S(1)}, bf16[256,256]{1,0:T(8,128)(2,1)S(1)}, u32[]{:S(2)}, u32[]{:S(2)}) collective-permute-start(bf16[256,256]{1,0:T(8,128)(2,1)S(1)} %get-tuple-element.40), channel_id=1, source_target_pairs={{12,0},{14,2},{8,4},{10,6},{4,8},{6,10},{0,12},{2,14},{13,1},{15,3... | collective-permute-start | bytes 393224 | tf_op jit(solution)/shard_map/ppermute | solution.py:33
  8.0 9.1 %collective-permute-start.1 = (bf16[256,256]{1,0:T(8,128)(2,1)S(1)}, bf16[256,256]{1,0:T(8,128)(2,1)S(1)}, u32[]{:S(2)}, u32[]{:S(2)}) collective-permute-start(bf16[256,256]{1,0:T(8,128)(2,1)S(1)} %get-tuple-element.41), channel_id=1, source_target_pairs={{14,0},{4,2},{2,4},{8,6},{6,8},{12,10},{10,12},{0,14},{15,1},{5,3}... | collective-permute-start | bytes 393224 | tf_op jit(solution)/shard_map/ppermute | solution.py:33
  9.2 8.2 %collective-permute-start.2 = (bf16[256,256]{1,0:T(8,128)(2,1)S(1)}, bf16[256,256]{1,0:T(8,128)(2,1)S(1)}, u32[]{:S(2)}, u32[]{:S(2)}) collective-permute-start(bf16[256,256]{1,0:T(8,128)(2,1)S(1)} %get-tuple-element.42), channel_id=1, source_target_pairs={{4,0},{6,2},{0,4},{2,6},{12,8},{14,10},{8,12},{10,14},{5,1},{7,3},... | collective-permute-start | bytes 393224 | tf_op jit(solution)/shard_map/ppermute | solution.py:33
  11.0 7.2 %collective-permute-start.3 = (bf16[256,256]{1,0:T(8,128)(2,1)S(1)}, bf16[256,256]{1,0:T(8,128)(2,1)S(1)}, u32[]{:S(2)}, u32[]{:S(2)}) collective-permute-start(bf16[256,256]{1,0:T(8,128)(2,1)S(1)} %get-tuple-element.43), channel_id=1, source_target_pairs={{2,0},{0,2},{6,4},{4,6},{10,8},{8,10},{14,12},{12,14},{3,1},{1,3},... | collective-permute-start | bytes 393224 | tf_op jit(solution)/shard_map/ppermute | solution.py:33
  20.0 4.5 %collective-permute-start.10 = (f32[136,128]{1,0:T(8,128)S(1)}, f32[136,128]{1,0:T(8,128)S(1)}, u32[]{:S(2)}, u32[]{:S(2)}) collective-permute-start(f32[136,128]{1,0:T(8,128)S(1)} %get-tuple-element.59), channel_id=1, source_target_pairs={{3,0},{2,1},{1,2},{0,3},{7,4},{6,5},{5,6},{4,7},{11,8},{10,9},{9,1... | collective-permute-start | bytes 208904 | tf_op jit(solution)/shard_map/ppermute | solution.py:382
  20.2 5.3 %collective-permute-start.9 = (f32[136,128]{1,0:T(8,128)S(1)}, f32[136,128]{1,0:T(8,128)S(1)}, u32[]{:S(2)}, u32[]{:S(2)}) collective-permute-start(f32[136,128]{1,0:T(8,128)S(1)} %get-tuple-element.59), channel_id=1, source_target_pairs={{2,0},{0,2},{6,4},{4,6},{10,8},{8,10},{14,12},{12,14},{3,1},{1,3},... | collective-permute-start | bytes 208904 | tf_op jit(solution)/shard_map/ppermute | solution.py:379
  21.2 4.3 %collective-permute-start.8 = (f32[136,128]{1,0:T(8,128)S(1)}, f32[136,128]{1,0:T(8,128)S(1)}, u32[]{:S(2)}, u32[]{:S(2)}) collective-permute-start(f32[136,128]{1,0:T(8,128)S(1)} %get-tuple-element.59), channel_id=1, source_target_pairs={{1,0},{0,1},{3,2},{2,3},{5,4},{4,5},{7,6},{6,7},{9,8},{8,9},{11,10... | collective-permute-start | bytes 208904 | tf_op jit(solution)/shard_map/ppermute | solution.py:381
  25.5 5.6 %collective-permute-start.11 = (f32[136,128]{1,0:T(8,128)S(1)}, f32[136,128]{1,0:T(8,128)S(1)}, u32[]{:S(2)}, u32[]{:S(2)}) collective-permute-start(f32[136,128]{1,0:T(8,128)S(1)} %add_add_fusion), channel_id=1, source_target_pairs={{4,0},{6,2},{0,4},{2,6},{12,8},{14,10},{8,12},{10,14},{5,1},{7,3},... | collective-permute-start | bytes 208904 | tf_op jit(solution)/shard_map/ppermute | solution.py:379
  26.8 8.1 %collective-permute-start.4 = (bf16[128,256]{1,0:T(8,128)(2,1)S(1)}, bf16[128,256]{1,0:T(8,128)(2,1)S(1)}, u32[]{:S(2)}, u32[]{:S(2)}) collective-permute-start(bf16[128,256]{1,0:T(8,128)(2,1)S(1)} %get-tuple-element.53), channel_id=1, source_target_pairs={{12,0},{14,2},{8,4},{10,6},{4,8},{6,10},{0,12},{2,14},{13,1},{15,3... | collective-permute-start | bytes 196616 | tf_op jit(solution)/shard_map/ppermute | solution.py:33
  27.6 7.4 %collective-permute-start.5 = (bf16[128,256]{1,0:T(8,128)(2,1)S(1)}, bf16[128,256]{1,0:T(8,128)(2,1)S(1)}, u32[]{:S(2)}, u32[]{:S(2)}) collective-permute-start(bf16[128,256]{1,0:T(8,128)(2,1)S(1)} %get-tuple-element.54), channel_id=1, source_target_pairs={{14,0},{4,2},{2,4},{8,6},{6,8},{12,10},{10,12},{0,14},{15,1},{5,3}... | collective-permute-start | bytes 196616 | tf_op jit(solution)/shard_map/ppermute | solution.py:33
  30.7 4.8 %collective-permute-start.6 = (bf16[128,256]{1,0:T(8,128)(2,1)S(1)}, bf16[128,256]{1,0:T(8,128)(2,1)S(1)}, u32[]{:S(2)}, u32[]{:S(2)}) collective-permute-start(bf16[128,256]{1,0:T(8,128)(2,1)S(1)} %get-tuple-element.55), channel_id=1, source_target_pairs={{4,0},{6,2},{0,4},{2,6},{12,8},{14,10},{8,12},{10,14},{5,1},{7,3},... | collective-permute-start | bytes 196616 | tf_op jit(solution)/shard_map/ppermute | solution.py:33
  30.7 4.8 %collective-permute-start.7 = (bf16[128,256]{1,0:T(8,128)(2,1)S(1)}, bf16[128,256]{1,0:T(8,128)(2,1)S(1)}, u32[]{:S(2)}, u32[]{:S(2)}) collective-permute-start(bf16[128,256]{1,0:T(8,128)(2,1)S(1)} %get-tuple-element.56), channel_id=1, source_target_pairs={{2,0},{0,2},{6,4},{4,6},{10,8},{8,10},{14,12},{12,14},{3,1},{1,3},... | collective-permute-start | bytes 196616 | tf_op jit(solution)/shard_map/ppermute | solution.py:33
  31.1 6.1 %collective-permute-start.12 = (f32[136,128]{1,0:T(8,128)S(1)}, f32[136,128]{1,0:T(8,128)S(1)}, u32[]{:S(2)}, u32[]{:S(2)}) collective-permute-start(f32[136,128]{1,0:T(8,128)S(1)} %add.15.mine), channel_id=1, source_target_pairs={{8,0},{10,2},{12,4},{14,6},{0,8},{2,10},{4,12},{6,14},{9,1},{11,3}... | collective-permute-start | bytes 208904 | tf_op jit(solution)/shard_map/ppermute | solution.py:379
